TPU v7x, 32 devices: a whole 2x2x4 slice. The times are simulated.
32 devices in a mesh: rows: 8 (over z, x), ch: 4 (over y, core).
Axes of the slice: x: 2, y: 2, z: 4, core: 2. Of those that a mesh axis runs over, the one named last changes fastest.
Arguments:
- hidden_in: bfloat16 [2048, 512], P('rows', 'ch'), may hold values from -6 to 6
- lengths: int32 [3], replicated, may hold values from 772 to 1024, as said below
- norm_gain: float32 [256], replicated, may hold values from 0.5 to 1.5
- in_weight: bfloat16 [2, 256, 512], P(None, None, 'ch'), may hold values from -0.375 to 0.375
- conv_weight: float32 [2, 4, 512], P(None, None, 'ch'), may hold values from -3 to 3
- conv_bias: float32 [2, 512], P(None, 'ch'), may hold values from -2 to 2
- select_weight: bfloat16 [2, 512, 48], P(None, 'ch'), may hold values from -0.25 to 0.25
- step_weight: bfloat16 [2, 16, 512], P(None, None, 'ch'), may hold values from -1.5 to 1.5
- step_bias: float32 [2, 512], P(None, 'ch'), may hold values from -7 to -2
- decay_log: float32 [2, 16, 512], P(None, None, 'ch'), may hold values from -9 to 1
- skip_gain: float32 [2, 512], P(None, 'ch'), may hold values from 0.5 to 1.5
- out_weight: bfloat16 [512, 256], P('ch'), may hold values from -0.25 to 0.25
- cotangent: bfloat16 [2048, 512], P('rows', 'ch'), may hold values from -6 to 6
Outputs:
- result: bfloat16 [2048, 512], P('rows', 'ch')
- input_grad: float32 [2048, 512], P('rows', 'ch')
- gain_grad: float32 [256], replicated
- in_weight_grad: float32 [2, 256, 512], P(None, None, 'ch')
- conv_weight_grad: float32 [2, 4, 512], P(None, None, 'ch')
- conv_bias_grad: float32 [2, 512], P(None, 'ch')
- select_weight_grad: float32 [2, 512, 48], P(None, 'ch')
- step_weight_grad: float32 [2, 16, 512], P(None, None, 'ch')
- step_bias_grad: float32 [2, 512], P(None, 'ch')
- decay_log_grad: float32 [2, 16, 512], P(None, None, 'ch')
- skip_gain_grad: float32 [2, 512], P(None, 'ch')
- out_weight_grad: float32 [512, 256], P('ch')
Inputs may be any that keep to these rules, and one draw needn't show every extreme that they name: `lengths`: some window has exactly 1024 valid positions in every draw.
All inputs are finite; a program needn't handle non-finite values.
Results may differ from a plain program's by a relative error of at most 0.0087.
Values may be sent and summed in bfloat16 or wider, within the bound.
No kernel may reach another device: no remote copies, remote signals or barrier semaphores. Data moves between devices by JAX's collectives and lax.ppermute only.
A program may use at most 192 MiB of HBM per device.

v0:
```python
import jax
import jax.numpy as jnp
from jax import lax
from jax.sharding import PartitionSpec as P

N = 16
R = 16
BLOCK = 64
WINDOW = 16384


epsilon = 1e-06
direction_flips = ((False, True), (True, False))


def extended(shard, sides, width):
    for axis, dim in sides:
        count, length = (lax.axis_size(axis), shard.shape[dim])
        up = [(i, (i + 1) % count) for i in range(count - 1)]
        down = [(j, i) for i, j in up]
        last = lax.slice_in_dim(shard, length - width, length, axis=dim)
        first = lax.slice_in_dim(shard, 0, width, axis=dim)
        before = lax.ppermute(last, axis, up)
        after = lax.ppermute(first, axis, down)
        shard = jnp.concatenate([before, shard, after], axis=dim)
    return shard


def carried_in(part, axis, combine, identity, reverse):
    count = lax.axis_size(axis)
    place = lax.axis_index(axis)
    ahead = count - 1 - place if reverse else place
    gathered = jax.tree.map(lambda a: lax.all_gather(a, axis), part)
    state = jax.tree.map(lambda a, e: jnp.zeros_like(a) + jnp.asarray(e, a.dtype), part, identity)

    def one(step, state):
        source = count - 1 - step if reverse else step
        return combine(
            state, jax.tree.map(lambda a: lax.dynamic_index_in_dim(a, source, 0, False), gathered)
        )

    return lax.fori_loop(0, ahead, one, state)


def entering(shard, axis, combine, identity):
    count, place = (lax.axis_size(axis), lax.axis_index(axis))
    everything = jax.tree.map(
        lambda part, kind: lax.all_gather(part.astype(kind), axis),
        shard,
        jax.tree.map(lambda a: jnp.bfloat16 if a.dtype == jnp.float32 else a.dtype, shard),
    )
    start = jax.tree.map(
        lambda part, zero: jnp.broadcast_to(jnp.asarray(zero, part.dtype), part.shape),
        shard,
        identity,
    )

    def step(k, before):
        at = count - 1 - k
        reached = at > place
        new = combine(
            before, jax.tree.map(lambda part, own: part[at].astype(own.dtype), everything, shard)
        )
        return jax.tree.map(lambda a, b: jnp.where(reached, a, b), new, before)

    return lax.fori_loop(0, count, step, start)


def rms_parts(source):
    inverse = lax.rsqrt(jnp.mean(source * source, axis=-1, keepdims=True) + epsilon)
    return (source * inverse, inverse)


def orient(values, flipped):
    return values[::-1] if flipped else values


def join_pairs(earlier, later):
    return tuple(
        (
            (first[0] * second[0], first[1] * second[0] + second[1])
            for first, second in zip(earlier, later)
        )
    )


def join_single(earlier, later):
    return (earlier[0] * later[0], earlier[1] * later[0] + later[1])


def silu_slope(values):
    logistic = jax.nn.sigmoid(values)
    return logistic * (1.0 + values * (1.0 - logistic))


def conv_apply(padded_one, weight, bias_row, anticausal, tok_rows):
    rim_width = weight.shape[0] - 1
    running = jnp.zeros((tok_rows, weight.shape[1]), jnp.float32) + bias_row[None, :]
    for tap_index in range(weight.shape[0]):
        begin_at = 2 * rim_width - tap_index if anticausal else tap_index
        running = running + weight[tap_index][None, :] * padded_one[begin_at : begin_at + tok_rows]
    return running


def block_scan(step_row, input_row, write_row, read_row, a_matrix, start_state):
    tok_rows, lane_count = step_row.shape
    blocks = tok_rows // BLOCK

    def block_advance(carried, pieces):
        step_block, input_block, write_block, read_block = pieces
        decays = jnp.exp(step_block[:, None, :] * a_matrix[None])
        drives = write_block[:, :, None] * (step_block * input_block)[:, None, :]
        run_decay, run_drive = lax.associative_scan(join_single, (decays, drives), axis=0)
        states = run_decay * carried[None] + run_drive
        outputs = jnp.sum(read_block[:, :, None] * states, axis=1)
        return (states[-1], outputs)

    pieces = (
        step_row.reshape(blocks, BLOCK, lane_count),
        input_row.reshape(blocks, BLOCK, lane_count),
        write_row.reshape(blocks, BLOCK, -1),
        read_row.reshape(blocks, BLOCK, -1),
    )
    final_state, outputs = lax.scan(block_advance, start_state, pieces)
    return (outputs.reshape(tok_rows, lane_count), final_state)


def end_state(step_row, input_row, write_row, a_matrix):
    tok_rows, lane_count = step_row.shape
    blocks = tok_rows // BLOCK

    def end_advance(carried, pieces):
        step_block, input_block, write_block = pieces
        block_sum = jnp.sum(step_block, axis=0)
        later_sum = block_sum[None, :] - jnp.cumsum(step_block, axis=0)
        weighted = (
            jnp.exp(later_sum[:, None, :] * a_matrix[None])
            * write_block[:, :, None]
            * (step_block * input_block)[:, None, :]
        )
        return (jnp.exp(block_sum[None, :] * a_matrix) * carried + jnp.sum(weighted, axis=0), None)

    anchor = jnp.zeros(a_matrix.shape, jnp.float32)
    pieces = (
        step_row.reshape(blocks, BLOCK, lane_count),
        input_row.reshape(blocks, BLOCK, lane_count),
        write_row.reshape(blocks, BLOCK, -1),
    )
    final_state, _ = lax.scan(end_advance, anchor, pieces)
    return final_state


def entry_weight(step_row, grad_row, read_row, a_matrix):
    tok_rows, lane_count = step_row.shape
    blocks = tok_rows // BLOCK

    def entry_advance(carried, pieces):
        prior_sum, summed = carried
        step_block, grad_block, read_block = pieces
        running = prior_sum[None, :] + jnp.cumsum(step_block, axis=0)
        factors = jnp.exp(running[:, None, :] * a_matrix[None])
        summed = summed + jnp.sum(factors * read_block[:, :, None] * grad_block[:, None, :], axis=0)
        return ((running[-1], summed), None)

    anchor = (jnp.zeros((lane_count,), jnp.float32), jnp.zeros(a_matrix.shape, jnp.float32))
    pieces = (
        step_row.reshape(blocks, BLOCK, lane_count),
        grad_row.reshape(blocks, BLOCK, lane_count),
        read_row.reshape(blocks, BLOCK, -1),
    )
    (_, summed), _ = lax.scan(entry_advance, anchor, pieces)
    return summed


def scan_piece(
    step_row, input_row, write_row, read_row, gate_row, start_state, decay_row, skip_row
):
    a_matrix = -jnp.exp(decay_row)
    scanned, final_state = block_scan(
        step_row, input_row, write_row, read_row, a_matrix, start_state
    )
    mixed_out = (scanned + skip_row[None, :] * input_row) * jax.nn.silu(gate_row)
    return (mixed_out, final_state)


def on_device(
    hidden_in,
    lengths,
    norm_gain,
    in_weight,
    conv_weight,
    conv_bias,
    select_weight,
    step_weight,
    step_bias,
    decay_log,
    skip_gain,
    out_weight,
    cotangent,
):
    tok_rows = hidden_in.shape[0]
    col_width = hidden_in.shape[1]
    model_width = in_weight.shape[1]
    lane_count = in_weight.shape[2]
    rim_width = conv_weight.shape[1] - 1
    window = min(WINDOW, tok_rows * lax.axis_size("rows") // 2)
    shifted_row = lax.axis_index("rows") * tok_rows + window // 2
    offset = shifted_row % window
    window_id = shifted_row // window
    length_here = jnp.sum(
        jnp.where(jnp.arange(lengths.shape[0], dtype=jnp.int32) == window_id, lengths, 0)
    )
    valid_rows = (offset + jnp.arange(tok_rows, dtype=jnp.int32) < length_here).astype(jnp.float32)
    keep_start = jnp.where(offset == 0, 0.0, 1.0).astype(jnp.float32)
    keep_end = jnp.where((offset + tok_rows) % window == 0, 0.0, 1.0).astype(jnp.float32)
    gathered, cot_rows = (
        lax.all_gather(hidden_in, "ch", axis=1, tiled=True),
        lax.all_gather(cotangent, "ch", axis=1, tiled=True),
    )
    full_rows = gathered.astype(jnp.float32)
    sources = (full_rows[:, :model_width], full_rows[:, model_width:][:, ::-1])
    unit_rows, inverses, normed = ([], [], [])
    for source in sources:
        unit_one, inverse = rms_parts(source)
        unit_rows.append(unit_one)
        inverses.append(inverse)
        normed.append((unit_one * norm_gain[None, :]).astype(jnp.bfloat16))
    stacked = jnp.stack(normed)
    projected_in = jnp.einsum(
        "std,kde->kste", stacked, in_weight, preferred_element_type=jnp.float32
    )
    input_low = (projected_in[0] * valid_rows[None, :, None]).astype(jnp.bfloat16)
    gate_rows = projected_in[1]
    padded = extended(input_low, (("rows", 1),), rim_width).astype(jnp.float32)
    padded = jnp.concatenate(
        [
            padded[:, :rim_width] * keep_start,
            padded[:, rim_width : rim_width + tok_rows],
            padded[:, rim_width + tok_rows :] * keep_end,
        ],
        axis=1,
    )
    conv_pre, act_rows, partial_proj = ([], [], [])
    for member in range(4):
        strand, course = (member // 2, member % 2)
        pre_act = conv_apply(
            padded[strand],
            conv_weight[course],
            conv_bias[course],
            direction_flips[strand][course],
            tok_rows,
        )
        act_low = jax.nn.silu(pre_act).astype(jnp.bfloat16)
        conv_pre.append(pre_act)
        act_rows.append(act_low)
        partial_proj.append(
            jnp.dot(act_low, select_weight[course], preferred_element_type=jnp.float32)
        )
    projections = lax.psum(
        (partial_proj[0], partial_proj[1], partial_proj[2], partial_proj[3]), "ch"
    )
    step_lows, step_raws, oriented, totals, zero_ends = ([], [], [], [], [])
    for member in range(4):
        strand, course = (member // 2, member % 2)
        flipped = direction_flips[strand][course]
        projection = projections[member]
        step_low = projection[:, :R].astype(jnp.bfloat16)
        step_raw = (
            jnp.dot(step_low, step_weight[course], preferred_element_type=jnp.float32)
            + step_bias[course][None, :]
        )
        step_row = orient(jax.nn.softplus(step_raw) * valid_rows[:, None], flipped)
        input_row = orient(act_rows[member].astype(jnp.float32), flipped)
        write_row = orient(projection[:, R : R + N], flipped)
        read_row = orient(projection[:, R + N :], flipped)
        gate_row = orient(gate_rows[strand], flipped)
        a_matrix = -jnp.exp(decay_log[course])
        step_lows.append(step_low)
        step_raws.append(step_raw)
        oriented.append((step_row, input_row, write_row, read_row, gate_row))
        totals.append(jnp.exp(jnp.sum(step_row, axis=0)[None, :] * a_matrix))
        zero_ends.append(end_state(step_row, input_row, write_row, a_matrix))
    ones_state = jnp.ones_like(totals[0])
    zero_state = jnp.zeros_like(totals[0])
    identity = ((ones_state, zero_state), (ones_state, zero_state))
    up_prefix = carried_in(
        ((totals[0] * keep_start, zero_ends[0]), (totals[3] * keep_start, zero_ends[3])),
        "rows",
        join_pairs,
        identity,
        False,
    )
    down_prefix = entering(
        ((totals[1] * keep_end, zero_ends[1]), (totals[2] * keep_end, zero_ends[2])),
        "rows",
        join_pairs,
        identity,
    )
    entries = [
        up_prefix[0][1] * keep_start,
        down_prefix[0][1] * keep_end,
        down_prefix[1][1] * keep_end,
        up_prefix[1][1] * keep_start,
    ]
    pull_backs, outs_local = ([], [])
    for member in range(4):
        strand, course = (member // 2, member % 2)
        step_row, input_row, write_row, read_row, gate_row = oriented[member]
        (mixed_out, _), pull_back = jax.vjp(
            scan_piece,
            step_row,
            input_row,
            write_row,
            read_row,
            gate_row,
            entries[member],
            decay_log[course],
            skip_gain[course],
        )
        pull_backs.append(pull_back)
        outs_local.append(orient(mixed_out, direction_flips[strand][course]))
    mixed = [
        ((outs_local[2 * strand] + outs_local[2 * strand + 1]) * valid_rows[:, None]).astype(
            jnp.bfloat16
        )
        for strand in range(2)
    ]
    branches = [
        jnp.dot(mixed[strand], out_weight, preferred_element_type=jnp.float32)
        for strand in range(2)
    ]
    out_terms = jnp.concatenate([branches[0], branches[1][:, ::-1]], axis=1)
    added = lax.psum_scatter(out_terms, "ch", scatter_dimension=1, tiled=True)
    result = (hidden_in.astype(jnp.float32) + added).astype(jnp.bfloat16)
    cot_parts = (cot_rows[:, :model_width], cot_rows[:, model_width:][:, ::-1])
    grad_out = jnp.einsum(
        "te,td->ed", mixed[0], cot_parts[0], preferred_element_type=jnp.float32
    ) + jnp.einsum("te,td->ed", mixed[1], cot_parts[1], preferred_element_type=jnp.float32)
    grad_mixed = [
        jnp.einsum("td,ed->te", cot_parts[strand], out_weight, preferred_element_type=jnp.float32)
        * valid_rows[:, None]
        for strand in range(2)
    ]
    weights_in, grads_oriented = ([], [])
    for member in range(4):
        strand, course = (member // 2, member % 2)
        step_row, input_row, write_row, read_row, gate_row = oriented[member]
        grad_here = orient(grad_mixed[strand], direction_flips[strand][course])
        grads_oriented.append(grad_here)
        weights_in.append(
            entry_weight(
                step_row, grad_here * jax.nn.silu(gate_row), read_row, -jnp.exp(decay_log[course])
            )
        )
    high_adjoint = carried_in(
        (
            (totals[0] * keep_start, weights_in[0] * keep_start),
            (totals[3] * keep_start, weights_in[3] * keep_start),
        ),
        "rows",
        join_pairs,
        identity,
        True,
    )
    low_adjoint = carried_in(
        (
            (totals[1] * keep_end, weights_in[1] * keep_end),
            (totals[2] * keep_end, weights_in[2] * keep_end),
        ),
        "rows",
        join_pairs,
        identity,
        False,
    )
    exits = [high_adjoint[0][1], low_adjoint[0][1], low_adjoint[1][1], high_adjoint[1][1]]
    grad_step_w = [jnp.zeros((R, lane_count), jnp.float32), jnp.zeros((R, lane_count), jnp.float32)]
    grad_step_b = [jnp.zeros((lane_count,), jnp.float32), jnp.zeros((lane_count,), jnp.float32)]
    grad_decay = [jnp.zeros((N, lane_count), jnp.float32), jnp.zeros((N, lane_count), jnp.float32)]
    grad_skip = [jnp.zeros((lane_count,), jnp.float32), jnp.zeros((lane_count,), jnp.float32)]
    gate_grads = [
        jnp.zeros((tok_rows, lane_count), jnp.float32),
        jnp.zeros((tok_rows, lane_count), jnp.float32),
    ]
    proj_partial, act_grads = ([], [])
    for member in range(4):
        strand, course = (member // 2, member % 2)
        flipped = direction_flips[strand][course]
        grads = pull_backs[member]((grads_oriented[member], exits[member]))
        (
            grad_step,
            grad_input,
            grad_write,
            grad_read,
            grad_gate,
            _,
            grad_decay_one,
            grad_skip_one,
        ) = grads
        raw_grad = (
            orient(grad_step, flipped) * valid_rows[:, None] * jax.nn.sigmoid(step_raws[member])
        ).astype(jnp.bfloat16)
        grad_step_w[course] = grad_step_w[course] + jnp.einsum(
            "tr,te->re", step_lows[member], raw_grad, preferred_element_type=jnp.float32
        )
        grad_step_b[course] = grad_step_b[course] + jnp.sum(raw_grad.astype(jnp.float32), axis=0)
        step_in_grad = jnp.einsum(
            "te,re->tr", raw_grad, step_weight[course], preferred_element_type=jnp.float32
        )
        proj_partial.append(
            jnp.concatenate(
                [step_in_grad, orient(grad_write, flipped), orient(grad_read, flipped)], axis=1
            )
        )
        act_grads.append(orient(grad_input, flipped))
        gate_grads[strand] = gate_grads[strand] + orient(grad_gate, flipped)
        grad_decay[course] = grad_decay[course] + grad_decay_one
        grad_skip[course] = grad_skip[course] + grad_skip_one
    proj_grads = lax.psum(
        (proj_partial[0], proj_partial[1], proj_partial[2], proj_partial[3]), "ch"
    )
    grad_select = [
        jnp.zeros(select_weight.shape[1:], jnp.float32),
        jnp.zeros(select_weight.shape[1:], jnp.float32),
    ]
    grad_conv_w = [
        jnp.zeros(conv_weight.shape[1:], jnp.float32),
        jnp.zeros(conv_weight.shape[1:], jnp.float32),
    ]
    grad_conv_b = [jnp.zeros((lane_count,), jnp.float32), jnp.zeros((lane_count,), jnp.float32)]
    pad_grad = jnp.zeros(padded.shape, jnp.float32)
    for member in range(4):
        strand, course = (member // 2, member % 2)
        flipped = direction_flips[strand][course]
        proj_low = proj_grads[member].astype(jnp.bfloat16)
        grad_select[course] = grad_select[course] + jnp.einsum(
            "te,tp->ep", act_rows[member], proj_low, preferred_element_type=jnp.float32
        )
        act_total = act_grads[member] + jnp.einsum(
            "tp,ep->te", proj_low, select_weight[course], preferred_element_type=jnp.float32
        )
        pre_grad = act_total * silu_slope(conv_pre[member])
        grad_conv_b[course] = grad_conv_b[course] + jnp.sum(pre_grad, axis=0)
        for tap_index in range(rim_width + 1):
            begin_at = 2 * rim_width - tap_index if flipped else tap_index
            grad_conv_w[course] = (
                grad_conv_w[course]
                .at[tap_index]
                .add(jnp.sum(pre_grad * padded[strand, begin_at : begin_at + tok_rows], axis=0))
            )
            pad_grad = pad_grad.at[strand, begin_at : begin_at + tok_rows].add(
                conv_weight[course][tap_index][None, :] * pre_grad
            )
    rims = jnp.concatenate(
        [pad_grad[:, :rim_width] * keep_start, pad_grad[:, rim_width + tok_rows :] * keep_end],
        axis=1,
    )
    rim_rows = extended(rims, (("rows", 1),), rim_width)
    input_grad_rows = pad_grad[:, rim_width : rim_width + tok_rows]
    input_grad_rows = input_grad_rows.at[:, :rim_width].add(rim_rows[:, :rim_width])
    input_grad_rows = input_grad_rows.at[:, tok_rows - rim_width :].add(
        rim_rows[:, 3 * rim_width :]
    )
    input_grad_low = (
        input_grad_rows.astype(jnp.bfloat16) * valid_rows.astype(jnp.bfloat16)[None, :, None]
    )
    gate_grad_low = jnp.stack(gate_grads).astype(jnp.bfloat16)
    both_grads = jnp.stack([input_grad_low, gate_grad_low])
    grad_in = jnp.einsum("std,kste->kde", stacked, both_grads, preferred_element_type=jnp.float32)
    normed_grad = jnp.einsum(
        "kste,kde->std", both_grads, in_weight, preferred_element_type=jnp.float32
    )
    grad_terms = jnp.concatenate([normed_grad[0], normed_grad[1][:, ::-1]], axis=1)
    col_start = lax.axis_index("ch") * col_width
    full_grad = lax.psum(grad_terms, "ch")
    pieces = (full_grad[:, :model_width], full_grad[:, model_width:][:, ::-1])
    back_rows = []
    grad_gain = jnp.zeros((model_width,), jnp.float32)
    for strand in range(2):
        scaled = pieces[strand] * norm_gain[None, :]
        row_mean = jnp.mean(scaled * unit_rows[strand], axis=-1, keepdims=True)
        back_rows.append(inverses[strand] * (scaled - unit_rows[strand] * row_mean))
        grad_gain = grad_gain + jnp.sum(pieces[strand] * unit_rows[strand], axis=0)
    back_full = jnp.concatenate([back_rows[0], back_rows[1][:, ::-1]], axis=1)
    own_grad = lax.dynamic_slice_in_dim(back_full, col_start, col_width, 1)
    input_grad = cotangent.astype(jnp.float32) + own_grad
    summed = lax.psum(
        (
            grad_gain,
            grad_in,
            jnp.stack(grad_conv_w),
            jnp.stack(grad_conv_b),
            jnp.stack(grad_select),
            jnp.stack(grad_step_w),
            jnp.stack(grad_step_b),
            jnp.stack(grad_decay),
            jnp.stack(grad_skip),
            grad_out,
        ),
        "rows",
    )
    return (
        result,
        input_grad,
        summed[0],
        summed[1],
        summed[2],
        summed[3],
        summed[4],
        summed[5],
        summed[6],
        summed[7],
        summed[8],
        summed[9],
    )


def solution(mesh):
    placed = (
        P("rows", "ch"),
        P(),
        P(),
        P(None, None, "ch"),
        P(None, None, "ch"),
        P(None, "ch"),
        P(None, "ch", None),
        P(None, None, "ch"),
        P(None, "ch"),
        P(None, None, "ch"),
        P(None, "ch"),
        P("ch", None),
        P("rows", "ch"),
    )
    return jax.shard_map(
        on_device,
        mesh=mesh,
        in_specs=placed,
        out_specs=(
            P("rows", "ch"),
            P("rows", "ch"),
            P(),
            P(None, None, "ch"),
            P(None, None, "ch"),
            P(None, "ch"),
            P(None, "ch", None),
            P(None, None, "ch"),
            P(None, "ch"),
            P(None, None, "ch"),
            P(None, "ch"),
            P("ch", None),
        ),
        check_vma=False,
    )
```

profile of v0, /device:TPU:0, one launch (start us, length us, event | category | flops | bytes accessed | tf_op | source)
XLA Modules:
  0.0 2703.8 jit_solution(18069524099442490276)
XLA Ops:
  49.9 31.2 %all-reduce.335.cloned.1.call-done = (f32[256,48]{0,1:T(8,128)}, f32[256,48]{0,1:T(8,128)}, f32[256,48]{0,1:T(8,128)}, f32[256,48]{0,1:T(8,128)}) async-done(((f32[256,48]{0,1:T(8,128)}, f32[256,48]{0,1:T(8,128)}, f32[256,48]{0,1:T(8,128)}, f32[256,48]{0,1:T(8,128)}), (f32[256,48]{0,1:T(8,128)}, f32[256,48]{0,1:T(8,128)}, f32[256,48]{0,1:T(8,128)}, f32[256,48]{0,1:T(8,128)})) %all-reduce.335.cloned.1.call-update) | async-done | bytes 196624 | tf_op jit(solution)/shard_map/psum | solution.py:259
  91.3 10.8 while.681
  102.1 30.6 %all-gather = f32[128,128]{1,0:T(8,128)S(1)} all-gather(f32[16,128]{1,0:T(8,128)S(1)} %get-tuple-element.6384), channel_id=2, replica_groups=mesh['rows'=8,'ch'=4] {'rows'}, dimensions={0}, use_global_device_ids=true | all-gather | bytes 73728 | tf_op jit(solution)/shard_map/all_gather | solution.py:33
  133.4 10.8 while.682
  144.1 30.5 %all-gather.1 = f32[128,128]{1,0:T(8,128)S(1)} all-gather(f32[16,128]{1,0:T(8,128)S(1)} %get-tuple-element.6385), channel_id=3, replica_groups=mesh['rows'=8,'ch'=4] {'rows'}, dimensions={0}, use_global_device_ids=true | all-gather | bytes 73728 | tf_op jit(solution)/shard_map/all_gather | solution.py:33
  178.6 30.5 %all_gather.83 = f32[8,16,128]{2,1,0:T(8,128)S(1)} all-gather(f32[1,16,128]{2,1,0:T(8,128)S(1)} %get-tuple-element.11021), channel_id=1, replica_groups=mesh['rows'=8,'ch'=4] {'rows'}, dimensions={0}, use_global_device_ids=true | all-gather | bytes 73728 | tf_op jit(solution)/shard_map/all_gather | solution.py:33
  209.1 30.5 %all_gather.86 = f32[8,16,128]{2,1,0:T(8,128)S(1)} all-gather(f32[1,16,128]{2,1,0:T(8,128)S(1)} %get-tuple-element.11024), channel_id=1, replica_groups=mesh['rows'=8,'ch'=4] {'rows'}, dimensions={0}, use_global_device_ids=true | all-gather | bytes 73728 | tf_op jit(solution)/shard_map/all_gather | solution.py:33
  274.9 246.8 %while.678 = (s32[]{:T(128)}, f32[16,128]{1,0:T(8,128)}, f32[4,64,128]{2,1,0:T(8,128)}, f32[4,64,1,128]{3,2,1,0:T(1,128)}, f32[4,64,16,128]{3,2,1,0:T(8,128)}, /...) while((s32[]{:T(128)}, f32[16,128]{1,0:T(8,128)}, ...), condition=%wide.region_46.47_spmd, body=%wide.region_44.46_spmd.sunk | while | flops 2899970 | bytes 42123256 | solution.py:124
  282.0 10.3 pad.4838
  293.2 10.3 pad.4839
  343.7 10.3 pad.4838
  354.9 10.3 pad.4839
  405.5 10.3 pad.4838
  467.1 10.3 pad.4838
  522.5 12.1 while.686
  535.4 30.5 %all-gather.4 = f32[128,128]{1,0:T(8,128)S(1)} all-gather(f32[16,128]{1,0:T(8,128)S(1)} %broadcast_multiply_fusion.9), channel_id=6, replica_groups=mesh['rows'=8,'ch'=4] {'rows'}, dimensions={0}, use_global_device_ids=true | all-gather | bytes 73728 | tf_op jit(solution)/shard_map/all_gather | solution.py:33
  573.9 30.9 %all-gather.5 = f32[128,128]{1,0:T(8,128)S(1)} all-gather(f32[16,128]{1,0:T(8,128)S(1)} %broadcast_multiply_fusion.8), channel_id=7, replica_groups=mesh['rows'=8,'ch'=4] {'rows'}, dimensions={0}, use_global_device_ids=true | all-gather | bytes 73728 | tf_op jit(solution)/shard_map/all_gather | solution.py:33
  617.3 156.5 %while.693 = (s32[]{:T(128)}, f32[16,128]{1,0:T(8,128)}, f32[16,128]{1,0:T(8,128)}, f32[4,64,128]{2,1,0:T(8,128)}, f32[4,64,128]{2,1,0:T(8,128)}, /*index=5*/f32...) while((s32[]{:T(128)}, f32[16,128]{1,0:T(8,128)}, ...), condition=%wide.region_107.108_spmd.clone, body=%wide.region_100.107_spmd.clone.sunk | while | flops 5183492 | bytes 42439728 | solution.py:124
  775.4 18.7 while.684
  794.9 30.6 %all-gather.3 = bf16[128,128]{1,0:T(8,128)(2,1)S(1)} all-gather(bf16[16,128]{1,0:T(8,128)(2,1)S(1)} %convert_element_type.252), channel_id=5, replica_groups=mesh['rows'=8,'ch'=4] {'rows'}, dimensions={0}, use_global_device_ids=true | all-gather | bytes 36864 | tf_op jit(solution)/shard_map/all_gather | solution.py:48
  826.4 10.8 while.683
  837.1 30.6 %all-gather.2 = bf16[128,128]{1,0:T(8,128)(2,1)S(1)} all-gather(bf16[16,128]{1,0:T(8,128)(2,1)S(1)} %convert_element_type.246), channel_id=4, replica_groups=mesh['rows'=8,'ch'=4] {'rows'}, dimensions={0}, use_global_device_ids=true | all-gather | bytes 36864 | tf_op jit(solution)/shard_map/all_gather | solution.py:48
  867.8 30.6 %all_gather.89 = bf16[8,16,128]{2,1,0:T(8,128)(2,1)S(1)} all-gather(bf16[1,16,128]{2,1,0:T(8,128)(2,1)S(1)} %copy-done.302), channel_id=1, replica_groups=mesh['rows'=8,'ch'=4] {'rows'}, dimensions={0}, use_global_device_ids=true | all-gather | bytes 36864 | tf_op jit(solution)/shard_map/all_gather | solution.py:48
  898.4 30.6 %all_gather.92 = bf16[8,16,128]{2,1,0:T(8,128)(2,1)S(1)} all-gather(bf16[1,16,128]{2,1,0:T(8,128)(2,1)S(1)} %copy-done.301), channel_id=1, replica_groups=mesh['rows'=8,'ch'=4] {'rows'}, dimensions={0}, use_global_device_ids=true | all-gather | bytes 36864 | tf_op jit(solution)/shard_map/all_gather | solution.py:48
  964.7 247.0 %while.676 = (s32[]{:T(128)}, f32[16,128]{1,0:T(8,128)}, f32[4,64,128]{2,1,0:T(8,128)}, f32[4,64,1,128]{3,2,1,0:T(1,128)}, f32[4,64,16,128]{3,2,1,0:T(8,128)}, /...) while((s32[]{:T(128)}, f32[16,128]{1,0:T(8,128)}, ...), condition=%wide.region_40.41_spmd, body=%wide.region_38.40_spmd.sunk | while | flops 2899970 | bytes 42123256 | solution.py:124
  971.8 10.4 pad.4746
  983.0 10.3 pad.4747
  1033.6 10.4 pad.4746
  1044.8 10.3 pad.4747
  1095.3 10.4 pad.4746
  1106.5 10.3 pad.4747
  1157.1 10.4 pad.4746
  1168.3 10.3 pad.4747
  1246.9 247.2 %while.675 = (s32[]{:T(128)}, f32[16,128]{1,0:T(8,128)}, f32[4,64,128]{2,1,0:T(8,128)}, f32[4,64,1,128]{3,2,1,0:T(1,128)}, f32[4,64,16,128]{3,2,1,0:T(8,128)}, /...) while((s32[]{:T(128)}, f32[16,128]{1,0:T(8,128)}, ...), condition=%wide.region_21.22_spmd, body=%wide.region_19.21_spmd.sunk | while | flops 2899970 | bytes 42123256 | solution.py:124
  1265.2 10.3 pad.4701
  1276.6 10.3 pad.4699
  1327.1 10.3 pad.4701
  1338.4 10.3 pad.4699
  1388.9 10.3 pad.4701
  1400.2 10.3 pad.4699
  1450.7 10.3 pad.4701
  1462.0 10.3 pad.4699
  1496.8 156.6 %while.688 = (s32[]{:T(128)}, f32[16,128]{1,0:T(8,128)}, f32[16,128]{1,0:T(8,128)}, f32[4,64,128]{2,1,0:T(8,128)}, f32[4,64,128]{2,1,0:T(8,128)}, /*index=5*/f32...) while((s32[]{:T(128)}, f32[16,128]{1,0:T(8,128)}, ...), condition=%wide.region_65.66_spmd.clone, body=%wide.region_58.65_spmd.clone.sunk | while | flops 5183492 | bytes 42439720 | solution.py:124
  1690.1 247.3 %while.677 = (s32[]{:T(128)}, f32[16,128]{1,0:T(8,128)}, f32[4,64,128]{2,1,0:T(8,128)}, f32[4,64,1,128]{3,2,1,0:T(1,128)}, f32[4,64,16,128]{3,2,1,0:T(8,128)}, /...) while((s32[]{:T(128)}, f32[16,128]{1,0:T(8,128)}, ...), condition=%wide.region_43.44_spmd, body=%wide.region_41.43_spmd.sunk | while | flops 2899970 | bytes 42123256 | solution.py:124
  1708.4 10.3 pad.4793
  1719.8 10.3 pad.4791
  1770.3 10.3 pad.4793
  1781.6 10.3 pad.4791
  1832.2 10.3 pad.4793
  1843.5 10.3 pad.4791
  1893.9 10.3 pad.4793
  1905.2 10.3 pad.4791
  1940.1 15.2 while.689
  1955.9 30.5 %all-gather.6 = f32[128,128]{1,0:T(8,128)S(1)} all-gather(f32[16,128]{1,0:T(8,128)S(1)} %broadcast_multiply_fusion.5), channel_id=8, replica_groups=mesh['rows'=8,'ch'=4] {'rows'}, dimensions={0}, use_global_device_ids=true | all-gather | bytes 73728 | tf_op jit(solution)/shard_map/all_gather | solution.py:33
  1996.7 30.5 %all-gather.7 = f32[128,128]{1,0:T(8,128)S(1)} all-gather(f32[16,128]{1,0:T(8,128)S(1)} %broadcast_multiply_fusion.4), channel_id=9, replica_groups=mesh['rows'=8,'ch'=4] {'rows'}, dimensions={0}, use_global_device_ids=true | all-gather | bytes 73728 | tf_op jit(solution)/shard_map/all_gather | solution.py:33
  2027.3 30.5 %all_gather.100 = f32[8,16,128]{2,1,0:T(8,128)S(1)} all-gather(f32[1,16,128]{2,1,0:T(8,128)S(1)} %copy-done.297), channel_id=1, replica_groups=mesh['rows'=8,'ch'=4] {'rows'}, dimensions={0}, use_global_device_ids=true | all-gather | bytes 73728 | tf_op jit(solution)/shard_map/all_gather | solution.py:33
  2057.8 30.5 %all_gather.103 = f32[8,16,128]{2,1,0:T(8,128)S(1)} all-gather(f32[1,16,128]{2,1,0:T(8,128)S(1)} %copy-done.296), channel_id=1, replica_groups=mesh['rows'=8,'ch'=4] {'rows'}, dimensions={0}, use_global_device_ids=true | all-gather | bytes 73728 | tf_op jit(solution)/shard_map/all_gather | solution.py:33
  2091.0 143.3 %while.691 = (s32[]{:T(128)}, f32[16,128]{1,0:T(8,128)}, f32[16,128]{1,0:T(8,128)S(1)}, f32[4,64,128]{2,1,0:T(8,128)}, f32[4,64,128]{2,1,0:T(8,128)}, /*index=5*...) while((s32[]{:T(128)}, f32[16,128]{1,0:T(8,128)}, ...), condition=%wide.region_87.88_spmd.clone, body=%wide.region_80.87_spmd.clone.sunk | while | flops 5183492 | bytes 42669160 | solution.py:124
  2238.5 156.7 %while.692 = (s32[]{:T(128)}, f32[16,128]{1,0:T(8,128)}, f32[16,128]{1,0:T(8,128)}, f32[4,64,128]{2,1,0:T(8,128)}, f32[4,64,128]{2,1,0:T(8,128)}, /*index=5*/f32...) while((s32[]{:T(128)}, f32[16,128]{1,0:T(8,128)}, ...), condition=%wide.region_98.99_spmd.clone, body=%wide.region_91.98_spmd.clone.sunk | while | flops 5183492 | bytes 42439752 | solution.py:124
  2413.1 13.1 all-reduce.336
  2477.1 31.0 %all-reduce.329.cloned.1.call-done = f32[256,512]{1,0:T(8,128)} async-done(((f32[256,512]{1,0:T(8,128)}), f32[256,512]{1,0:T(8,128)}) %all-reduce.329.cloned.1.call-update) | async-done | bytes 524304 | tf_op jit(solution)/shard_map/psum | solution.py:474
  2511.9 73.0 %all-reduce.333.cloned.1.call-done = (f32[2,256,128]{1,2,0:T(8,128)}, f32[128,256]{1,0:T(8,128)}) async-done(((f32[2,256,128]{1,2,0:T(8,128)}, f32[128,256]{1,0:T(8,128)}), (f32[2,256,128]{1,2,0:T(8,128)}, f32[128,256]{1,0:T(8,128)})) %all-reduce.333.cloned.1.call-update) | async-done | bytes 393232 | tf_op jit(solution)/shard_map/psum | solution.py:486
  2586.7 21.3 reduce-scatter.2.cloned.1.call-done
  2609.6 75.6 %all-reduce.331.cloned.1.call-done = (f32[256]{0:T(256)}, f32[2,4,128]{2,1,0:T(4,128)}, f32[2,128]{1,0:T(2,128)}, f32[2,128,48]{1,2,0:T(8,128)}, f32[2,16,128]{2...) async-done(((f32[256]{0:T(256)}, f32[2,4,128]{2,1,0:T(4,128)}, f32[2,128]{1,0:T(2,128)}, f32[2,128,48]{1,2,0:T(8,128)}, ...) | async-done | bytes 90128 | tf_op jit(solution)/shard_map/psum | solution.py:486
  (5560 shorter events, 1705.2 us)
Async XLA Ops:
  7.2 73.9 %all-reduce.335.cloned.1.call-start = ((), (), s32[]{:S(2)}) async-start(), calls=%async_computation.5 | async-start | bytes 393216 | tf_op jit(solution)/shard_map/psum | solution.py:259
  16.9 72.6 %copy-start.300 = (f32[256]{0:T(256)}, f32[256]{0:T(256)S(1)}, u32[]{:S(2)}) copy-start(f32[256]{0:T(256)S(1)} %compare_convert_fusion) | copy-start | bytes 3076
  18.0 21.7 copy-start.151
  18.1 19.9 collective-permute-start
  21.6 16.4 collective-permute-start.1
  24.3 22.1 copy-start.309
  24.3 22.1 copy-start.311
  24.3 22.1 copy-start.313
  24.3 22.1 copy-start.315
  43.8 38.6 %copy-start.290 = (bf16[2,16,128]{2,1,0:T(8,128)(2,1)S(1)}, bf16[2,16,128]{2,1,0:T(8,128)(2,1)}, u32[]{:S(2)}) copy-start(bf16[2,16,128]{2,1,0:T(8,128)(2,1)} %param.128) | copy-start | bytes 24580
  46.3 2461.8 %all-reduce.329.cloned.1.call-start = ((), (), s32[]{:S(2)}) async-start(), calls=%async_computation.2 | async-start | bytes 1048576 | tf_op jit(solution)/shard_map/psum | solution.py:474
  102.0 74.0 %copy-start.193 = (f32[16,128]{1,0:T(8,128)}, f32[16,128]{1,0:T(8,128)S(1)}, u32[]{:S(2)}) copy-start(f32[16,128]{1,0:T(8,128)S(1)} %get-tuple-element.16946) | copy-start | bytes 24580
  144.1 99.9 %copy-start.195 = (f32[16,128]{1,0:T(8,128)}, f32[16,128]{1,0:T(8,128)S(1)}, u32[]{:S(2)}) copy-start(f32[16,128]{1,0:T(8,128)S(1)} %get-tuple-element.16949) | copy-start | bytes 24580
  293.2 21.6 copy-start.1
  354.9 21.6 copy-start.1
  416.6 21.6 copy-start.1
  478.3 21.6 copy-start.1
  521.7 44.2 %copy-start.196 = (f32[16,128]{1,0:T(8,128)S(1)}, f32[16,128]{1,0:T(8,128)}, u32[]{:S(2)}) copy-start(f32[16,128]{1,0:T(8,128)} %copy-done.195) | copy-start | bytes 24580
  521.7 44.2 %copy-start.252 = (f32[16,128]{1,0:T(8,128)S(1)}, f32[16,128]{1,0:T(8,128)}, u32[]{:S(2)}) copy-start(f32[16,128]{1,0:T(8,128)} %custom-call.7) | copy-start | bytes 24580
  534.7 80.7 %copy-start.244 = (f32[4,64,16]{1,0,2:T(4,128)}, f32[4,64,16]{1,0,2:T(4,128)S(1)}, u32[]{:S(2)}) copy-start(f32[4,64,16]{1,0,2:T(4,128)S(1)} %get-tuple-element.17072) | copy-start | bytes 49156
  565.9 51.4 %copy-start.202 = (pred[2]{0:T(512)(128)(4,1)S(1)}, pred[2]{0:T(512)(128)(4,1)}, u32[]{:S(2)}) copy-start(pred[2]{0:T(512)(128)(4,1)} %constant.1739.clone.2) | copy-start | bytes 10
  773.9 51.6 %copy-start.293 = (f32[256,16]{0,1:T(8,128)S(1)}, f32[256,16]{0,1:T(8,128)}, u32[]{:S(2)}) copy-start(f32[256,16]{0,1:T(8,128)} %get-tuple-element.11013) | copy-start | bytes 49156
  773.9 52.5 %copy-start.197 = (f32[16,128]{1,0:T(8,128)S(1)}, f32[16,128]{1,0:T(8,128)}, u32[]{:S(2)}) copy-start(f32[16,128]{1,0:T(8,128)} %copy-done.195) | copy-start | bytes 24580
  773.9 52.5 %copy-start.265 = (f32[16,128]{1,0:T(8,128)S(1)}, f32[16,128]{1,0:T(8,128)}, u32[]{:S(2)}) copy-start(f32[16,128]{1,0:T(8,128)} %custom-call.2) | copy-start | bytes 24580
  794.1 73.6 %copy-start.302 = (bf16[1,16,128]{2,1,0:T(8,128)(2,1)S(1)}, bf16[1,16,128]{2,1,0:T(8,128)(2,1)}, u32[]{:S(2)}) copy-start(bf16[1,16,128]{2,1,0:T(8,128)(2,1)} %get-tuple-element.11025) | copy-start | bytes 12292
  794.1 104.2 %copy-start.301 = (bf16[1,16,128]{2,1,0:T(8,128)(2,1)S(1)}, bf16[1,16,128]{2,1,0:T(8,128)(2,1)}, u32[]{:S(2)}) copy-start(bf16[1,16,128]{2,1,0:T(8,128)(2,1)} %get-tuple-element.11022) | copy-start | bytes 12292
  794.1 134.8 %copy-start.249 = (f32[16,128]{1,0:T(8,128)S(1)}, f32[16,128]{1,0:T(8,128)}, u32[]{:S(2)}) copy-start(f32[16,128]{1,0:T(8,128)} %custom-call.4) | copy-start | bytes 24580
  794.2 134.8 %copy-start.250 = (f32[16,128]{1,0:T(8,128)S(1)}, f32[16,128]{1,0:T(8,128)}, u32[]{:S(2)}) copy-start(f32[16,128]{1,0:T(8,128)} %custom-call.5) | copy-start | bytes 24580
  825.6 104.3 %copy-start.292 = (f32[256,16]{0,1:T(8,128)S(1)}, f32[256,16]{0,1:T(8,128)}, u32[]{:S(2)}) copy-start(f32[256,16]{0,1:T(8,128)} %get-tuple-element.11012) | copy-start | bytes 49156
  837.1 96.7 %copy-start.198 = (f32[16,128]{1,0:T(8,128)}, f32[16,128]{1,0:T(8,128)S(1)}, u32[]{:S(2)}) copy-start(f32[16,128]{1,0:T(8,128)S(1)} %get-tuple-element.16951) | copy-start | bytes 24580
  1265.2 21.7 copy-start.3
  1327.1 21.7 copy-start.3
  1388.9 21.7 copy-start.3
  1450.6 21.7 copy-start.3
  1708.4 21.7 copy-start.4
  1770.3 21.7 copy-start.4
  1832.1 21.7 copy-start.4
  1893.9 21.7 copy-start.4
  1937.4 49.1 %copy-start.189 = (f32[4,64,128]{2,1,0:T(8,128)S(1)}, f32[4,64,128]{2,1,0:T(8,128)}, u32[]{:S(2)}) copy-start(f32[4,64,128]{2,1,0:T(8,128)} %get-tuple-element.16944) | copy-start | bytes 393220
  1937.4 49.1 %copy-start.216 = (f32[256,128]{1,0:T(8,128)S(1)}, f32[256,128]{1,0:T(8,128)}, u32[]{:S(2)}) copy-start(f32[256,128]{1,0:T(8,128)} %rev.101) | copy-start | bytes 393220
  1937.4 49.1 %copy-start.217 = (f32[256,128]{1,0:T(8,128)S(1)}, f32[256,128]{1,0:T(8,128)}, u32[]{:S(2)}) copy-start(f32[256,128]{1,0:T(8,128)} %rev.106) | copy-start | bytes 393220
  1937.4 49.1 %copy-start.220 = (f32[4,64,128]{2,1,0:T(8,128)S(1)}, f32[4,64,128]{2,1,0:T(8,128)}, u32[]{:S(2)}) copy-start(f32[4,64,128]{2,1,0:T(8,128)} %get-tuple-element.6393) | copy-start | bytes 393220
  1937.4 49.1 %copy-start.221 = (f32[4,64,128]{2,1,0:T(8,128)S(1)}, f32[4,64,128]{2,1,0:T(8,128)}, u32[]{:S(2)}) copy-start(f32[4,64,128]{2,1,0:T(8,128)} %get-tuple-element.6440) | copy-start | bytes 393220
  1937.4 49.1 %copy-start.325 = (f32[128]{0:T(128)S(1)}, f32[128]{0:T(128)}, u32[]{:S(2)}) copy-start(f32[128]{0:T(128)} %get-tuple-element.11047) | copy-start | bytes 1540
  1940.1 48.7 %copy-start.194 = (f32[16,128]{1,0:T(8,128)S(1)}, f32[16,128]{1,0:T(8,128)}, u32[]{:S(2)}) copy-start(f32[16,128]{1,0:T(8,128)} %get-tuple-element.16948) | copy-start | bytes 24580
  1940.1 48.7 %copy-start.248 = (f32[16,128]{1,0:T(8,128)S(1)}, f32[16,128]{1,0:T(8,128)}, u32[]{:S(2)}) copy-start(f32[16,128]{1,0:T(8,128)} %custom-call.10) | copy-start | bytes 24580
  1986.5 40.8 %copy-start.297 = (f32[1,16,128]{2,1,0:T(8,128)S(1)}, f32[1,16,128]{2,1,0:T(8,128)}, u32[]{:S(2)}) copy-start(f32[1,16,128]{2,1,0:T(8,128)} %get-tuple-element.11026) | copy-start | bytes 24580
  1986.5 71.3 %copy-start.296 = (f32[1,16,128]{2,1,0:T(8,128)S(1)}, f32[1,16,128]{2,1,0:T(8,128)}, u32[]{:S(2)}) copy-start(f32[1,16,128]{2,1,0:T(8,128)} %get-tuple-element.11023) | copy-start | bytes 24580
  1988.8 102.2 %copy-start.107 = (f32[1,16,128]{2,1,0:T(8,128)S(1)}, f32[1,16,128]{2,1,0:T(8,128)}, u32[]{:S(2)}) copy-start(f32[1,16,128]{2,1,0:T(8,128)} %copy-done.106) | copy-start | bytes 24580
  1988.8 102.2 %copy-start.205 = (pred[2]{0:T(512)(128)(4,1)S(1)}, pred[2]{0:T(512)(128)(4,1)}, u32[]{:S(2)}) copy-start(pred[2]{0:T(512)(128)(4,1)} %get-tuple-element.17010) | copy-start | bytes 10
  1996.7 94.3 %copy-start.169 = (f32[4,64,128]{2,1,0:T(8,128)}, f32[4,64,128]{2,1,0:T(8,128)S(1)}, u32[]{:S(2)}) copy-start(f32[4,64,128]{2,1,0:T(8,128)S(1)} %get-tuple-element.16937) | copy-start | bytes 393220
  2430.6 22.6 copy-start.310
  2462.0 9.8 collective-permute-start.2
  2463.3 8.7 collective-permute-start.3
  2473.9 111.1 %all-reduce.333.cloned.1.call-start = ((), (), s32[]{:S(2)}) async-start(), calls=%async_computation.4 | async-start | bytes 786432 | tf_op jit(solution)/shard_map/psum | solution.py:486
  2474.2 34.0 %copy-start.133 = (f32[256,512]{1,0:T(8,128)S(1)}, f32[256,512]{1,0:T(8,128)}, u32[]{:S(2)}) copy-start(f32[256,512]{1,0:T(8,128)} %copy-done.132) | copy-start | bytes 1572868
  2474.2 34.0 %copy-start.306 = (f32[256]{0:T(256)S(1)}, f32[256]{0:T(256)}, u32[]{:S(2)}) copy-start(f32[256]{0:T(256)} %param.123) | copy-start | bytes 3076
  2474.2 34.0 %copy-start.308 = (f32[256]{0:T(256)S(1)}, f32[256]{0:T(256)}, u32[]{:S(2)}) copy-start(f32[256]{0:T(256)} %copy-done.307) | copy-start | bytes 3076
  2475.2 34.6 %copy-start.125 = (f32[256,256]{1,0:T(8,128)S(1)}, f32[256,256]{1,0:T(8,128)}, u32[]{:S(2)}) copy-start(f32[256,256]{1,0:T(8,128)} %copy-done.124) | copy-start | bytes 786436
  2475.2 34.6 %copy-start.304 = (f32[256]{0:T(256)S(1)}, f32[256]{0:T(256)}, u32[]{:S(2)}) copy-start(f32[256]{0:T(256)} %copy-done.303) | copy-start | bytes 3076
  2475.2 132.7 %reduce-scatter.2.cloned.1.call-start = ((), (), s32[]{:S(2)}) async-start(), calls=%async_computation.1 | async-start | bytes 655360 | tf_op jit(solution)/shard_map/reduce_scatter | solution.py:333
  2477.1 34.2 %copy-start.267 = (bf16[256,128]{1,0:T(8,128)(2,1)S(1)}, bf16[256,128]{1,0:T(8,128)(2,1)}, u32[]{:S(2)}) copy-start(bf16[256,128]{1,0:T(8,128)(2,1)} %param.133) | copy-start | bytes 196612
  2477.1 208.1 %all-reduce.331.cloned.1.call-start = ((), (), s32[]{:S(2)}) async-start(), calls=%async_computation.3 | async-start | bytes 180224 | tf_op jit(solution)/shard_map/psum | solution.py:486
  2509.8 98.1 %copy-start.269 = (bf16[256,128]{0,1:T(8,128)(2,1)S(1)}, bf16[256,128]{0,1:T(8,128)(2,1)}, u32[]{:S(2)}) copy-start(bf16[256,128]{0,1:T(8,128)(2,1)} %copy.210) | copy-start | bytes 196612
  (883 other events, 4449.1 us)
Sparse Core Ops, SparseCore 0:
  46.4 34.6 all-reduce.334
  2474.0 34.1 all-reduce.328
  2512.8 72.1 all-reduce.332
  2587.3 20.6 reduce-scatter.1
  2613.2 71.9 all-reduce.330
where the time goes:
time: 2750 us; the launch traced here: 2700 us
  local copies, waits for them, and re-layouts  1170 us (43%)
  other arithmetic  769 us (28%)
  blocking collectives  455 us (17%)
  waiting for transfers between devices  232 us (8%)
    pad x928, local copies, waits for them, and re-layouts, block_advance(): lax.associative_scan(join_single, (decays, drives), axis=0)  600 us
    all_gather x10, blocking collectives, carried_in(): gathered = jax.tree.map(lambda a: lax.all_gather(a, axis), part)  306 us
    mul x368, other arithmetic, join_single(): return (earlier[0] * later[0], earlier[1] * later[0] + later[1])  251 us
    dynamic_update_slice x144, other arithmetic, block_scan(): final_state, outputs = lax.scan(block_advance, start_state, pieces)  206 us
    dynamic_update_slice x224, local copies, waits for them, and re-layouts, block_scan(): final_state, outputs = lax.scan(block_advance, start_state, pieces)  172 us
    another operation x201, local copies, waits for them, and re-layouts  150 us
    psum x2, waiting for transfers between devices, on_device(): lax.psum((grad_gain, grad_in, jnp.stack(grad_conv_w), jnp.stack(grad_conv...  149 us
    all_gather x4, blocking collectives, entering(): lax.all_gather(part.astype(kind), axis)  122 us

commit v1 on v0

v1 whole, which is shorter than its diff:
```python
import functools

import jax
import jax.numpy as jnp
from jax import lax
from jax.experimental import pallas as pl
from jax.experimental.pallas import tpu as pltpu
from jax.sharding import PartitionSpec as P

N = 16
R = 16
WINDOW = 16384
LANES = 128
CHUNKS = 8
EPSILON = 1e-06
LOG2E = 1.4426950408889634
F32 = jnp.float32
BF16 = jnp.bfloat16
VM = pl.BlockSpec(memory_space=pltpu.VMEM)
SM = pl.BlockSpec(memory_space=pltpu.SMEM)
FLIPS = (False, True, True, False)


def nn(left, right):
    return lax.dot_general(left, right, (((1,), (0,)), ((), ())), preferred_element_type=F32)


def nt(left, right):
    return lax.dot_general(left, right, (((1,), (1,)), ((), ())), preferred_element_type=F32)


def tn(left, right):
    return lax.dot_general(left, right, (((0,), (0,)), ((), ())), preferred_element_type=F32)


def iota(shape, dim):
    return lax.broadcasted_iota(jnp.int32, shape, dim)


def one_hot(mask):
    return jnp.where(mask, 1.0, 0.0).astype(BF16)


def permuter(tok):
    steps = tok // CHUNKS
    row, col = iota((tok, tok), 0), iota((tok, tok), 1)
    return one_hot((row % CHUNKS) * steps + row // CHUNKS == col)


def unpermuter(tok):
    steps = tok // CHUNKS
    row, col = iota((tok, tok), 0), iota((tok, tok), 1)
    return one_hot((col % CHUNKS) * steps + col // CHUNKS == row)


def mirror(width):
    return one_hot(iota((width, width), 0) + iota((width, width), 1) == width - 1)


def sigmoid(v):
    return 1.0 / (1.0 + jnp.exp(-v))


def silu(v):
    return v * sigmoid(v)


def silu_slope(v):
    logistic = sigmoid(v)
    return logistic * (1.0 + v * (1.0 - logistic))


def softplus(v):
    return jnp.maximum(v, 0.0) + jnp.log1p(jnp.exp(-jnp.abs(v)))


def low(v):
    return v.astype(BF16)


class Geometry:
    def __init__(self, tok, rows):
        self.tok = tok
        self.rows = rows
        self.window = min(WINDOW, tok * rows // 2)
        self.members = self.window // tok
        self.steps = tok // CHUNKS

    def place(self, lengths_ref):
        row = lax.axis_index("rows")
        shifted = row * self.tok + self.window // 2
        offset = lax.rem(shifted, self.window)
        length = lengths_ref[lax.div(shifted, self.window)]
        return row, offset, length

    def valid(self, lengths_ref):
        _, offset, length = self.place(lengths_ref)
        row = iota((self.tok, 1), 0)
        token = (row % CHUNKS) * self.steps + row // CHUNKS
        return jnp.where(offset + token < length, 1.0, 0.0)

    def local(self):
        row = lax.axis_index("rows")
        return lax.rem(row + self.members // 2, self.members)

    def near(self):
        return [(i, i ^ 1) for i in range(self.rows)]

    def far(self):
        if self.members == 4:
            return self.swaps(lambda k: 3 - k)
        out = []
        for i in range(1, self.rows, 2):
            out += [(i, (i + 1) % self.rows), ((i + 1) % self.rows, i)]
        return out

    def across(self):
        return self.swaps(lambda k: (k + 2) % 4)

    def swaps(self, other):
        out = []
        for i in range(self.rows):
            local = (i + 2) % 4
            j = i - local + other(local)
            out.append((i, j if 0 <= j < self.rows else i ^ 1))
        return out


def run(kernel, outs, *args, smem=0, scratch=(), name=None, cost=None):
    single = isinstance(outs, tuple)
    shapes = [outs] if single else list(outs)
    got = pl.pallas_call(
        kernel,
        out_shape=[jax.ShapeDtypeStruct(s, d) for s, d in shapes],
        in_specs=[SM] * smem + [VM] * (len(args) - smem),
        out_specs=[VM] * len(shapes),
        scratch_shapes=list(scratch),
        name=name,
        compiler_params=pltpu.CompilerParams(vmem_limit_bytes=48 * 1024 * 1024),
    )(*args)
    return got[0] if single else got


def assemble(refs, scratch):
    mine = lax.axis_index("ch")
    for distance, ref in enumerate(refs):
        scratch[lax.bitwise_xor(mine, distance)] = ref[...]
    return (
        jnp.concatenate([scratch[0], scratch[1]], axis=1),
        jnp.concatenate([scratch[2], scratch[3]], axis=1),
    )


def project_kernel(geo, lengths, xo, xc, xy, xd, gain, w, normed, inputs, gates, near, far, scratch):
    tok = geo.tok
    width = w.shape[1]
    valid = geo.valid(lengths)
    sides = assemble((xo, xc, xy, xd), scratch)
    even = lax.rem(lax.axis_index("rows"), 2) == 0
    for half, side in enumerate(sides):
        first, last = side[:16], side[tok - 16 :]
        lanes = slice(half * width, (half + 1) * width)
        near[:, lanes] = jnp.where(even, last.astype(F32), first.astype(F32)).astype(BF16)
        far[:, lanes] = jnp.where(even, first.astype(F32), last.astype(F32)).astype(BF16)
    mover = permuter(tok)
    both = jnp.concatenate([w[0], w[1]], axis=1)
    for strand in range(2):
        side = sides[strand]
        if strand == 1:
            side = low(nn(side, mirror(width)))
        source = nn(mover, side)
        inverse = lax.rsqrt(jnp.mean(source * source, axis=-1, keepdims=True) + EPSILON)
        rows = low(source * inverse * gain[...])
        normed[strand] = rows
        out = nn(rows, both)
        lanes = out.shape[1] // 2
        inputs[strand] = low(out[:, :lanes] * valid)
        gates[strand] = out[:, lanes:]


def cotangent_kernel(geo, lengths, co, cc, cy, cd, gates, ow, moved, gm, dys, scratch):
    tok = geo.tok
    valid = geo.valid(lengths)
    sides = assemble((co, cc, cy, cd), scratch)
    mover = permuter(tok)
    for strand in range(2):
        side = sides[strand]
        if strand == 1:
            side = low(nn(side, mirror(side.shape[1])))
        rows = low(nn(mover, side))
        moved[strand] = rows
        grad = nt(rows, ow[...]) * valid
        gm[strand] = grad
        dys[strand] = grad * silu(gates[strand])


def rim_valid(geo, lengths_ref):
    _, offset, length = geo.place(lengths_ref)
    row = iota((32, 1), 0)
    token = jnp.where(row < 16, row - 16, geo.tok + row - 16) + offset
    index = token - offset + lax.axis_index("rows") * geo.tok
    inside = (token >= 0) & (token < geo.window) & (token < length)
    inside = inside & (index >= 0) & (index < geo.tok * geo.rows)
    return jnp.where(inside, 1.0, 0.0)


def fill_padded(padded, main, rims, steps):
    rim = padded.shape[0] // CHUNKS - steps
    rim = rim // 2
    lanes = main.shape[1]
    sub = iota((CHUNKS, lanes), 0)
    padded[rim * CHUNKS : (rim + steps) * CHUNKS] = main
    for k in range(1, rim + 1):
        block = main[(steps - k) * CHUNKS : (steps - k + 1) * CHUNKS]
        moved = pltpu.roll(block, 1, 0)
        edge = jnp.broadcast_to(rims[16 - k : 17 - k], (CHUNKS, lanes))
        padded[(rim - k) * CHUNKS : (rim - k + 1) * CHUNKS] = jnp.where(sub == 0, edge, moved)
    for k in range(rim):
        block = main[k * CHUNKS : (k + 1) * CHUNKS]
        moved = pltpu.roll(block, CHUNKS - 1, 0)
        edge = jnp.broadcast_to(rims[16 + k : 17 + k], (CHUNKS, lanes))
        at = rim + steps + k
        padded[at * CHUNKS : (at + 1) * CHUNKS] = jnp.where(sub == CHUNKS - 1, edge, moved)


def tap_start(tap, taps, flipped):
    return (2 * (taps - 1) - tap if flipped else tap) * CHUNKS


def conv_kernel(
    geo, lengths, inputs, near, far, gain, w, cw, cb, sw, padded, rims_normed, pre, act, message, select
):
    tok, steps = geo.tok, geo.steps
    taps = cw.shape[1]
    lanes = w.shape[2]
    width = w.shape[1]
    edge_valid = rim_valid(geo, lengths)
    even = lax.rem(lax.axis_index("rows"), 2) == 0
    select[...] = jnp.zeros_like(select)
    columns = sw.shape[2]
    for course in range(2):
        select[course, :, 64 * course : 64 * course + columns] = sw[course].astype(F32)
    for strand in range(2):
        part = slice(strand * width, (strand + 1) * width)
        one, two = near[:, part].astype(F32), far[:, part].astype(F32)
        source = jnp.concatenate([jnp.where(even, two, one), jnp.where(even, one, two)], axis=0)
        if strand == 1:
            source = nn(low(source), mirror(width))
        inverse = lax.rsqrt(jnp.mean(source * source, axis=-1, keepdims=True) + EPSILON)
        rows = low(source * inverse * gain[...])
        rims_normed[strand] = rows
        edges = low(nn(rows, w[0]) * edge_valid).astype(F32)
        main = inputs[strand].astype(F32)
        fill_padded(padded.at[strand], main, edges, steps)
        total = jnp.zeros((tok, LANES), F32)
        for course in range(2):
            member = 2 * strand + course
            running = jnp.broadcast_to(cb[course : course + 1], (tok, lanes))
            for tap in range(taps):
                at = tap_start(tap, taps, FLIPS[member])
                running = running + cw[course, tap : tap + 1] * padded[strand, at : at + tok]
            pre[member] = running
            active = low(silu(running))
            act[member] = active
            total = total + nn(active, low(select[course]))
        message[strand] = low(total)


def bcast(block, lane):
    return jnp.broadcast_to(block[:, lane : lane + 1], block.shape)


def summary_kernel(
    geo, lengths, one, two, act, dys, stw, stb, decay,
    proj, raw, step, drive, chunk_p, chunk_h, chunk_w, near, far, a2, up, down,
):
    tok, steps = geo.tok, geo.steps
    valid = geo.valid(lengths)
    for strand in range(2):
        total = one[strand].astype(F32) + two[strand].astype(F32)
        for course in range(2):
            member = 2 * strand + course
            here = total if course == 0 else pltpu.roll(total, 64, 1)
            proj[member] = here
            step_raw = nn(low(here)[:, :R], stw[course]) + stb[course : course + 1]
            step_row = softplus(step_raw) * valid
            raw[member] = step_raw
            step[member] = step_row
            drive[member] = step_row * act[member].astype(F32)
    for course in range(2):
        table = -LOG2E * jnp.exp(decay[course])
        for n in range(N):
            a2[course, n] = jnp.broadcast_to(table[n : n + 1], (CHUNKS, LANES))

    def sweep(member, flipped):
        strand, course = member // 2, lax.rem(member, 2)
        for base in range(0, N, 8):

            def body(k, carry):
                ps, hs, ws = carry
                t = steps - 1 - k if flipped else k
                rows = pl.ds(pl.multiple_of(t * CHUNKS, CHUNKS), CHUNKS)
                s, d, y = step[member, rows], drive[member, rows], dys[strand, rows]
                block = proj[member, rows]
                np_, nh, nw = [], [], []
                for i in range(8):
                    n = base + i
                    decay_here = jnp.exp2(s * a2[course, n])
                    p = ps[i] * decay_here
                    np_.append(p)
                    nh.append(hs[i] * decay_here + bcast(block, R + n) * d)
                    nw.append(ws[i] + p * (bcast(block, R + N + n) * y))
                return tuple(np_), tuple(nh), tuple(nw)

            zero = jnp.zeros((CHUNKS, LANES), F32)
            start = (tuple([zero + 1.0] * 8), (zero,) * 8, (zero,) * 8)
            ps, hs, ws = lax.fori_loop(0, steps, body, start, unroll=2)
            for i in range(8):
                rows = slice((base + i) * CHUNKS, (base + i + 1) * CHUNKS)
                chunk_p[member, rows] = ps[i]
                chunk_h[member, rows] = hs[i]
                chunk_w[member, rows] = ws[i]

    lax.fori_loop(0, 2, lambda i, c: (sweep(3 * i, False), c)[1], 0)
    lax.fori_loop(0, 2, lambda i, c: (sweep(1 + i, True), c)[1], 0)

    slots = {0: (0, 2), 3: (1, 3), 1: (2, 0), 2: (3, 1)}
    for member in range(4):
        h = jnp.zeros((N, LANES), F32)
        w = jnp.zeros((N, LANES), F32)
        order = list(range(CHUNKS))
        forward = order[::-1] if FLIPS[member] else order
        for j in forward:
            rows = pl.ds(j, N, stride=CHUNKS)
            h = chunk_p[member, rows] * h + chunk_h[member, rows]
        for j in forward[::-1]:
            rows = pl.ds(j, N, stride=CHUNKS)
            w = chunk_p[member, rows] * w + chunk_w[member, rows]
        length = jnp.sum(step[member], axis=0, keepdims=True)
        slot_up, slot_down = slots[member]
        goes_up, goes_down = (w, h) if FLIPS[member] else (h, w)
        up[slot_up * N : (slot_up + 1) * N] = goes_up
        down[slot_down * N : (slot_down + 1) * N] = goes_down
        up[4 * N + slot_up : 4 * N + slot_up + 1] = length
        down[4 * N + slot_down : 4 * N + slot_down + 1] = length
    up[4 * N + 4 :] = jnp.zeros((4, LANES), F32)
    down[4 * N + 4 :] = jnp.zeros((4, LANES), F32)
    if near is not None:
        local = geo.local()
        near[...] = jnp.where(lax.rem(local, 2) == 0, up[...], down[...])
        far[...] = jnp.where(local < 2, up[...], down[...])


UP_MEMBERS = (0, 3, 1, 2)
DOWN_MEMBERS = (1, 2, 0, 3)


def scan_kernel(
    geo, lengths, slot_refs, act, proj, raw, step, drive, chunk_p, chunk_h, chunk_w,
    dys, gm, gates, stw, decay, skip,
    mixed, dgate, dact, message, small,
    slots, a2, a1, enter, adjoint, states, quads, picks, out_y, slope_y, pull_y, dproj, dacc,
):
    tok, steps = geo.tok, geo.steps
    count = geo.members
    valid = geo.valid(lengths)
    row = lax.axis_index("rows")
    local = geo.local()
    base_row = row - local
    if len(slot_refs) == 1:
        slots = slot_refs[0]
    else:
        slots[local] = jnp.zeros(slots.shape[1:], F32)
        others = (lax.bitwise_xor(local, 1), lax.rem(local + 2, 4), 3 - local)
        for at, ref in zip(others, slot_refs):
            slots[at] = ref[...]
    for course in range(2):
        natural = -jnp.exp(decay[course])
        for n in range(N):
            wide = jnp.broadcast_to(natural[n : n + 1], (CHUNKS, LANES))
            a1[course, n] = wide
            a2[course, n] = wide * LOG2E
    depth = picks.shape[0]
    picks[...] = one_hot(iota((depth, LANES), 1) == R + iota((depth, LANES), 0) // LANES)
    dacc[...] = jnp.zeros_like(dacc)

    def fold(ascending, carried):
        members = UP_MEMBERS if ascending else DOWN_MEMBERS
        tables = [-LOG2E * jnp.exp(decay[m % 2]) for m in members]

        def one(i, carried):
            k = i if ascending else count - 1 - i
            there = base_row + k
            use = (k < local) if ascending else (k > local)
            use = use & (there >= 0) & (there < geo.rows)
            out = []
            for q in range(4):
                length = slots[k, 4 * N + q : 4 * N + q + 1]
                new = jnp.exp2(tables[q] * length) * carried[q] + slots[k, q * N : (q + 1) * N]
                out.append(jnp.where(use, new, carried[q]))
            return tuple(out)

        return lax.fori_loop(0, count, one, carried)

    zero = (jnp.zeros((N, LANES), F32),) * 4
    from_below = fold(True, zero)
    from_above = fold(False, zero)
    order = list(range(CHUNKS))
    for q in range(4):
        for value, member, js in (
            (from_below[q], UP_MEMBERS[q], order),
            (from_above[q], DOWN_MEMBERS[q], order[::-1]),
        ):
            target, source = (enter, chunk_h) if q < 2 else (adjoint, chunk_w)
            for j in js:
                rows = pl.ds(j, N, stride=CHUNKS)
                target[member, rows] = value
                value = chunk_p[member, rows] * value + source[member, rows]

    def sweep(member, flipped):
        strand, course = member // 2, lax.rem(member, 2)
        states[: N * CHUNKS] = enter[member]

        def ahead(i, carry):
            hs = list(carry)
            kept = []
            for sub in range(2):
                k = 2 * i + sub
                t = steps - 1 - k if flipped else k
                rows = pl.ds(pl.multiple_of(t * CHUNKS, CHUNKS), CHUNKS)
                s, d, y = step[member, rows], drive[member, rows], dys[strand, rows]
                block = proj[member, rows]
                total = jnp.zeros((CHUNKS, LANES), F32)
                products = []
                for n in range(N):
                    hs[n] = hs[n] * jnp.exp2(s * a2[course, n]) + bcast(block, R + n) * d
                    total = total + bcast(block, R + N + n) * hs[n]
                    products.append(y * hs[n])
                    at = pl.multiple_of(((k + 1) * N + n) * CHUNKS, CHUNKS)
                    states[pl.ds(at, CHUNKS)] = hs[n]
                out_y[member, rows] = total
                kept.append(products)
            pair = steps // 2 - 1 - i if flipped else i
            rows = pl.ds(pl.multiple_of(pair * 16, 16), 16)
            first, second = (kept[1], kept[0]) if flipped else (kept[0], kept[1])
            for n in range(N):
                both = low(jnp.concatenate([first[n], second[n]], axis=0))
                quads[rows, (N + n) * LANES : (N + n + 1) * LANES] = both
            return tuple(hs)

        start = tuple(enter[member, n * CHUNKS : (n + 1) * CHUNKS] for n in range(N))
        lax.fori_loop(0, steps // 2, ahead, start)

        def back(i, carry):
            cs, ds = list(carry[0]), list(carry[1])
            kept = []
            for sub in range(2):
                k = steps - 1 - (2 * i + sub)
                t = steps - 1 - k if flipped else k
                rows = pl.ds(pl.multiple_of(t * CHUNKS, CHUNKS), CHUNKS)
                s, d, y = step[member, rows], drive[member, rows], dys[strand, rows]
                block = proj[member, rows]
                pulled = jnp.zeros((CHUNKS, LANES), F32)
                slope = jnp.zeros((CHUNKS, LANES), F32)
                products = []
                for n in range(N):
                    lam = y * bcast(block, R + N + n) + cs[n]
                    pulled = pulled + lam * bcast(block, R + n)
                    products.append(lam * d)
                    cs[n] = lam * jnp.exp2(s * a2[course, n])
                    at = pl.multiple_of((k * N + n) * CHUNKS, CHUNKS)
                    u = cs[n] * states[pl.ds(at, CHUNKS)]
                    slope = slope + u * a1[course, n]
                    ds[n] = ds[n] + u * s
                slope_y[member, rows] = slope
                pull_y[member, rows] = pulled
                kept.append(products)
            pair = i if flipped else steps // 2 - 1 - i
            rows = pl.ds(pl.multiple_of(pair * 16, 16), 16)
            first, second = (kept[0], kept[1]) if flipped else (kept[1], kept[0])
            for n in range(N):
                both = low(jnp.concatenate([first[n], second[n]], axis=0))
                quads[rows, n * LANES : (n + 1) * LANES] = both
            return tuple(cs), tuple(ds)

        start = tuple(adjoint[member, n * CHUNKS : (n + 1) * CHUNKS] for n in range(N))
        zeros = (jnp.zeros((CHUNKS, LANES), F32),) * N
        _, ds = lax.fori_loop(0, steps // 2, back, (start, zeros))
        for n in range(N):
            rows = slice(n * CHUNKS, (n + 1) * CHUNKS)
            dacc[course, rows] = dacc[course, rows] + ds[n]
        dproj[member] = nn(quads[...], picks[...])

    lax.fori_loop(0, 2, lambda i, c: (sweep(3 * i, False), c)[1], 0)
    lax.fori_loop(0, 2, lambda i, c: (sweep(1 + i, True), c)[1], 0)

    small[...] = jnp.zeros_like(small)
    for course in range(2):
        for n in range(N):
            total = jnp.sum(dacc[course, n * CHUNKS : (n + 1) * CHUNKS], axis=0, keepdims=True)
            at = 2 * R + course * N + n
            small[at : at + 1] = total * a1[course, n, :1]
    for strand in range(2):
        joined = jnp.zeros((tok, LANES), F32)
        sent = jnp.zeros((tok, LANES), F32)
        grad = dys[strand]
        for course in range(2):
            member = 2 * strand + course
            active = act[member].astype(F32)
            joined = joined + out_y[member] + skip[course : course + 1] * active
            raw_grad = slope_y[member] + pull_y[member] * active
            rounded = low(raw_grad * valid * sigmoid(raw[member]))
            dact[member] = pull_y[member] * step[member] + grad * skip[course : course + 1]
            rows = slice(course * R, (course + 1) * R)
            small[rows] += tn(low(proj[member]), rounded)[:R]
            at = 2 * R + 2 * N + course
            small[at : at + 1] += jnp.sum(rounded.astype(F32), axis=0, keepdims=True)
            small[at + 2 : at + 3] += jnp.sum(grad * active, axis=0, keepdims=True)
            wide = jnp.concatenate([stw[course], jnp.zeros((LANES - R, LANES), BF16)], axis=0)
            here = dproj[member] + nt(rounded, wide)
            sent = sent + (here if course == 0 else pltpu.roll(here, 64, 1))
        message[strand] = low(sent)
        gate = gates[strand]
        mixed[strand] = low(joined * silu(gate) * valid)
        dgate[strand] = low(gm[strand] * joined * silu_slope(gate))


def dense_kernel(geo, mixed, ow, moved, dgate, normed, w, kept, sent, g_out, g_gate, dn_gate):
    tok = geo.tok
    mover = unpermuter(tok)
    width = w.shape[1]
    turn = mirror(width)
    second = lax.axis_index("ch") >= 2
    branches = []
    grad_out = jnp.zeros(g_out.shape, F32)
    grad_gate = jnp.zeros(g_gate.shape, F32)
    for strand in range(2):
        out_w, gate_w = ow[...], w[1]
        if strand == 1:
            out_w, gate_w = low(nn(out_w, turn)), low(nn(turn, gate_w))
        branches.append(nn(low(nn(mover, mixed[strand])), out_w))
        grad_out = grad_out + tn(mixed[strand], moved[strand])
        grad_gate = grad_gate + tn(normed[strand], dgate[strand])
        dn_gate[strand] = nt(low(nn(mover, dgate[strand])), gate_w)
    kept[...] = jnp.where(second, branches[1], branches[0])
    sent[...] = low(jnp.where(second, branches[0], branches[1]))
    g_out[...] = grad_out
    g_gate[...] = grad_gate


GRAD_ROWS = 992


def conv_back_kernel(
    geo, lengths, one, two, act, dact, pre, padded, cw, select, normed, rims_normed, gain, w,
    g_gate, g_out, small, res_kept, res_got,
    xg, near, far, keep, send, gain_part, res_own, res_sent,
    pad_grad, pack,
):
    tok, steps = geo.tok, geo.steps
    taps = cw.shape[1]
    width = w.shape[1]
    valid = geo.valid(lengths)
    edge_valid = rim_valid(geo, lengths)
    even = lax.rem(lax.axis_index("rows"), 2) == 0
    rim = taps - 1
    sub = iota((CHUNKS, LANES), 0)
    pack[...] = jnp.zeros_like(pack)
    grad_select = jnp.zeros((LANES, LANES), F32)
    grad_in = jnp.zeros((width, LANES), F32)
    at_conv = 3 * width + LANES
    for strand in range(2):
        pad_grad[...] = jnp.zeros_like(pad_grad)
        rounded = low(one[strand].astype(F32) + two[strand].astype(F32))
        lane = iota((LANES, LANES), 1)
        for course in range(2):
            member = 2 * strand + course
            here = tn(act[member], rounded)
            grad_select = grad_select + jnp.where((lane >= 64) == (course == 1), here, 0.0)
            total = dact[member] + nt(rounded, low(select[course]))
            grad = total * silu_slope(pre[member])
            row = at_conv + 8 + course
            pack[row : row + 1] += jnp.sum(grad, axis=0, keepdims=True)
            for tap in range(taps):
                at = tap_start(tap, taps, FLIPS[member])
                row = at_conv + course * taps + tap
                pack[row : row + 1] += jnp.sum(grad * padded[strand, at : at + tok], axis=0, keepdims=True)
                pad_grad[at : at + tok] += cw[course, tap : tap + 1] * grad
        before = [jnp.zeros((1, LANES), F32)] * (16 - rim)
        after = []
        for k in range(rim, 0, -1):
            block = pad_grad[(rim - k) * CHUNKS : (rim - k + 1) * CHUNKS]
            before.append(block[:1])
            moved = jnp.where(sub == CHUNKS - 1, 0.0, pltpu.roll(block, CHUNKS - 1, 0))
            at = (rim + steps - k) * CHUNKS
            pad_grad[at : at + CHUNKS] += moved
        for k in range(rim):
            at = (rim + steps + k) * CHUNKS
            block = pad_grad[at : at + CHUNKS]
            after.append(block[CHUNKS - 1 :])
            moved = jnp.where(sub == 0, 0.0, pltpu.roll(block, 1, 0))
            at = (rim + k) * CHUNKS
            pad_grad[at : at + CHUNKS] += moved
        after += [jnp.zeros((1, LANES), F32)] * (16 - rim)
        rims = jnp.concatenate(before + after, axis=0) * edge_valid
        main = pad_grad[rim * CHUNKS : (rim + steps) * CHUNKS]
        xg[strand] = main
        grad_in = grad_in + tn(normed[strand], low(main * valid)) + tn(rims_normed[strand], low(rims))
        near[strand] = jnp.where(even, rims[16:], rims[:16])
        far[strand] = jnp.where(even, rims[:16], rims[16:])
    pack[:width] = grad_in
    pack[width : 2 * width] = g_gate[...]
    pack[2 * width : 2 * width + LANES] = g_out[:, :LANES]
    pack[2 * width + LANES : 3 * width] = g_out[:, LANES:]
    pack[3 * width : at_conv] = grad_select
    pack[at_conv + 16 : at_conv + 16 + small.shape[0]] = small[...]
    product = grad_in * w[0].astype(F32) + g_gate[...] * w[1].astype(F32)
    high = low(product)
    ones = jnp.ones((8, LANES), BF16)
    gain_part[...] = (nt(ones, high) + nt(ones, low(product - high.astype(F32)))) / gain[...]
    half = GRAD_ROWS // 2
    if keep.shape[0] == GRAD_ROWS:
        keep[...] = pack[...]
    else:
        mine = lax.rem(lax.axis_index("rows"), 2)
        keep[...] = pack[pl.ds(pl.multiple_of(mine * half, 16), half)]
        send[...] = low(pack[pl.ds(pl.multiple_of((1 - mine) * half, 16), half)])
    total = res_kept[...] + res_got[...].astype(F32)
    odd = lax.rem(lax.axis_index("ch"), 2) == 1
    res_own[...] = jnp.where(odd, total[:, LANES:], total[:, :LANES])
    res_sent[...] = low(jnp.where(odd, total[:, :LANES], total[:, LANES:]))


def normed_back_kernel(geo, lengths, xg, near, far, dn_gate, w, hidden, res_own, res_got, kept, sent, result):
    tok, steps = geo.tok, geo.steps
    valid = geo.valid(lengths)
    even = lax.rem(lax.axis_index("rows"), 2) == 0
    mover = unpermuter(tok)
    turn = mirror(w.shape[1])
    second = lax.axis_index("ch") >= 2
    row = iota((tok, LANES), 0)
    token = (row % CHUNKS) * steps + row // CHUNKS
    grads = []
    for strand in range(2):
        one, two = near[strand], far[strand]
        ahead = jnp.where(even, two, one)
        behind = jnp.where(even, one, two)
        total = xg[strand]
        for k in range(3):
            total = total + jnp.where(token == k, ahead[k : k + 1], 0.0)
            total = total + jnp.where(token == tok - 1 - k, behind[15 - k : 16 - k], 0.0)
        rounded = low(total * valid)
        in_w = w[0]
        if strand == 1:
            in_w = low(nn(turn, in_w))
        grads.append(nt(low(nn(mover, rounded)), in_w) + dn_gate[strand])
    kept[...] = jnp.where(second, grads[1], grads[0])
    sent[...] = low(jnp.where(second, grads[0], grads[1]))
    out = hidden[...].astype(F32) + res_own[...] + res_got[...].astype(F32)
    result[...] = low(out)


def finish_kernel(geo, one, two, xo, xc, gain, cot, input_grad):
    width = one.shape[1]
    mine = lax.axis_index("ch")
    odd = lax.rem(mine, 2) == 1
    a, b = xo[...].astype(F32), xc[...].astype(F32)
    source = jnp.concatenate([jnp.where(odd, b, a), jnp.where(odd, a, b)], axis=1)
    inverse = lax.rsqrt(jnp.mean(source * source, axis=-1, keepdims=True) + EPSILON)
    unit = source * inverse
    plain = jnp.broadcast_to(gain[...], (8, width))
    high = low(plain)
    rest = plain - high.astype(F32)
    middle = low(rest)
    turn = mirror(width)
    turned = nn(high, turn) + nn(middle, turn) + nn(low(rest - middle.astype(F32)), turn)
    here = jnp.where(mine >= 2, turned, plain)[:1]
    scaled = (one[...].astype(F32) + two[...].astype(F32)) * here
    back = inverse * (scaled - unit * jnp.mean(scaled * unit, axis=-1, keepdims=True))
    input_grad[...] = cot[...].astype(F32) + jnp.where(odd, back[:, LANES:], back[:, :LANES])


def unpack_kernel(halves, gain_sum, in_g, out_g, sel_g, cw_g, cb_g, stw_g, stb_g, decay_g, skip_g, gain_g, pack):
    if len(halves) == 1:
        pack[...] = halves[0][...].astype(F32)
    else:
        half = GRAD_ROWS // 2
        mine = lax.rem(lax.axis_index("rows"), 2)
        pack[pl.ds(pl.multiple_of(mine * half, 16), half)] = halves[0][...].astype(F32)
        pack[pl.ds(pl.multiple_of((1 - mine) * half, 16), half)] = halves[1][...].astype(F32)
    width = in_g.shape[1]
    in_g[0] = pack[:width]
    in_g[1] = pack[width : 2 * width]
    out_g[:, :LANES] = pack[2 * width : 2 * width + LANES]
    out_g[:, LANES:] = pack[2 * width + LANES : 3 * width]
    at = 3 * width + LANES
    select = pack[3 * width : at]
    columns = sel_g.shape[2]
    sel_g[0] = select[:, :columns]
    sel_g[1] = pltpu.roll(select, 64, 1)[:, :columns]
    taps = cw_g.shape[1]
    for course in range(2):
        cw_g[course] = pack[at + course * taps : at + (course + 1) * taps]
    cb_g[...] = pack[at + 2 * taps : at + 2 * taps + 2]
    at = at + 16
    for course in range(2):
        stw_g[course] = pack[at + course * R : at + (course + 1) * R]
        decay_g[course] = pack[at + 2 * R + course * N : at + 2 * R + (course + 1) * N]
    at = at + 2 * R + 2 * N
    stb_g[...] = pack[at : at + 2]
    skip_g[...] = pack[at + 2 : at + 4]
    gain_g[...] = gain_sum[:1]


def swap(value, axis, distance):
    count = lax.axis_size(axis)
    return lax.ppermute(value, axis, [(i, i ^ distance) for i in range(count)])


def gather_channels(value):
    across = swap(value, "ch", 2)
    return value, swap(value, "ch", 1), across, swap(across, "ch", 1)


def partner_sum(value):
    joined = low(value.astype(F32) + swap(value, "ch", 2).astype(F32))
    return joined, swap(joined, "ch", 1)


def on_device(
    hidden_in, lengths, norm_gain, in_weight, conv_weight, conv_bias, select_weight,
    step_weight, step_bias, decay_log, skip_gain, out_weight, cotangent,
):
    tok = hidden_in.shape[0]
    rows = lax.axis_size("rows")
    geo = Geometry(tok, rows)
    steps = geo.steps
    width = in_weight.shape[1]
    gain = norm_gain[None, :]
    small_mesh = geo.members == 4 and rows == 8
    padded_rows = (steps + 2 * (conv_weight.shape[1] - 1)) * CHUNKS

    def kernel(f):
        return functools.partial(f, geo)

    def lifted(f, first, amount):
        def body(*refs):
            return f(*refs[:first], refs[first : first + amount], *refs[first + amount :])

        return body

    x_parts = gather_channels(hidden_in)
    c_parts = gather_channels(cotangent)

    normed, inputs, gates, near, far = run(
        kernel(project_kernel),
        [
            ((2, tok, width), BF16),
            ((2, tok, LANES), BF16),
            ((2, tok, LANES), F32),
            ((16, 2 * width), BF16),
            ((16, 2 * width), BF16),
        ],
        lengths, *x_parts, gain, in_weight,
        smem=1, scratch=[pltpu.VMEM((4, tok, LANES), BF16)], name="project",
    )
    near = lax.ppermute(near, "rows", geo.near())
    far = lax.ppermute(far, "rows", geo.far())
    moved, gm, dys = run(
        kernel(cotangent_kernel),
        [((2, tok, width), BF16), ((2, tok, LANES), F32), ((2, tok, LANES), F32)],
        lengths, *c_parts, gates, out_weight,
        smem=1, scratch=[pltpu.VMEM((4, tok, LANES), BF16)], name="cotangents",
    )
    padded, rims_normed, pre, act, message, select = run(
        kernel(conv_kernel),
        [
            ((2, padded_rows, LANES), F32),
            ((2, 32, width), BF16),
            ((4, tok, LANES), F32),
            ((4, tok, LANES), BF16),
            ((2, tok, LANES), BF16),
            ((2, LANES, LANES), F32),
        ],
        lengths, inputs, near, far, gain, in_weight, conv_weight, conv_bias, select_weight,
        smem=1, name="conv",
    )
    one, two = partner_sum(message)
    chunked = ((4, N * CHUNKS, LANES), F32)
    summary = ((4 * N + 8, LANES), F32)
    members = ((4, tok, LANES), F32)
    outs = [members, members, members, members, chunked, chunked, chunked]
    table = pltpu.VMEM((2, N, CHUNKS, LANES), F32)
    if small_mesh:

        def summarise(*refs):
            ins, out, rest = refs[:8], refs[8:15], refs[15:]
            near_ref, far_ref, a2, up, down = rest
            summary_kernel(geo, *ins, *out, near_ref, far_ref, a2, up, down)

        scratch = [table, pltpu.VMEM(summary[0], F32), pltpu.VMEM(summary[0], F32)]
    else:

        def summarise(*refs):
            ins, out, rest = refs[:8], refs[8:15], refs[15:]
            up, down, a2 = rest
            summary_kernel(geo, *ins, *out, None, None, a2, up, down)

        scratch = [table]
    got = run(
        summarise, outs + [summary, summary],
        lengths, one, two, act, dys, step_weight, step_bias, decay_log,
        smem=1, scratch=scratch, name="summary",
    )
    proj, raw, step, drive, chunk_p, chunk_h, chunk_w = got[:7]
    if small_mesh:
        slots = (
            lax.ppermute(got[7], "rows", geo.near()),
            lax.ppermute(got[8], "rows", geo.across()),
            lax.ppermute(got[8], "rows", geo.far()),
        )
        slot_scratch = pltpu.VMEM((4,) + summary[0], F32)
    else:
        up, down = lax.all_gather(got[7], "rows"), lax.all_gather(got[8], "rows")
        place = lax.axis_index("rows")
        base = place - geo.local()
        index = base + jnp.arange(geo.members)
        inside = jnp.clip(index, 0, rows - 1)
        slots = (jnp.where((index < place)[:, None, None], up[inside], down[inside]),)
        slot_scratch = pltpu.VMEM((8, LANES), F32)
    mixed, dgate, dact, message, small = run(
        lifted(kernel(scan_kernel), 1, len(slots)),
        [
            ((2, tok, LANES), BF16),
            ((2, tok, LANES), BF16),
            members,
            ((2, tok, LANES), BF16),
            ((80, LANES), F32),
        ],
        lengths, *slots, act, proj, raw, step, drive, chunk_p, chunk_h, chunk_w,
        dys, gm, gates, step_weight, decay_log, skip_gain,
        smem=1,
        scratch=[
            slot_scratch,
            table,
            table,
            pltpu.VMEM(chunked[0], F32),
            pltpu.VMEM(chunked[0], F32),
            pltpu.VMEM(((steps + 1) * N * CHUNKS, LANES), F32),
            pltpu.VMEM((tok, 2 * N * LANES), BF16),
            pltpu.VMEM((2 * N * LANES, LANES), BF16),
            pltpu.VMEM(members[0], F32),
            pltpu.VMEM(members[0], F32),
            pltpu.VMEM(members[0], F32),
            pltpu.VMEM(members[0], F32),
            pltpu.VMEM((2, N * CHUNKS, LANES), F32),
        ],
        name="scan",
    )
    one, two = partner_sum(message)
    res_kept, res_sent, g_out, g_gate, dn_gate = run(
        kernel(dense_kernel),
        [
            ((tok, width), F32),
            ((tok, width), BF16),
            ((LANES, width), F32),
            ((width, LANES), F32),
            ((2, tok, width), F32),
        ],
        mixed, out_weight, moved, dgate, normed, in_weight, name="dense",
    )
    res_got = swap(res_sent, "ch", 2)
    half = GRAD_ROWS // 2
    xg, near, far, keep, send, gain_part, res_own, res_sent = run(
        kernel(conv_back_kernel),
        [
            ((2, tok, LANES), F32),
            ((2, 16, LANES), F32),
            ((2, 16, LANES), F32),
            ((half if small_mesh else GRAD_ROWS, LANES), F32),
            ((half, LANES), BF16),
            ((8, width), F32),
            ((tok, LANES), F32),
            ((tok, LANES), BF16),
        ],
        lengths, one, two, act, dact, pre, padded, conv_weight, select, normed, rims_normed, gain, in_weight,
        g_gate, g_out, small, res_kept, res_got,
        smem=1, scratch=[pltpu.VMEM((padded_rows, LANES), F32), pltpu.VMEM((GRAD_ROWS, LANES), F32)],
        name="conv_back",
    )
    if small_mesh:
        grads = low(keep + swap(send, "rows", 1).astype(F32))
        others = [swap(grads, "rows", d) for d in (2, 4, 6)]
    near = lax.ppermute(near, "rows", geo.near())
    far = lax.ppermute(far, "rows", geo.far())
    res_got = swap(res_sent, "ch", 1)
    dn_kept, dn_sent, result = run(
        kernel(normed_back_kernel),
        [((tok, width), F32), ((tok, width), BF16), ((tok, LANES), BF16)],
        lengths, xg, near, far, dn_gate, in_weight, hidden_in, res_own, res_got,
        smem=1, name="normed_back",
    )
    dn = low(dn_kept + swap(dn_sent, "ch", 2).astype(F32))
    input_grad = run(
        kernel(finish_kernel), ((tok, LANES), F32),
        dn, swap(dn, "ch", 1), x_parts[0], x_parts[1], gain, cotangent, name="finish",
    )
    if small_mesh:
        gain_part = gain_part + swap(gain_part, "ch", 2)
        gain_part = gain_part + swap(gain_part, "ch", 1)
        gain_part = gain_part + swap(gain_part, "rows", 1)
        gain_part = gain_part + sum(swap(gain_part, "rows", d) for d in (2, 4, 6))
        grads = low(sum((g.astype(F32) for g in others), grads.astype(F32)))
        halves = (grads, swap(grads, "rows", 1))
    else:
        gain_part = lax.psum(gain_part, ("rows", "ch"))
        halves = (lax.psum(keep, "rows"),)
    got = run(
        lifted(unpack_kernel, 0, len(halves)),
        [
            (in_weight.shape, F32),
            (out_weight.shape, F32),
            (select_weight.shape, F32),
            (conv_weight.shape, F32),
            (conv_bias.shape, F32),
            (step_weight.shape, F32),
            (step_bias.shape, F32),
            (decay_log.shape, F32),
            (skip_gain.shape, F32),
            ((1, width), F32),
        ],
        *halves, gain_part, scratch=[pltpu.VMEM((GRAD_ROWS, LANES), F32)], name="unpack",
    )
    in_g, out_g, sel_g, cw_g, cb_g, stw_g, stb_g, decay_g, skip_g, gain_g = got
    return (
        result, input_grad, gain_g[0], in_g, cw_g, cb_g, sel_g, stw_g, stb_g, decay_g, skip_g, out_g,
    )


def solution(mesh):
    lanes = P(None, None, "ch")
    pair = P(None, "ch")
    columns = P(None, "ch", None)
    tokens = P("rows", "ch")
    return jax.shard_map(
        on_device,
        mesh=mesh,
        in_specs=(
            tokens, P(), P(), lanes, lanes, pair, columns, lanes, pair, lanes, pair, P("ch", None), tokens,
        ),
        out_specs=(
            tokens, tokens, P(), lanes, lanes, pair, columns, lanes, pair, lanes, pair, P("ch", None),
        ),
        check_vma=False,
    )
```

time: 2750 us -> 126 us (0.05); the launches traced: 2700 us -> 126 us
  local copies, waits for them, and re-layouts: 1170 us -> 3.95 us
  other arithmetic: 769 us -> 0.22 us
  blocking collectives: 455 us -> 0 us
  waiting for transfers between devices: 232 us -> 34.6 us
  Pallas kernels: 0 us -> 55.7 us
    pad x928 -> x0, local copies, waits for them, and re-layouts: 600 us -> none  [block_advance(): lax.associative_scan(join_single, (decays, drives), axis=0)]
    all_gather x16 -> x0, blocking collectives: 441 us -> none  [the longest x10 306 us: carried_in(): gathered = jax.tree.map(lambda a: lax.all_gather(a, axis), part)]
    mul x427 -> x0, other arithmetic: 294 us -> none  [the longest x368 251 us: join_single(): return (earlier[0] * later[0], earlier[1] * later[0] + later[1])]
    psum x4 -> x0, waiting for transfers between devices: 211 us -> none  [the longest x2 149 us: on_device(): lax.psum((grad_gain, grad_in, jnp.stack(grad_conv_w), jnp.stack(grad_conv...]
    dynamic_update_slice x144 -> x0, other arithmetic: 206 us -> none  [block_scan(): final_state, outputs = lax.scan(block_advance, start_state, pieces)]
    dynamic_update_slice x224 -> x0, local copies, waits for them, and re-layouts: 172 us -> none  [block_scan(): final_state, outputs = lax.scan(block_advance, start_state, pieces)]
    another operation x201 -> x0, local copies, waits for them, and re-layouts: 150 us -> none
    reduce_sum x123 -> x0, other arithmetic: 111 us -> none  [the longest x32 38.3 us: block_advance(): outputs = jnp.sum(read_block[:, :, None] * states, axis=1)]
where the time goes in v1:
time: 126 us
  Pallas kernels  55.7 us (44%)
  waiting for transfers between devices  34.6 us (27%)
  starting transfers between devices  30.6 us (24%)
  local copies, waits for them, and re-layouts  3.95 us (3%)
    pallas_call x10, Pallas kernels, run(): pl.pallas_call(kernel, out_shape=[jax.ShapeDtypeStruct(s, d) for s, d in...  55.7 us
    ppermute x25, waiting for transfers between devices, swap(): return lax.ppermute(value, axis, [(i, i ^ distance) for i in range(count)])  27.6 us
    ppermute x25, starting transfers between devices, swap(): return lax.ppermute(value, axis, [(i, i ^ distance) for i in range(count)])  23.8 us
    unnamed x32, local copies, waits for them, and re-layouts  3.95 us
    ppermute x2, starting transfers between devices, on_device(): near = lax.ppermute(near, 'rows', geo.near())  3.85 us
  transfers between devices with their start and end apart: 32, of which 20 were waited for; matrix products, arithmetic and copies ran while one was open for 0% of the time, Pallas kernels for 4%

profile of v1, /device:TPU:0, one launch (start us, length us, event | category | flops | bytes accessed | tf_op | source)
XLA Modules:
  0.0 125.9 jit_solution(3851297797181967539)
XLA Ops:
  0.7 3.1 %collective-permute-start.1 = (bf16[256,128]{1,0:T(8,128)(2,1)}, bf16[256,128]{1,0:T(8,128)(2,1)S(1)}, u32[]{:S(2)}, u32[]{:S(2)}) collective-permute-start(bf16[256,128]{1,0:T(8,128)(2,1)} %xo.3), channel_id=1, source_target_pairs={{0,2},{1,3},{2,0},{3,1},{4,6},{5,7},{6,4},{7,5},{8,10},{9,11},{10,... | collective-permute-start | bytes 196616 | tf_op jit(solution)/shard_map/ppermute | solution.py:717
  3.7 2.5 %collective-permute-done.1.xy = bf16[256,128]{1,0:T(8,128)(2,1)S(1)} collective-permute-done((bf16[256,128]{1,0:T(8,128)(2,1)}, bf16[256,128]{1,0:T(8,128)(2,1)S(1)}, u32[]{:S(2)}, u32[]{:S(2)}) %collective-permute-start.1) | collective-permute-done | bytes 65568 | tf_op jit(solution)/shard_map/ppermute | solution.py:717
  6.2 1.2 collective-permute-done.2.xd
  7.4 0.9 copy-done
  8.4 0.8 copy-done.2
  9.2 1.3 %project.1 = (bf16[2,256,256]{2,1,0:T(8,128)(2,1)S(1)}, bf16[2,256,128]{2,1,0:T(8,128)(2,1)S(1)}, f32[2,256,128]{2,1,0:T(8,128)S(1)}, bf16[16,512]{1,0:T(8,128)(2,1)S(1)}, bf16[16,512]{1,0:T(8,128)(2,1)S(1)}) custom-call(s32[3]{0:T(128)S(1)} %copy-done.8, bf16[256,128]{1,0:T(8,128)(2,1)S(1)} %copy-done.2, bf16[256,128]{1,0:T(8,128)(2,1)S(1)} %collective-permute-done.xc, ...), custom_call_target="tpu_custom_call" | custom-call | tf_op jit(solution)/shard_map/project/pallas_call | solution.py:132
  10.5 2.1 %collective-permute-start.3 = (bf16[16,512]{1,0:T(8,128)(2,1)S(1)}, bf16[16,512]{1,0:T(8,128)(2,1)S(1)}, u32[]{:S(2)}, u32[]{:S(2)}) collective-permute-start(bf16[16,512]{1,0:T(8,128)(2,1)S(1)} %get-tuple-element.67), channel_id=1, source_target_pairs={{0,4},{4,0},{8,12},{12,8},{16,20},{20,16},{24,28},{28,24},{1,5},{5... | collective-permute-start | bytes 49160 | tf_op jit(solution)/shard_map/ppermute | solution.py:767
  12.5 0.1 collective-permute-start.4
  12.6 0.1 copy.25.sw
  12.8 0.0 copy-start.11
  12.8 1.5 %collective-permute-done.3.near = bf16[16,512]{1,0:T(8,128)(2,1)S(1)} collective-permute-done((bf16[16,512]{1,0:T(8,128)(2,1)S(1)}, bf16[16,512]{1,0:T(8,128)(2,1)S(1)}, u32[]{:S(2)}, u32[]{:S(2)}) %collective-permute-start.3) | collective-permute-done | bytes 16416 | tf_op jit(solution)/shard_map/ppermute | solution.py:767
  14.3 2.0 %collective-permute-done.4.far = bf16[16,512]{1,0:T(8,128)(2,1)S(1)} collective-permute-done((bf16[16,512]{1,0:T(8,128)(2,1)S(1)}, bf16[16,512]{1,0:T(8,128)(2,1)S(1)}, u32[]{:S(2)}, u32[]{:S(2)}) %collective-permute-start.4) | collective-permute-done | bytes 16416 | tf_op jit(solution)/shard_map/ppermute | solution.py:768
  16.3 0.0 copy-start.4
  16.3 1.4 %conv.1 = (f32[2,304,128]{2,1,0:T(8,128)S(1)}, bf16[2,32,256]{2,1,0:T(8,128)(2,1)S(1)}, f32[4,256,128]{2,1,0:T(8,128)S(1)}, bf16[4,256,128]{2,1,0:T(8,128)(2,1)S...) custom-call(s32[3]{0:T(128)S(1)} %copy-done.8, bf16[2,256,128]{2,1,0:T(8,128)(2,1)S(1)} %get-tuple-element.66.inputs, ...), custom_call_target="tpu_custom_call" | custom-call | tf_op jit(solution)/shard_map/conv/pallas_call | solution.py:132
  17.7 1.6 %collective-permute-start.5 = (bf16[2,256,128]{2,1,0:T(8,128)(2,1)S(1)}, bf16[2,256,128]{2,1,0:T(8,128)(2,1)S(1)}, u32[]{:S(2)}, u32[]{:S(2)}) collective-permute-start(bf16[2,256,128]{2,1,0:T(8,128)(2,1)S(1)} %get-tuple-element.69), channel_id=1, source_target_pairs={{0,2},{1,3},{2,0},{3,1},{4,6},{5,7},{6,4},{7,5},{8,10},{9,11},{10,... | collective-permute-start | bytes 393224 | tf_op jit(solution)/shard_map/ppermute | solution.py:717
  19.3 0.5 collective-permute-start.8
  19.8 2.9 %collective-permute-done.5 = bf16[2,256,128]{2,1,0:T(8,128)(2,1)S(1)} collective-permute-done((bf16[2,256,128]{2,1,0:T(8,128)(2,1)S(1)}, bf16[2,256,128]{2,1,0:T(8,128)(2,1)S(1)}, u32[]{:S(2)}, u32[]{:S(2)}) %collective-permute-start.5) | collective-permute-done | bytes 131104 | tf_op jit(solution)/shard_map/ppermute | solution.py:717
  22.8 0.1 collective-permute-start.6
  22.9 0.5 collective-permute-start.7
  23.4 0.2 collective-permute-done.8.cy
  23.6 0.7 collective-permute-done.7.cc
  24.3 0.5 collective-permute-done.9.cd
  24.8 1.1 cotangents.1
  26.0 0.7 copy-done.12
  26.7 17.3 %summary.1 = (f32[4,256,128]{2,1,0:T(8,128)S(1)}, f32[4,256,128]{2,1,0:T(8,128)S(1)}, f32[4,256,128]{2,1,0:T(8,128)S(1)}, f32[4,256,128]{2,1,0:T(8,128)S(1)}, f3...) custom-call(s32[3]{0:T(128)S(1)} %copy-done.8, ...), custom_call_target="tpu_custom_call" | custom-call | tf_op jit(solution)/shard_map/summary/pallas_call | solution.py:132
  43.9 0.6 collective-permute-start.10
  44.5 1.5 %collective-permute-start.12 = (f32[72,128]{1,0:T(8,128)S(1)}, f32[72,128]{1,0:T(8,128)S(1)}, u32[]{:S(2)}, u32[]{:S(2)}) collective-permute-start(f32[72,128]{1,0:T(8,128)S(1)} %get-tuple-element.74), channel_id=1, source_target_pairs={{0,4},{4,0},{8,20},{12,16},{16,12},{20,8},{24,28},{28,24},{1,5},{5... | collective-permute-start | bytes 110600 | tf_op jit(solution)/shard_map/ppermute | solution.py:820
  46.0 0.5 collective-permute-start.11
  46.6 1.4 %collective-permute-done.10.refs_1_ = f32[72,128]{1,0:T(8,128)S(1)} collective-permute-done((f32[72,128]{1,0:T(8,128)S(1)}, f32[72,128]{1,0:T(8,128)S(1)}, u32[]{:S(2)}, u32[]{:S(2)}) %collective-permute-start.10) | collective-permute-done | bytes 36896 | tf_op jit(solution)/shard_map/ppermute | solution.py:818
  48.0 0.8 collective-permute-done.12.refs_3_
  48.8 1.2 collective-permute-done.11.refs_2_
  50.0 0.7 copy-done.13
  50.7 28.5 %scan.1 = (bf16[2,256,128]{2,1,0:T(8,128)(2,1)S(1)}, bf16[2,256,128]{2,1,0:T(8,128)(2,1)S(1)}, f32[4,256,128]{2,1,0:T(8,128)S(1)}, bf16[2,256,128]{2,1,0:T(8,128)(2,1)S(1)}, f32[80,128]{1,0:T(8,128)S(1)}) custom-call(s32[3]{0:T(128)S(1)} %copy-done.8, f32[72,128]{1,0:T(8,128)S(1)} %collective-permute-done.10.refs_1_, ...), custom_call_target="tpu_custom_call" | custom-call | tf_op jit(solution)/shard_map/scan/pallas_call | solution.py:132
  79.1 1.5 %collective-permute-start.13 = (bf16[2,256,128]{2,1,0:T(8,128)(2,1)S(1)}, bf16[2,256,128]{2,1,0:T(8,128)(2,1)S(1)}, u32[]{:S(2)}, u32[]{:S(2)}) collective-permute-start(bf16[2,256,128]{2,1,0:T(8,128)(2,1)S(1)} %get-tuple-element.83), channel_id=1, source_target_pairs={{0,2},{1,3},{2,0},{3,1},{4,6},{5,7},{6,4},{7,5},{8,10},{9,11},{10,... | collective-permute-start | bytes 393224 | tf_op jit(solution)/shard_map/ppermute | solution.py:717
  80.6 0.8 dense.1
  81.4 0.7 collective-permute-start.15
  82.1 3.4 %collective-permute-done.13 = bf16[2,256,128]{2,1,0:T(8,128)(2,1)S(1)} collective-permute-done((bf16[2,256,128]{2,1,0:T(8,128)(2,1)S(1)}, bf16[2,256,128]{2,1,0:T(8,128)(2,1)S(1)}, u32[]{:S(2)}, u32[]{:S(2)}) %collective-permute-start.13) | collective-permute-done | bytes 131104 | tf_op jit(solution)/shard_map/ppermute | solution.py:717
  85.5 0.1 collective-permute-start.14
  85.6 1.3 %collective-permute-done.15.res_got = bf16[256,256]{1,0:T(8,128)(2,1)S(1)} collective-permute-done((bf16[256,256]{1,0:T(8,128)(2,1)S(1)}, bf16[256,256]{1,0:T(8,128)(2,1)S(1)}, u32[]{:S(2)}, u32[]{:S(2)}) %collective-permute-start.15) | collective-permute-done | bytes 131104 | tf_op jit(solution)/shard_map/ppermute | solution.py:717
  86.9 0.1 collective-permute-done.14.two
  86.9 1.8 %conv_back.1 = (f32[2,256,128]{2,1,0:T(8,128)S(1)}, f32[2,16,128]{2,1,0:T(8,128)S(1)}, f32[2,16,128]{2,1,0:T(8,128)S(1)}, f32[496,128]{1,0:T(8,128)S(1)}, bf16[4...) custom-call(s32[3]{0:T(128)S(1)} %copy-done.8, ...), custom_call_target="tpu_custom_call" | custom-call | tf_op jit(solution)/shard_map/conv_back/pallas_call | solution.py:132
  88.7 0.3 collective-permute-start.21
  89.0 0.8 collective-permute-start.26
  89.8 2.8 %collective-permute-done.26 = f32[8,256]{1,0:T(8,128)S(1)} collective-permute-done((f32[8,256]{1,0:T(8,128)S(1)}, f32[8,256]{1,0:T(8,128)S(1)}, u32[]{:S(2)}, u32[]{:S(2)}) %collective-permute-start.26) | collective-permute-done | bytes 8224 | tf_op jit(solution)/shard_map/ppermute | solution.py:717
  92.6 1.8 %collective-permute-start.16 = (f32[2,16,128]{2,1,0:T(8,128)S(1)}, f32[2,16,128]{2,1,0:T(8,128)S(1)}, u32[]{:S(2)}, u32[]{:S(2)}) collective-permute-start(f32[2,16,128]{2,1,0:T(8,128)S(1)} %get-tuple-element.99), channel_id=1, source_target_pairs={{0,4},{4,0},{8,12},{12,8},{16,20},{20,16},{24,28},{28,24},{1,5},{5... | collective-permute-start | bytes 49160 | tf_op jit(solution)/shard_map/ppermute | solution.py:894
  94.4 0.2 collective-permute-start.17
  94.7 1.8 %collective-permute-start.28 = (f32[8,256]{1,0:T(8,128)S(1)}, f32[8,256]{1,0:T(8,128)S(1)}, u32[]{:S(2)}, u32[]{:S(2)}) collective-permute-start(f32[8,256]{1,0:T(8,128)S(1)} %add.47), channel_id=1, source_target_pairs={{0,4},{4,0},{8,12},{12,8},{16,20},{20,16},{24,28},{28,24},{1,5},{5... | collective-permute-start | bytes 24584 | tf_op jit(solution)/shard_map/ppermute | solution.py:717
  96.5 1.9 %collective-permute-done.28 = f32[8,256]{1,0:T(8,128)S(1)} collective-permute-done((f32[8,256]{1,0:T(8,128)S(1)}, f32[8,256]{1,0:T(8,128)S(1)}, u32[]{:S(2)}, u32[]{:S(2)}) %collective-permute-start.28) | collective-permute-done | bytes 8224 | tf_op jit(solution)/shard_map/ppermute | solution.py:717
  98.3 3.6 %collective-permute-start.31 = (f32[8,256]{1,0:T(8,128)S(1)}, f32[8,256]{1,0:T(8,128)S(1)}, u32[]{:S(2)}, u32[]{:S(2)}) collective-permute-start(f32[8,256]{1,0:T(8,128)S(1)} %add.48), channel_id=1, source_target_pairs={{0,24},{4,28},{8,16},{12,20},{16,8},{20,12},{24,0},{28,4},{1,25},{... | collective-permute-start | bytes 24584 | tf_op jit(solution)/shard_map/ppermute | solution.py:717
  101.9 2.0 %collective-permute-start.30 = (f32[8,256]{1,0:T(8,128)S(1)}, f32[8,256]{1,0:T(8,128)S(1)}, u32[]{:S(2)}, u32[]{:S(2)}) collective-permute-start(f32[8,256]{1,0:T(8,128)S(1)} %add.48), channel_id=1, source_target_pairs={{0,16},{4,20},{8,24},{12,28},{16,0},{20,4},{24,8},{28,12},{1,17},{... | collective-permute-start | bytes 24584 | tf_op jit(solution)/shard_map/ppermute | solution.py:717
  103.9 1.8 %normed_back.1 = (f32[256,256]{1,0:T(8,128)S(1)}, bf16[256,256]{1,0:T(8,128)(2,1)S(1)}, bf16[256,128]{1,0:T(8,128)(2,1)}) custom-call(s32[3]{0:T(128)S(1)} %copy-done.8, f32[2,256,128]{2,1,0:T(8,128)S(1)} %get-tuple-element.98.xg, f32[2,16,128]{2,1,0:T(8,128)S(1)} %collective-permute-done.16.near, f32[2,16,128]{2,1,0:T(8,128)S(1)} %collective-permute-done.17.far, ...), custom_call_target="tpu_custom_call" | custom-call | tf_op jit(solution)/shard_map/normed_back/pallas_call | solution.py:132
  105.7 0.8 collective-permute-start.19
  106.6 1.8 %collective-permute-start.24 = (bf16[496,128]{1,0:T(8,128)(2,1)S(1)}, bf16[496,128]{1,0:T(8,128)(2,1)S(1)}, u32[]{:S(2)}, u32[]{:S(2)}) collective-permute-start(bf16[496,128]{1,0:T(8,128)(2,1)S(1)} %add_convert_fusion.4), channel_id=1, source_target_pairs={{0,24},{4,28},{8,16},{12,20},{16,8},{20,12},{24,0},{28,4},{1,25},{... | collective-permute-start | bytes 380936 | tf_op jit(solution)/shard_map/ppermute | solution.py:717
  108.4 2.3 %collective-permute-done.19 = bf16[256,256]{1,0:T(8,128)(2,1)S(1)} collective-permute-done((bf16[256,256]{1,0:T(8,128)(2,1)S(1)}, bf16[256,256]{1,0:T(8,128)(2,1)S(1)}, u32[]{:S(2)}, u32[]{:S(2)}) %collective-permute-start.19) | collective-permute-done | bytes 131104 | tf_op jit(solution)/shard_map/ppermute | solution.py:717
  110.7 0.4 collective-permute-start.22
  111.1 3.4 %collective-permute-done.24 = bf16[496,128]{1,0:T(8,128)(2,1)S(1)} collective-permute-done((bf16[496,128]{1,0:T(8,128)(2,1)S(1)}, bf16[496,128]{1,0:T(8,128)(2,1)S(1)}, u32[]{:S(2)}, u32[]{:S(2)}) %collective-permute-start.24) | collective-permute-done | bytes 127008 | tf_op jit(solution)/shard_map/ppermute | solution.py:717
  114.5 3.1 %collective-permute-start.29 = (f32[8,256]{1,0:T(8,128)S(1)}, f32[8,256]{1,0:T(8,128)S(1)}, u32[]{:S(2)}, u32[]{:S(2)}) collective-permute-start(f32[8,256]{1,0:T(8,128)S(1)} %add.48), channel_id=1, source_target_pairs={{0,8},{4,12},{8,0},{12,4},{16,24},{20,28},{24,16},{28,20},{1,9},{5... | collective-permute-start | bytes 24584 | tf_op jit(solution)/shard_map/ppermute | solution.py:717
  117.6 0.8 collective-permute-done.23
  118.4 0.1 add_convert_fusion.3.refs_0_
  118.5 1.2 collective-permute-start.25
  119.8 1.0 finish.1
  120.8 3.6 %collective-permute-done.25.refs_1_ = bf16[496,128]{1,0:T(8,128)(2,1)S(1)} collective-permute-done((bf16[496,128]{1,0:T(8,128)(2,1)S(1)}, bf16[496,128]{1,0:T(8,128)(2,1)S(1)}, u32[]{:S(2)}, u32[]{:S(2)}) %collective-permute-start.25) | collective-permute-done | bytes 127008 | tf_op jit(solution)/shard_map/ppermute | solution.py:717
  124.4 0.9 unpack.1
  125.2 0.7 copy.26
  (51 shorter events, 0.2 us)
Async XLA Ops:
  0.6 6.8 %copy-start.8 = (s32[3]{0:T(128)S(1)}, s32[3]{0:T(128)}, u32[]{:S(2)}) copy-start(s32[3]{0:T(128)} %lengths.9) | copy-start | bytes 40
  0.7 6.8 %copy-start.9 = (f32[256]{0:T(256)S(1)}, f32[256]{0:T(256)}, u32[]{:S(2)}) copy-start(f32[256]{0:T(256)} %param.15) | copy-start | bytes 3076
  0.7 5.5 %collective-permute-start.1 = (bf16[256,128]{1,0:T(8,128)(2,1)}, bf16[256,128]{1,0:T(8,128)(2,1)S(1)}, u32[]{:S(2)}, u32[]{:S(2)}) collective-permute-start(bf16[256,128]{1,0:T(8,128)(2,1)} %xo.3), channel_id=1, source_target_pairs={{0,2},{1,3},{2,0},{3,1},{4,6},{5,7},{6,4},{7,5},{8,10},{9,11},{10,... | collective-permute-start | bytes 196616 | tf_op jit(solution)/shard_map/ppermute | solution.py:717
  3.7 2.5 %collective-permute-start = (bf16[256,128]{1,0:T(8,128)(2,1)}, bf16[256,128]{1,0:T(8,128)(2,1)S(1)}, u32[]{:S(2)}, u32[]{:S(2)}) collective-permute-start(bf16[256,128]{1,0:T(8,128)(2,1)} %xo.3), channel_id=1, source_target_pairs={{0,1},{1,0},{2,3},{3,2},{4,5},{5,4},{6,7},{7,6},{8,9},{9,8},{10,11... | collective-permute-start | bytes 196616 | tf_op jit(solution)/shard_map/ppermute | solution.py:717
  6.2 1.3 collective-permute-start.2
  7.4 0.9 copy-start
  8.4 0.8 copy-start.2
  9.2 3.4 %copy-start.14 = (bf16[2,128,48]{1,2,0:T(8,128)(2,1)S(1)}, bf16[2,128,48]{1,2,0:T(8,128)(2,1)}, u32[]{:S(2)}) copy-start(bf16[2,128,48]{1,2,0:T(8,128)(2,1)} %param.19) | copy-start | bytes 73732
  9.2 7.1 %copy-start.1 = (bf16[2,256,128]{2,1,0:T(8,128)(2,1)S(1)}, bf16[2,256,128]{2,1,0:T(8,128)(2,1)}, u32[]{:S(2)}) copy-start(bf16[2,256,128]{2,1,0:T(8,128)(2,1)} %w.9) | copy-start | bytes 393220
  10.5 3.8 %collective-permute-start.3 = (bf16[16,512]{1,0:T(8,128)(2,1)S(1)}, bf16[16,512]{1,0:T(8,128)(2,1)S(1)}, u32[]{:S(2)}, u32[]{:S(2)}) collective-permute-start(bf16[16,512]{1,0:T(8,128)(2,1)S(1)} %get-tuple-element.67), channel_id=1, source_target_pairs={{0,4},{4,0},{8,12},{12,8},{16,20},{20,16},{24,28},{28,24},{1,5},{5... | collective-permute-start | bytes 49160 | tf_op jit(solution)/shard_map/ppermute | solution.py:767
  12.5 3.7 %collective-permute-start.4 = (bf16[16,512]{1,0:T(8,128)(2,1)S(1)}, bf16[16,512]{1,0:T(8,128)(2,1)S(1)}, u32[]{:S(2)}, u32[]{:S(2)}) collective-permute-start(bf16[16,512]{1,0:T(8,128)(2,1)S(1)} %get-tuple-element.68), channel_id=1, source_target_pairs={{0,4},{4,0},{8,20},{12,16},{16,12},{20,8},{24,28},{28,24},{1,5},{5... | collective-permute-start | bytes 49160 | tf_op jit(solution)/shard_map/ppermute | solution.py:768
  12.6 3.7 %copy-start.10 = (f32[2,4,128]{2,1,0:T(4,128)S(1)}, f32[2,4,128]{2,1,0:T(4,128)}, u32[]{:S(2)}) copy-start(f32[2,4,128]{2,1,0:T(4,128)} %cw.3) | copy-start | bytes 12292
  12.8 3.5 %copy-start.11 = (f32[2,128]{1,0:T(2,128)S(1)}, f32[2,128]{1,0:T(2,128)}, u32[]{:S(2)}) copy-start(f32[2,128]{1,0:T(2,128)} %cb.1) | copy-start | bytes 3076
  16.3 3.0 %copy-start.4 = (bf16[256,128]{1,0:T(8,128)(2,1)S(1)}, bf16[256,128]{1,0:T(8,128)(2,1)}, u32[]{:S(2)}) copy-start(bf16[256,128]{1,0:T(8,128)(2,1)} %cot.1) | copy-start | bytes 196612
  17.7 7.1 %copy-start.5 = (bf16[128,256]{1,0:T(8,128)(2,1)S(1)}, bf16[128,256]{1,0:T(8,128)(2,1)}, u32[]{:S(2)}) copy-start(bf16[128,256]{1,0:T(8,128)(2,1)} %ow.3) | copy-start | bytes 196612
  17.7 5.0 %collective-permute-start.5 = (bf16[2,256,128]{2,1,0:T(8,128)(2,1)S(1)}, bf16[2,256,128]{2,1,0:T(8,128)(2,1)S(1)}, u32[]{:S(2)}, u32[]{:S(2)}) collective-permute-start(bf16[2,256,128]{2,1,0:T(8,128)(2,1)S(1)} %get-tuple-element.69), channel_id=1, source_target_pairs={{0,2},{1,3},{2,0},{3,1},{4,6},{5,7},{6,4},{7,5},{8,10},{9,11},{10,... | collective-permute-start | bytes 393224 | tf_op jit(solution)/shard_map/ppermute | solution.py:717
  19.3 4.3 %collective-permute-start.8 = (bf16[256,128]{1,0:T(8,128)(2,1)S(1)}, bf16[256,128]{1,0:T(8,128)(2,1)S(1)}, u32[]{:S(2)}, u32[]{:S(2)}) collective-permute-start(bf16[256,128]{1,0:T(8,128)(2,1)S(1)} %copy-done.4), channel_id=1, source_target_pairs={{0,2},{1,3},{2,0},{3,1},{4,6},{5,7},{6,4},{7,5},{8,10},{9,11},{10,... | collective-permute-start | bytes 196616 | tf_op jit(solution)/shard_map/ppermute | solution.py:717
  22.8 3.2 %collective-permute-start.6 = (bf16[2,256,128]{2,1,0:T(8,128)(2,1)S(1)}, bf16[2,256,128]{2,1,0:T(8,128)(2,1)S(1)}, u32[]{:S(2)}, u32[]{:S(2)}) collective-permute-start(bf16[2,256,128]{2,1,0:T(8,128)(2,1)S(1)} %add_convert_fusion.2.refs_1_), channel_id=1, source_target_pairs={{0,1},{1,0},{2,3},{3,2},{4,5},{5,4},{6,7},{7,6},{8,9},{9,8},{10,11... | collective-permute-start | bytes 393224 | tf_op jit(solution)/shard_map/ppermute | solution.py:717
  22.9 1.4 %collective-permute-start.7 = (bf16[256,128]{1,0:T(8,128)(2,1)S(1)}, bf16[256,128]{1,0:T(8,128)(2,1)S(1)}, u32[]{:S(2)}, u32[]{:S(2)}) collective-permute-start(bf16[256,128]{1,0:T(8,128)(2,1)S(1)} %copy-done.4), channel_id=1, source_target_pairs={{0,1},{1,0},{2,3},{3,2},{4,5},{5,4},{6,7},{7,6},{8,9},{9,8},{10,11... | collective-permute-start | bytes 196616 | tf_op jit(solution)/shard_map/ppermute | solution.py:717
  23.6 1.3 collective-permute-start.9
  24.8 1.2 copy-start.6
  24.8 1.2 copy-start.7
  26.0 0.7 copy-start.12
  43.9 4.0 %collective-permute-start.10 = (f32[72,128]{1,0:T(8,128)S(1)}, f32[72,128]{1,0:T(8,128)S(1)}, u32[]{:S(2)}, u32[]{:S(2)}) collective-permute-start(f32[72,128]{1,0:T(8,128)S(1)} %get-tuple-element.73), channel_id=1, source_target_pairs={{0,4},{4,0},{8,12},{12,8},{16,20},{20,16},{24,28},{28,24},{1,5},{5... | collective-permute-start | bytes 110600 | tf_op jit(solution)/shard_map/ppermute | solution.py:818
  44.5 4.2 %collective-permute-start.12 = (f32[72,128]{1,0:T(8,128)S(1)}, f32[72,128]{1,0:T(8,128)S(1)}, u32[]{:S(2)}, u32[]{:S(2)}) collective-permute-start(f32[72,128]{1,0:T(8,128)S(1)} %get-tuple-element.74), channel_id=1, source_target_pairs={{0,4},{4,0},{8,20},{12,16},{16,12},{20,8},{24,28},{28,24},{1,5},{5... | collective-permute-start | bytes 110600 | tf_op jit(solution)/shard_map/ppermute | solution.py:820
  46.0 4.0 %collective-permute-start.11 = (f32[72,128]{1,0:T(8,128)S(1)}, f32[72,128]{1,0:T(8,128)S(1)}, u32[]{:S(2)}, u32[]{:S(2)}) collective-permute-start(f32[72,128]{1,0:T(8,128)S(1)} %get-tuple-element.74), channel_id=1, source_target_pairs={{0,4},{4,0},{8,16},{12,20},{16,8},{20,12},{24,28},{28,24},{1,5},{5... | collective-permute-start | bytes 110600 | tf_op jit(solution)/shard_map/ppermute | solution.py:819
  50.0 0.7 copy-start.13
  79.1 6.3 %collective-permute-start.13 = (bf16[2,256,128]{2,1,0:T(8,128)(2,1)S(1)}, bf16[2,256,128]{2,1,0:T(8,128)(2,1)S(1)}, u32[]{:S(2)}, u32[]{:S(2)}) collective-permute-start(bf16[2,256,128]{2,1,0:T(8,128)(2,1)S(1)} %get-tuple-element.83), channel_id=1, source_target_pairs={{0,2},{1,3},{2,0},{3,1},{4,6},{5,7},{6,4},{7,5},{8,10},{9,11},{10,... | collective-permute-start | bytes 393224 | tf_op jit(solution)/shard_map/ppermute | solution.py:717
  81.4 5.5 %collective-permute-start.15 = (bf16[256,256]{1,0:T(8,128)(2,1)S(1)}, bf16[256,256]{1,0:T(8,128)(2,1)S(1)}, u32[]{:S(2)}, u32[]{:S(2)}) collective-permute-start(bf16[256,256]{1,0:T(8,128)(2,1)S(1)} %get-tuple-element.97), channel_id=1, source_target_pairs={{0,2},{1,3},{2,0},{3,1},{4,6},{5,7},{6,4},{7,5},{8,10},{9,11},{10,... | collective-permute-start | bytes 393224 | tf_op jit(solution)/shard_map/ppermute | solution.py:717
  85.5 1.4 %collective-permute-start.14 = (bf16[2,256,128]{2,1,0:T(8,128)(2,1)S(1)}, bf16[2,256,128]{2,1,0:T(8,128)(2,1)S(1)}, u32[]{:S(2)}, u32[]{:S(2)}) collective-permute-start(bf16[2,256,128]{2,1,0:T(8,128)(2,1)S(1)} %add_convert_fusion.1.one), channel_id=1, source_target_pairs={{0,1},{1,0},{2,3},{3,2},{4,5},{5,4},{6,7},{7,6},{8,9},{9,8},{10,11... | collective-permute-start | bytes 393224 | tf_op jit(solution)/shard_map/ppermute | solution.py:717
  88.7 15.2 %copy-start.3 = (bf16[256,128]{1,0:T(8,128)(2,1)S(1)}, bf16[256,128]{1,0:T(8,128)(2,1)}, u32[]{:S(2)}) copy-start(bf16[256,128]{1,0:T(8,128)(2,1)} %xo.3) | copy-start | bytes 196612
  88.7 17.9 %collective-permute-start.21 = (bf16[496,128]{1,0:T(8,128)(2,1)S(1)}, bf16[496,128]{1,0:T(8,128)(2,1)S(1)}, u32[]{:S(2)}, u32[]{:S(2)}) collective-permute-start(bf16[496,128]{1,0:T(8,128)(2,1)S(1)} %get-tuple-element.108), channel_id=1, source_target_pairs={{0,4},{4,0},{8,12},{12,8},{16,20},{20,16},{24,28},{28,24},{1,5},{5... | collective-permute-start | bytes 380936 | tf_op jit(solution)/shard_map/ppermute | solution.py:717
  89.0 14.9 %collective-permute-start.18 = (bf16[256,128]{1,0:T(8,128)(2,1)S(1)}, bf16[256,128]{1,0:T(8,128)(2,1)S(1)}, u32[]{:S(2)}, u32[]{:S(2)}) collective-permute-start(bf16[256,128]{1,0:T(8,128)(2,1)S(1)} %get-tuple-element.103), channel_id=1, source_target_pairs={{0,1},{1,0},{2,3},{3,2},{4,5},{5,4},{6,7},{7,6},{8,9},{9,8},{10,11... | collective-permute-start | bytes 196616 | tf_op jit(solution)/shard_map/ppermute | solution.py:717
  89.0 3.7 %collective-permute-start.26 = (f32[8,256]{1,0:T(8,128)S(1)}, f32[8,256]{1,0:T(8,128)S(1)}, u32[]{:S(2)}, u32[]{:S(2)}) collective-permute-start(f32[8,256]{1,0:T(8,128)S(1)} %get-tuple-element.109), channel_id=1, source_target_pairs={{0,2},{1,3},{2,0},{3,1},{4,6},{5,7},{6,4},{7,5},{8,10},{9,11},{10,... | collective-permute-start | bytes 24584 | tf_op jit(solution)/shard_map/ppermute | solution.py:717
  92.6 2.0 %collective-permute-start.27 = (f32[8,256]{1,0:T(8,128)S(1)}, f32[8,256]{1,0:T(8,128)S(1)}, u32[]{:S(2)}, u32[]{:S(2)}) collective-permute-start(f32[8,256]{1,0:T(8,128)S(1)} %add.46), channel_id=1, source_target_pairs={{0,1},{1,0},{2,3},{3,2},{4,5},{5,4},{6,7},{7,6},{8,9},{9,8},{10,11... | collective-permute-start | bytes 24584 | tf_op jit(solution)/shard_map/ppermute | solution.py:717
  92.6 9.3 %collective-permute-start.16 = (f32[2,16,128]{2,1,0:T(8,128)S(1)}, f32[2,16,128]{2,1,0:T(8,128)S(1)}, u32[]{:S(2)}, u32[]{:S(2)}) collective-permute-start(f32[2,16,128]{2,1,0:T(8,128)S(1)} %get-tuple-element.99), channel_id=1, source_target_pairs={{0,4},{4,0},{8,12},{12,8},{16,20},{20,16},{24,28},{28,24},{1,5},{5... | collective-permute-start | bytes 49160 | tf_op jit(solution)/shard_map/ppermute | solution.py:894
  94.4 9.5 %collective-permute-start.17 = (f32[2,16,128]{2,1,0:T(8,128)S(1)}, f32[2,16,128]{2,1,0:T(8,128)S(1)}, u32[]{:S(2)}, u32[]{:S(2)}) collective-permute-start(f32[2,16,128]{2,1,0:T(8,128)S(1)} %get-tuple-element.100), channel_id=1, source_target_pairs={{0,4},{4,0},{8,20},{12,16},{16,12},{20,8},{24,28},{28,24},{1,5},{5... | collective-permute-start | bytes 49160 | tf_op jit(solution)/shard_map/ppermute | solution.py:895
  94.7 3.7 %collective-permute-start.28 = (f32[8,256]{1,0:T(8,128)S(1)}, f32[8,256]{1,0:T(8,128)S(1)}, u32[]{:S(2)}, u32[]{:S(2)}) collective-permute-start(f32[8,256]{1,0:T(8,128)S(1)} %add.47), channel_id=1, source_target_pairs={{0,4},{4,0},{8,12},{12,8},{16,20},{20,16},{24,28},{28,24},{1,5},{5... | collective-permute-start | bytes 24584 | tf_op jit(solution)/shard_map/ppermute | solution.py:717
  98.3 21.4 %collective-permute-start.31 = (f32[8,256]{1,0:T(8,128)S(1)}, f32[8,256]{1,0:T(8,128)S(1)}, u32[]{:S(2)}, u32[]{:S(2)}) collective-permute-start(f32[8,256]{1,0:T(8,128)S(1)} %add.48), channel_id=1, source_target_pairs={{0,24},{4,28},{8,16},{12,20},{16,8},{20,12},{24,0},{28,4},{1,25},{... | collective-permute-start | bytes 24584 | tf_op jit(solution)/shard_map/ppermute | solution.py:717
  101.9 17.8 %collective-permute-start.30 = (f32[8,256]{1,0:T(8,128)S(1)}, f32[8,256]{1,0:T(8,128)S(1)}, u32[]{:S(2)}, u32[]{:S(2)}) collective-permute-start(f32[8,256]{1,0:T(8,128)S(1)} %add.48), channel_id=1, source_target_pairs={{0,16},{4,20},{8,24},{12,28},{16,0},{20,4},{24,8},{28,12},{1,17},{... | collective-permute-start | bytes 24584 | tf_op jit(solution)/shard_map/ppermute | solution.py:717
  105.7 5.0 %collective-permute-start.19 = (bf16[256,256]{1,0:T(8,128)(2,1)S(1)}, bf16[256,256]{1,0:T(8,128)(2,1)S(1)}, u32[]{:S(2)}, u32[]{:S(2)}) collective-permute-start(bf16[256,256]{1,0:T(8,128)(2,1)S(1)} %get-tuple-element.106), channel_id=1, source_target_pairs={{0,2},{1,3},{2,0},{3,1},{4,6},{5,7},{6,4},{7,5},{8,10},{9,11},{10,... | collective-permute-start | bytes 393224 | tf_op jit(solution)/shard_map/ppermute | solution.py:717
  106.6 7.9 %collective-permute-start.24 = (bf16[496,128]{1,0:T(8,128)(2,1)S(1)}, bf16[496,128]{1,0:T(8,128)(2,1)S(1)}, u32[]{:S(2)}, u32[]{:S(2)}) collective-permute-start(bf16[496,128]{1,0:T(8,128)(2,1)S(1)} %add_convert_fusion.4), channel_id=1, source_target_pairs={{0,24},{4,28},{8,16},{12,20},{16,8},{20,12},{24,0},{28,4},{1,25},{... | collective-permute-start | bytes 380936 | tf_op jit(solution)/shard_map/ppermute | solution.py:717
  108.4 10.0 %collective-permute-start.23 = (bf16[496,128]{1,0:T(8,128)(2,1)S(1)}, bf16[496,128]{1,0:T(8,128)(2,1)S(1)}, u32[]{:S(2)}, u32[]{:S(2)}) collective-permute-start(bf16[496,128]{1,0:T(8,128)(2,1)S(1)} %add_convert_fusion.4), channel_id=1, source_target_pairs={{0,16},{4,20},{8,24},{12,28},{16,0},{20,4},{24,8},{28,12},{1,17},{... | collective-permute-start | bytes 380936 | tf_op jit(solution)/shard_map/ppermute | solution.py:717
  110.7 7.7 %collective-permute-start.22 = (bf16[496,128]{1,0:T(8,128)(2,1)S(1)}, bf16[496,128]{1,0:T(8,128)(2,1)S(1)}, u32[]{:S(2)}, u32[]{:S(2)}) collective-permute-start(bf16[496,128]{1,0:T(8,128)(2,1)S(1)} %add_convert_fusion.4), channel_id=1, source_target_pairs={{0,8},{4,12},{8,0},{12,4},{16,24},{20,28},{24,16},{28,20},{1,9},{5... | collective-permute-start | bytes 380936 | tf_op jit(solution)/shard_map/ppermute | solution.py:717
  114.5 5.3 %collective-permute-start.29 = (f32[8,256]{1,0:T(8,128)S(1)}, f32[8,256]{1,0:T(8,128)S(1)}, u32[]{:S(2)}, u32[]{:S(2)}) collective-permute-start(f32[8,256]{1,0:T(8,128)S(1)} %add.48), channel_id=1, source_target_pairs={{0,8},{4,12},{8,0},{12,4},{16,24},{20,28},{24,16},{28,20},{1,9},{5... | collective-permute-start | bytes 24584 | tf_op jit(solution)/shard_map/ppermute | solution.py:717
  118.4 1.4 %collective-permute-start.20 = (bf16[256,256]{1,0:T(8,128)(2,1)S(1)}, bf16[256,256]{1,0:T(8,128)(2,1)S(1)}, u32[]{:S(2)}, u32[]{:S(2)}) collective-permute-start(bf16[256,256]{1,0:T(8,128)(2,1)S(1)} %add_convert_fusion.one), channel_id=1, source_target_pairs={{0,1},{1,0},{2,3},{3,2},{4,5},{5,4},{6,7},{7,6},{8,9},{9,8},{10,11... | collective-permute-start | bytes 393224 | tf_op jit(solution)/shard_map/ppermute | solution.py:717
  118.5 5.9 %collective-permute-start.25 = (bf16[496,128]{1,0:T(8,128)(2,1)S(1)}, bf16[496,128]{1,0:T(8,128)(2,1)S(1)}, u32[]{:S(2)}, u32[]{:S(2)}) collective-permute-start(bf16[496,128]{1,0:T(8,128)(2,1)S(1)} %add_convert_fusion.3.refs_0_), channel_id=1, source_target_pairs={{0,4},{4,0},{8,12},{12,8},{16,20},{20,16},{24,28},{28,24},{1,5},{5... | collective-permute-start | bytes 380936 | tf_op jit(solution)/shard_map/ppermute | solution.py:717

commit v2 on v1

v2 whole, which is shorter than its diff:
```python
import functools

import jax
import jax.numpy as jnp
from jax import lax
from jax.experimental import pallas as pl
from jax.experimental.pallas import tpu as pltpu
from jax.sharding import PartitionSpec as P

N = 16
R = 16
WINDOW = 16384
LANES = 128
CHUNKS = 8
EPSILON = 1e-06
LOG2E = 1.4426950408889634
F32 = jnp.float32
BF16 = jnp.bfloat16
VM = pl.BlockSpec(memory_space=pltpu.VMEM)
FLIPS = (False, True, True, False)


def nn(left, right):
    return lax.dot_general(left, right, (((1,), (0,)), ((), ())), preferred_element_type=F32)


def nt(left, right):
    return lax.dot_general(left, right, (((1,), (1,)), ((), ())), preferred_element_type=F32)


def tn(left, right):
    return lax.dot_general(left, right, (((0,), (0,)), ((), ())), preferred_element_type=F32)


def iota(shape, dim):
    return lax.broadcasted_iota(jnp.int32, shape, dim)


def one_hot(mask):
    return jnp.where(mask, 1.0, 0.0).astype(BF16)


def permuter(tok):
    steps = tok // CHUNKS
    row, col = iota((tok, tok), 0), iota((tok, tok), 1)
    return one_hot((row % CHUNKS) * steps + row // CHUNKS == col)


def unpermuter(tok):
    steps = tok // CHUNKS
    row, col = iota((tok, tok), 0), iota((tok, tok), 1)
    return one_hot((col % CHUNKS) * steps + col // CHUNKS == row)


def mirror(width):
    return one_hot(iota((width, width), 0) + iota((width, width), 1) == width - 1)


def sigmoid(v):
    return 1.0 / (1.0 + jnp.exp(-v))


def silu(v):
    return v * sigmoid(v)


def silu_slope(v):
    logistic = sigmoid(v)
    return logistic * (1.0 + v * (1.0 - logistic))


def softplus(v):
    return jnp.maximum(v, 0.0) + jnp.log1p(jnp.exp(-jnp.abs(v)))


def low(v):
    return v.astype(BF16)


class Geometry:
    def __init__(self, tok, rows):
        self.tok = tok
        self.rows = rows
        self.window = min(WINDOW, tok * rows // 2)
        self.members = self.window // tok
        self.steps = tok // CHUNKS

    def place(self, lengths_ref):
        row = lax.axis_index("rows")
        shifted = row * self.tok + self.window // 2
        offset = lax.rem(shifted, self.window)
        length = lengths_ref[lax.div(shifted, self.window)]
        return row, offset, length

    def valid(self, lengths_ref):
        _, offset, length = self.place(lengths_ref)
        row = iota((self.tok, 1), 0)
        token = (row % CHUNKS) * self.steps + row // CHUNKS
        return jnp.where(offset + token < length, 1.0, 0.0)

    def local(self):
        row = lax.axis_index("rows")
        return lax.rem(row + self.members // 2, self.members)

    def near(self):
        return [(i, i ^ 1) for i in range(self.rows)]

    def far(self):
        if self.members == 4:
            return self.swaps(lambda k: 3 - k)
        out = []
        for i in range(1, self.rows, 2):
            out += [(i, (i + 1) % self.rows), ((i + 1) % self.rows, i)]
        return out

    def across(self):
        return self.swaps(lambda k: (k + 2) % 4)

    def swaps(self, other):
        out = []
        for i in range(self.rows):
            local = (i + 2) % 4
            j = i - local + other(local)
            out.append((i, j if 0 <= j < self.rows else i ^ 1))
        return out


def run(kernel, outs, *args, anywhere=0, scratch=(), name=None, micros=1):
    single = isinstance(outs, tuple)
    shapes = [outs] if single else list(outs)
    args = [pltpu.with_memory_space_constraint(a, pltpu.HBM) for a in args[:anywhere]] + list(args[anywhere:])
    got = pl.pallas_call(
        kernel,
        out_shape=[jax.ShapeDtypeStruct(s, d) for s, d in shapes],
        in_specs=[pl.BlockSpec(memory_space=pltpu.HBM)] * anywhere + [VM] * (len(args) - anywhere),
        out_specs=[VM] * len(shapes),
        scratch_shapes=list(scratch),
        name=name,
        compiler_params=pltpu.CompilerParams(vmem_limit_bytes=48 * 1024 * 1024),
        cost_estimate=pl.CostEstimate(flops=0, bytes_accessed=int(micros * 3.0e6), transcendentals=0),
    )(*args)
    return got[0] if single else got


def assemble(refs, scratch):
    mine = lax.axis_index("ch")
    for distance, ref in enumerate(refs):
        scratch[lax.bitwise_xor(mine, distance)] = ref[...]
    return (
        jnp.concatenate([scratch[0], scratch[1]], axis=1),
        jnp.concatenate([scratch[2], scratch[3]], axis=1),
    )


def prepare_kernel(
    geo, lengths_in, x_in, c_in, w_in, ow_in, stw_in, gain_in, cw_in, cb_in, sw_in, stb_in, decay_in, skip_in,
    x_out, c_out, valid, edge, turn, mover, back, gains, weights, outs, select, table, spread, tiny, stw,
    lengths, gain, cw, cb, sw, stb, decay, skip, sems,
):
    pairs = (
        (lengths_in, lengths), (w_in, weights.at[0:2]), (ow_in, outs.at[0]), (stw_in, stw), (gain_in, gain),
        (cw_in, cw), (cb_in, cb), (sw_in, sw), (stb_in, stb), (decay_in, decay), (skip_in, skip),
        (x_in, x_out), (c_in, c_out),
    )
    copies = [pltpu.make_async_copy(source, target, sems.at[i]) for i, (source, target) in enumerate(pairs)]
    for copy in copies:
        copy.start()
    tok = geo.tok
    width = turn.shape[0]
    flip = mirror(width)
    turn[...] = flip
    mover[...] = permuter(tok)
    back[...] = unpermuter(tok)
    for at in range(0, 2 * N):
        key = iota((LANES, LANES), 0) % 64
        spread[:, at * LANES : (at + 1) * LANES] = one_hot(key == R + at)
    select[...] = jnp.zeros_like(select)
    tiny[...] = jnp.zeros_like(tiny)
    for copy in copies:
        copy.wait()
    valid[...] = jnp.broadcast_to(geo.valid(lengths), valid.shape)
    edge[...] = jnp.broadcast_to(rim_valid(geo, lengths), edge.shape)
    plain = jnp.broadcast_to(gain[...], (8, width))
    high = low(plain)
    rest = plain - high.astype(F32)
    middle = low(rest)
    turned = nn(high, flip) + nn(middle, flip) + nn(low(rest - middle.astype(F32)), flip)
    gains[:1] = gain[...]
    gains[1:] = turned[:1]
    for k in range(2):
        weights[2 + k] = low(nn(flip, weights[k]))
    outs[1] = low(nn(outs[0], flip))
    amount = sw.shape[1]
    for course in range(2):
        select[course, 64 * course : 64 * course + amount] = sw[course]
        natural = -jnp.exp(decay[course])
        for n in range(N):
            level = jnp.broadcast_to(natural[n : n + 1], (CHUNKS, LANES))
            table[course, n] = level
            table[2 + course, n] = level * LOG2E
    taps = cw.shape[1]
    for course in range(2):
        tiny[course * taps : (course + 1) * taps] = cw[course]
        tiny[24 + course * N : 24 + (course + 1) * N] = -LOG2E * jnp.exp(decay[course])
    tiny[8:10] = cb[...]
    tiny[10:12] = stb[...]
    tiny[12:14] = skip[...]


def project_kernel(geo, xo, xc, xy, xd, valid, turn, mover, gains, w, normed, inputs, gates, near, far, scratch):
    tok = geo.tok
    width = w.shape[1]
    sides = assemble((xo, xc, xy, xd), scratch)
    even = lax.rem(lax.axis_index("rows"), 2) == 0
    for half, side in enumerate(sides):
        first, last = side[:16], side[tok - 16 :]
        lanes = slice(half * width, (half + 1) * width)
        near[:, lanes] = jnp.where(even, last.astype(F32), first.astype(F32)).astype(BF16)
        far[:, lanes] = jnp.where(even, first.astype(F32), last.astype(F32)).astype(BF16)
    both = jnp.concatenate([w[0], w[1]], axis=1)
    for strand in range(2):
        side = sides[strand]
        if strand == 1:
            side = low(nn(side, turn[...]))
        source = nn(mover[...], side)
        inverse = lax.rsqrt(jnp.mean(source * source, axis=-1, keepdims=True) + EPSILON)
        rows = low(source * inverse * gains[:1])
        normed[strand] = rows
        out = nn(rows, both)
        lanes = out.shape[1] // 2
        inputs[strand] = low(out[:, :lanes] * valid[...])
        gates[strand] = out[:, lanes:]


def cotangent_kernel(geo, co, cc, cy, cd, gates, valid, turn, mover, outs, moved, gm, dys, scratch):
    tok = geo.tok
    sides = assemble((co, cc, cy, cd), scratch)
    for strand in range(2):
        side = sides[strand]
        if strand == 1:
            side = low(nn(side, turn[...]))
        rows = low(nn(mover[...], side))
        moved[strand] = rows
        grad = nt(rows, outs[0]) * valid[...]
        gm[strand] = grad
        dys[strand] = grad * silu(gates[strand])


def rim_valid(geo, lengths_ref):
    _, offset, length = geo.place(lengths_ref)
    row = iota((32, 1), 0)
    token = jnp.where(row < 16, row - 16, geo.tok + row - 16) + offset
    index = token - offset + lax.axis_index("rows") * geo.tok
    inside = (token >= 0) & (token < geo.window) & (token < length)
    inside = inside & (index >= 0) & (index < geo.tok * geo.rows)
    return jnp.where(inside, 1.0, 0.0)


def fill_padded(padded, main, rims, steps):
    rim = padded.shape[0] // CHUNKS - steps
    rim = rim // 2
    lanes = main.shape[1]
    sub = iota((CHUNKS, lanes), 0)
    padded[rim * CHUNKS : (rim + steps) * CHUNKS] = main
    for k in range(1, rim + 1):
        block = main[(steps - k) * CHUNKS : (steps - k + 1) * CHUNKS]
        moved = pltpu.roll(block, 1, 0)
        edge = jnp.broadcast_to(rims[16 - k : 17 - k], (CHUNKS, lanes))
        padded[(rim - k) * CHUNKS : (rim - k + 1) * CHUNKS] = jnp.where(sub == 0, edge, moved)
    for k in range(rim):
        block = main[k * CHUNKS : (k + 1) * CHUNKS]
        moved = pltpu.roll(block, CHUNKS - 1, 0)
        edge = jnp.broadcast_to(rims[16 + k : 17 + k], (CHUNKS, lanes))
        at = rim + steps + k
        padded[at * CHUNKS : (at + 1) * CHUNKS] = jnp.where(sub == CHUNKS - 1, edge, moved)


def tap_start(tap, taps, flipped):
    return (2 * (taps - 1) - tap if flipped else tap) * CHUNKS


def conv_kernel(
    geo, inputs, near, far, edge, turn, gains, w, select, tiny, after, padded, rims_normed, pre, act, message
):
    tok, steps = geo.tok, geo.steps
    taps = (padded.shape[1] // CHUNKS - steps) // 2 + 1
    lanes = w.shape[2]
    width = w.shape[1]
    even = lax.rem(lax.axis_index("rows"), 2) == 0
    for strand in range(2):
        part = slice(strand * width, (strand + 1) * width)
        one, two = near[:, part].astype(F32), far[:, part].astype(F32)
        source = jnp.concatenate([jnp.where(even, two, one), jnp.where(even, one, two)], axis=0)
        if strand == 1:
            source = nn(low(source), turn[...])
        inverse = lax.rsqrt(jnp.mean(source * source, axis=-1, keepdims=True) + EPSILON)
        rows = low(source * inverse * gains[:1])
        rims_normed[strand] = rows
        edges = low(nn(rows, w[0]) * edge[...]).astype(F32)
        main = inputs[strand].astype(F32)
        fill_padded(padded.at[strand], main, edges, steps)
        total = jnp.zeros((tok, LANES), F32)
        for course in range(2):
            member = 2 * strand + course
            running = jnp.broadcast_to(tiny[8 + course : 9 + course], (tok, lanes))
            for tap in range(taps):
                at = tap_start(tap, taps, FLIPS[member])
                row = course * taps + tap
                running = running + tiny[row : row + 1] * padded[strand, at : at + tok]
            pre[member] = running
            active = low(silu(running))
            act[member] = active
            total = total + nt(active, select[course])
        message[strand] = low(total)


def columns(n):
    return slice(n * LANES, (n + 1) * LANES)


def summary_kernel(
    geo, one, two, act, dys, stw, tiny, table, spread, valid,
    proj, raw, step, drive, chunk_p, chunk_h, chunk_w, wide, near, far, up, down,
):
    tok, steps = geo.tok, geo.steps
    for strand in range(2):
        total = one[strand].astype(F32) + two[strand].astype(F32)
        for course in range(2):
            member = 2 * strand + course
            here = total if course == 0 else pltpu.roll(total, 64, 1)
            rounded = low(here)
            proj[member] = rounded
            rest = pltpu.roll(here - rounded.astype(F32), 64, 1)
            lane = iota(here.shape, 1)
            split = low(jnp.where(lane < 64, here, rest))
            for at in range(0, 2 * N * LANES, 512):
                wide[member, :, at : at + 512] = nn(split, spread[:, at : at + 512])
            step_raw = nn(rounded[:, :R], stw[course]) + tiny[10 + course : 11 + course]
            step_row = softplus(step_raw) * valid[...]
            raw[member] = step_raw
            step[member] = step_row
            drive[member] = step_row * act[member].astype(F32)
    def sweep(member, flipped):
        strand, course = member // 2, lax.rem(member, 2)
        for base in range(0, N, 8):

            def body(k, carry):
                ps, hs, ws = carry
                t = steps - 1 - k if flipped else k
                rows = pl.ds(pl.multiple_of(t * CHUNKS, CHUNKS), CHUNKS)
                s, d, y = step[member, rows], drive[member, rows], dys[strand, rows]
                np_, nh, nw = [], [], []
                for i in range(8):
                    n = base + i
                    decay_here = jnp.exp2(s * table[2 + course, n])
                    p = ps[i] * decay_here
                    np_.append(p)
                    nh.append(hs[i] * decay_here + wide[member, rows, columns(n)] * d)
                    nw.append(ws[i] + p * (wide[member, rows, columns(N + n)] * y))
                return tuple(np_), tuple(nh), tuple(nw)

            zero = jnp.zeros((CHUNKS, LANES), F32)
            start = (tuple([zero + 1.0] * 8), (zero,) * 8, (zero,) * 8)
            ps, hs, ws = lax.fori_loop(0, steps, body, start, unroll=4)
            for i in range(8):
                rows = slice((base + i) * CHUNKS, (base + i + 1) * CHUNKS)
                chunk_p[member, rows] = ps[i]
                chunk_h[member, rows] = hs[i]
                chunk_w[member, rows] = ws[i]

    lax.fori_loop(0, 2, lambda i, c: (sweep(3 * i, False), c)[1], 0)
    lax.fori_loop(0, 2, lambda i, c: (sweep(1 + i, True), c)[1], 0)

    slots = {0: (0, 2), 3: (1, 3), 1: (2, 0), 2: (3, 1)}
    for member in range(4):
        h = jnp.zeros((N, LANES), F32)
        w = jnp.zeros((N, LANES), F32)
        order = list(range(CHUNKS))
        forward = order[::-1] if FLIPS[member] else order
        for j in forward:
            rows = pl.ds(j, N, stride=CHUNKS)
            h = chunk_p[member, rows] * h + chunk_h[member, rows]
        for j in forward[::-1]:
            rows = pl.ds(j, N, stride=CHUNKS)
            w = chunk_p[member, rows] * w + chunk_w[member, rows]
        length = jnp.sum(step[member], axis=0, keepdims=True)
        slot_up, slot_down = slots[member]
        goes_up, goes_down = (w, h) if FLIPS[member] else (h, w)
        up[slot_up * N : (slot_up + 1) * N] = goes_up
        down[slot_down * N : (slot_down + 1) * N] = goes_down
        up[4 * N + slot_up : 4 * N + slot_up + 1] = length
        down[4 * N + slot_down : 4 * N + slot_down + 1] = length
    up[4 * N + 4 :] = jnp.zeros((4, LANES), F32)
    down[4 * N + 4 :] = jnp.zeros((4, LANES), F32)
    if near is not None:
        local = geo.local()
        near[...] = jnp.where(lax.rem(local, 2) == 0, up[...], down[...])
        far[...] = jnp.where(local < 2, up[...], down[...])


UP_MEMBERS = (0, 3, 1, 2)
DOWN_MEMBERS = (1, 2, 0, 3)


def scan_kernel(
    geo, slot_refs, act, proj, raw, step, drive, chunk_p, chunk_h, chunk_w, wide, spread,
    dys, gm, gates, stw, tiny, table, valid,
    mixed, dgate, dact, message, small,
    slots, enter, adjoint, states, quads, out_y, slope_y, pull_y, dproj, dacc,
):
    tok, steps = geo.tok, geo.steps
    count = geo.members
    row = lax.axis_index("rows")
    local = geo.local()
    base_row = row - local
    if len(slot_refs) == 1:
        slots = slot_refs[0]
    else:
        slots[local] = jnp.zeros(slots.shape[1:], F32)
        others = (lax.bitwise_xor(local, 1), lax.rem(local + 2, 4), 3 - local)
        for at, ref in zip(others, slot_refs):
            slots[at] = ref[...]
    dacc[...] = jnp.zeros_like(dacc)

    def fold(ascending, carried):
        members = UP_MEMBERS if ascending else DOWN_MEMBERS
        tables = [tiny[24 + N * (m % 2) : 24 + N * (m % 2) + N] for m in members]

        def one(i, carried):
            k = i if ascending else count - 1 - i
            there = base_row + k
            use = (k < local) if ascending else (k > local)
            use = use & (there >= 0) & (there < geo.rows)
            out = []
            for q in range(4):
                length = slots[k, 4 * N + q : 4 * N + q + 1]
                new = jnp.exp2(tables[q] * length) * carried[q] + slots[k, q * N : (q + 1) * N]
                out.append(jnp.where(use, new, carried[q]))
            return tuple(out)

        return lax.fori_loop(0, count, one, carried)

    zero = (jnp.zeros((N, LANES), F32),) * 4
    from_below = fold(True, zero)
    from_above = fold(False, zero)
    order = list(range(CHUNKS))
    for q in range(4):
        for value, member, js in (
            (from_below[q], UP_MEMBERS[q], order),
            (from_above[q], DOWN_MEMBERS[q], order[::-1]),
        ):
            target, source = (enter, chunk_h) if q < 2 else (adjoint, chunk_w)
            for j in js:
                rows = pl.ds(j, N, stride=CHUNKS)
                target[member, rows] = value
                value = chunk_p[member, rows] * value + source[member, rows]

    def sweep(member, flipped):
        strand, course = member // 2, lax.rem(member, 2)
        states[: N * CHUNKS] = enter[member]

        def ahead(i, carry):
            hs = list(carry)
            kept = []
            for sub in range(2):
                k = 2 * i + sub
                t = steps - 1 - k if flipped else k
                rows = pl.ds(pl.multiple_of(t * CHUNKS, CHUNKS), CHUNKS)
                s, d, y = step[member, rows], drive[member, rows], dys[strand, rows]
                total = jnp.zeros((CHUNKS, LANES), F32)
                products = []
                for n in range(N):
                    hs[n] = hs[n] * jnp.exp2(s * table[2 + course, n]) + wide[member, rows, columns(n)] * d
                    total = total + wide[member, rows, columns(N + n)] * hs[n]
                    products.append(y * hs[n])
                    at = pl.multiple_of(((k + 1) * N + n) * CHUNKS, CHUNKS)
                    states[pl.ds(at, CHUNKS)] = hs[n]
                out_y[member, rows] = total
                kept.append(products)
            pair = steps // 2 - 1 - i if flipped else i
            rows = pl.ds(pl.multiple_of(pair * 16, 16), 16)
            first, second = (kept[1], kept[0]) if flipped else (kept[0], kept[1])
            for n in range(N):
                both = low(jnp.concatenate([first[n], second[n]], axis=0))
                quads[rows, (N + n) * LANES : (N + n + 1) * LANES] = both
            return tuple(hs)

        start = tuple(enter[member, n * CHUNKS : (n + 1) * CHUNKS] for n in range(N))
        lax.fori_loop(0, steps // 2, ahead, start)

        def back(i, carry):
            cs, ds = list(carry[0]), list(carry[1])
            kept = []
            for sub in range(2):
                k = steps - 1 - (2 * i + sub)
                t = steps - 1 - k if flipped else k
                rows = pl.ds(pl.multiple_of(t * CHUNKS, CHUNKS), CHUNKS)
                s, d, y = step[member, rows], drive[member, rows], dys[strand, rows]
                pulled = jnp.zeros((CHUNKS, LANES), F32)
                slope = jnp.zeros((CHUNKS, LANES), F32)
                products = []
                for n in range(N):
                    lam = y * wide[member, rows, columns(N + n)] + cs[n]
                    pulled = pulled + lam * wide[member, rows, columns(n)]
                    products.append(lam * d)
                    cs[n] = lam * jnp.exp2(s * table[2 + course, n])
                    at = pl.multiple_of((k * N + n) * CHUNKS, CHUNKS)
                    u = cs[n] * states[pl.ds(at, CHUNKS)]
                    slope = slope + u * table[course, n]
                    ds[n] = ds[n] + u * s
                slope_y[member, rows] = slope
                pull_y[member, rows] = pulled
                kept.append(products)
            pair = i if flipped else steps // 2 - 1 - i
            rows = pl.ds(pl.multiple_of(pair * 16, 16), 16)
            first, second = (kept[0], kept[1]) if flipped else (kept[1], kept[0])
            for n in range(N):
                both = low(jnp.concatenate([first[n], second[n]], axis=0))
                quads[rows, n * LANES : (n + 1) * LANES] = both
            return tuple(cs), tuple(ds)

        start = tuple(adjoint[member, n * CHUNKS : (n + 1) * CHUNKS] for n in range(N))
        zeros = (jnp.zeros((CHUNKS, LANES), F32),) * N
        _, ds = lax.fori_loop(0, steps // 2, back, (start, zeros))
        for n in range(N):
            rows = slice(n * CHUNKS, (n + 1) * CHUNKS)
            dacc[course, rows] = dacc[course, rows] + ds[n]
        dproj[member] = nt(spread[:64], quads[...])

    lax.fori_loop(0, 2, lambda i, c: (sweep(3 * i, False), c)[1], 0)
    lax.fori_loop(0, 2, lambda i, c: (sweep(1 + i, True), c)[1], 0)

    small[...] = jnp.zeros_like(small)
    for course in range(2):
        for n in range(N):
            total = jnp.sum(dacc[course, n * CHUNKS : (n + 1) * CHUNKS], axis=0, keepdims=True)
            at = 2 * R + course * N + n
            small[at : at + 1] = total * table[course, n, :1]
    for strand in range(2):
        joined = jnp.zeros((tok, LANES), F32)
        grad = dys[strand]
        for course in range(2):
            member = 2 * strand + course
            active = act[member].astype(F32)
            joined = joined + out_y[member] + tiny[12 + course : 13 + course] * active
            raw_grad = slope_y[member] + pull_y[member] * active
            rounded = low(raw_grad * valid[...] * sigmoid(raw[member]))
            dact[member] = pull_y[member] * step[member] + grad * tiny[12 + course : 13 + course]
            rows = slice(course * R, (course + 1) * R)
            small[rows] += tn(proj[member], rounded)[:R]
            at = 2 * R + 2 * N + course
            small[at : at + 1] += jnp.sum(rounded.astype(F32), axis=0, keepdims=True)
            small[at + 2 : at + 3] += jnp.sum(grad * active, axis=0, keepdims=True)
            message[strand, 64 * course : 64 * course + R] = low(nt(stw[course], rounded))
            message[strand, 64 * course + R : 64 * course + 64] = low(dproj[member, R:])
        gate = gates[strand]
        mixed[strand] = low(joined * silu(gate) * valid[...])
        dgate[strand] = low(gm[strand] * joined * silu_slope(gate))


E_ROWS = 608
L_ROWS = 384
GAIN_ROWS = 16


def halves(pack, total, keep, send):
    half = total // 2
    mine = lax.rem(lax.axis_index("rows"), 2)
    if keep.shape[0] >= total:
        keep[:total] = pack[:total]
        send[:half] = jnp.zeros((half, LANES), BF16)
    else:
        keep[:half] = pack[pl.ds(pl.multiple_of(mine * half, 16), half)]
        send[:half] = low(pack[pl.ds(pl.multiple_of((1 - mine) * half, 16), half)])


def dense_kernel(
    geo, mixed, outs, moved, dgate, normed, weights, back, small, kept, sent, keep, send, g_gate, dn_gate, pack
):
    width = weights.shape[1]
    second = lax.axis_index("ch") >= 2
    branches = []
    grad_out = jnp.zeros((LANES, width), F32)
    grad_gate = jnp.zeros(g_gate.shape, F32)
    for strand in range(2):
        branches.append(nn(low(nn(back[...], mixed[strand])), outs[strand]))
        grad_out = grad_out + tn(mixed[strand], moved[strand])
        grad_gate = grad_gate + tn(normed[strand], dgate[strand])
        dn_gate[strand] = nt(low(nn(back[...], dgate[strand])), weights[1 + 2 * strand])
    kept[...] = jnp.where(second, branches[1], branches[0])
    sent[...] = low(jnp.where(second, branches[0], branches[1]))
    g_gate[...] = grad_gate
    pack[:width] = grad_gate
    pack[width : width + LANES] = grad_out[:, :LANES]
    pack[width + LANES : width + 2 * LANES] = grad_out[:, LANES:]
    pack[width + 2 * LANES : width + 2 * LANES + 80] = small[...]
    pack[width + 2 * LANES + 80 :] = jnp.zeros((16, LANES), F32)
    halves(pack, E_ROWS, keep, send)


def conv_back_kernel(
    geo, one, two, act, dact, pre, padded, tiny, select, normed, rims_normed, gains, w, g_gate, valid, edge,
    res_kept, res_got,
    xg, near, far, keep, send, res_own, res_sent,
    pad_grad, pack,
):
    tok, steps = geo.tok, geo.steps
    taps = (padded.shape[1] // CHUNKS - steps) // 2 + 1
    width = w.shape[1]
    even = lax.rem(lax.axis_index("rows"), 2) == 0
    rim = taps - 1
    sub = iota((CHUNKS, LANES), 0)
    pack[...] = jnp.zeros_like(pack)
    grad_select = [jnp.zeros((64, LANES), F32)] * 2
    grad_in = jnp.zeros((width, LANES), F32)
    at_conv = width + LANES - 32
    for strand in range(2):
        pad_grad[...] = jnp.zeros_like(pad_grad)
        rounded = low(one[strand].astype(F32) + two[strand].astype(F32))
        for course in range(2):
            member = 2 * strand + course
            mine = slice(64 * course, 64 * course + 64)
            grad_select[course] = grad_select[course] + nn(rounded[mine], act[member])
            total = dact[member] + tn(rounded, select[course])
            grad = total * silu_slope(pre[member])
            row = at_conv + 8 + course
            pack[row : row + 1] += jnp.sum(grad, axis=0, keepdims=True)
            for tap in range(taps):
                at = tap_start(tap, taps, FLIPS[member])
                row = at_conv + course * taps + tap
                pack[row : row + 1] += jnp.sum(grad * padded[strand, at : at + tok], axis=0, keepdims=True)
                at_tap = course * taps + tap
                pad_grad[at : at + tok] += tiny[at_tap : at_tap + 1] * grad
        before = [jnp.zeros((1, LANES), F32)] * (16 - rim)
        after = []
        for k in range(rim, 0, -1):
            block = pad_grad[(rim - k) * CHUNKS : (rim - k + 1) * CHUNKS]
            before.append(block[:1])
            moved = jnp.where(sub == CHUNKS - 1, 0.0, pltpu.roll(block, CHUNKS - 1, 0))
            at = (rim + steps - k) * CHUNKS
            pad_grad[at : at + CHUNKS] += moved
        for k in range(rim):
            at = (rim + steps + k) * CHUNKS
            block = pad_grad[at : at + CHUNKS]
            after.append(block[CHUNKS - 1 :])
            moved = jnp.where(sub == 0, 0.0, pltpu.roll(block, 1, 0))
            at = (rim + k) * CHUNKS
            pad_grad[at : at + CHUNKS] += moved
        after += [jnp.zeros((1, LANES), F32)] * (16 - rim)
        rims = jnp.concatenate(before + after, axis=0) * edge[...]
        main = pad_grad[rim * CHUNKS : (rim + steps) * CHUNKS]
        xg[strand] = main
        grad_in = grad_in + tn(normed[strand], low(main * valid[...])) + tn(rims_normed[strand], low(rims))
        near[strand] = jnp.where(even, rims[16:], rims[:16])
        far[strand] = jnp.where(even, rims[:16], rims[16:])
    pack[:width] = grad_in
    amount = LANES // 2 - 16
    for course in range(2):
        pack[width + course * amount : width + (course + 1) * amount] = grad_select[course][:amount]
    halves(pack, L_ROWS, keep, send)
    product = grad_in * w[0].astype(F32) + g_gate[...] * w[1].astype(F32)
    high = low(product)
    ones = jnp.ones((8, LANES), BF16)
    gain_part = (nt(ones, high) + nt(ones, low(product - high.astype(F32)))) / gains[:1]
    at = keep.shape[0] - GAIN_ROWS
    keep[at : at + 8] = gain_part[:, :LANES]
    keep[at + 8 :] = gain_part[:, LANES:]
    at = send.shape[0] - GAIN_ROWS
    send[at:] = low(jnp.concatenate([gain_part[:, :LANES], gain_part[:, LANES:]], axis=0))
    total = res_kept[...] + res_got[...].astype(F32)
    odd = lax.rem(lax.axis_index("ch"), 2) == 1
    res_own[...] = jnp.where(odd, total[:, LANES:], total[:, :LANES])
    res_sent[...] = low(jnp.where(odd, total[:, :LANES], total[:, LANES:]))


def normed_back_kernel(
    geo, xg, near, far, dn_gate, weights, valid, back, hidden, res_own, res_got, kept, sent, result
):
    tok, steps = geo.tok, geo.steps
    even = lax.rem(lax.axis_index("rows"), 2) == 0
    second = lax.axis_index("ch") >= 2
    row = iota((tok, LANES), 0)
    token = (row % CHUNKS) * steps + row // CHUNKS
    grads = []
    for strand in range(2):
        one, two = near[strand], far[strand]
        ahead = jnp.where(even, two, one)
        behind = jnp.where(even, one, two)
        total = xg[strand]
        for k in range(3):
            total = total + jnp.where(token == k, ahead[k : k + 1], 0.0)
            total = total + jnp.where(token == tok - 1 - k, behind[15 - k : 16 - k], 0.0)
        rounded = low(total * valid[...])
        grads.append(nt(low(nn(back[...], rounded)), weights[2 * strand]) + dn_gate[strand])
    kept[...] = jnp.where(second, grads[1], grads[0])
    sent[...] = low(jnp.where(second, grads[0], grads[1]))
    out = hidden[...].astype(F32) + res_own[...] + res_got[...].astype(F32)
    result[...] = low(out)


def finish_kernel(geo, one, two, xo, xc, gains, cot, input_grad):
    mine = lax.axis_index("ch")
    odd = lax.rem(mine, 2) == 1
    a, b = xo[...].astype(F32), xc[...].astype(F32)
    source = jnp.concatenate([jnp.where(odd, b, a), jnp.where(odd, a, b)], axis=1)
    inverse = lax.rsqrt(jnp.mean(source * source, axis=-1, keepdims=True) + EPSILON)
    unit = source * inverse
    here = jnp.where(mine >= 2, gains[1:], gains[:1])
    scaled = (one[...].astype(F32) + two[...].astype(F32)) * here
    back = inverse * (scaled - unit * jnp.mean(scaled * unit, axis=-1, keepdims=True))
    input_grad[...] = cot[...].astype(F32) + jnp.where(odd, back[:, LANES:], back[:, :LANES])


def unpack_kernel(e_parts, l_parts, gain_sum, in_g, out_g, sel_g, cw_g, cb_g, stw_g, stb_g, decay_g, skip_g, gain_g, e_pack, l_pack):
    mine = lax.rem(lax.axis_index("rows"), 2)
    for parts, pack in ((e_parts, e_pack), (l_parts, l_pack)):
        total = pack.shape[0]
        half = total // 2
        if len(parts) == 1:
            pack[...] = parts[0][:total].astype(F32)
        else:
            pack[pl.ds(pl.multiple_of(mine * half, 16), half)] = parts[0][:half].astype(F32)
            pack[pl.ds(pl.multiple_of((1 - mine) * half, 16), half)] = parts[1][:half].astype(F32)
    width = in_g.shape[1]
    in_g[0] = l_pack[:width]
    in_g[1] = e_pack[:width]
    out_g[:, :LANES] = e_pack[width : width + LANES]
    out_g[:, LANES:] = e_pack[width + LANES : width + 2 * LANES]
    amount = sel_g.shape[1]
    for course in range(2):
        sel_g[course] = l_pack[width + course * amount : width + (course + 1) * amount]
    at = width + 2 * amount
    taps = cw_g.shape[1]
    for course in range(2):
        cw_g[course] = l_pack[at + course * taps : at + (course + 1) * taps]
    cb_g[...] = l_pack[at + 2 * taps : at + 2 * taps + 2]
    at = width + 2 * LANES
    for course in range(2):
        stw_g[course] = e_pack[at + course * R : at + (course + 1) * R]
        decay_g[course] = e_pack[at + 2 * R + course * N : at + 2 * R + (course + 1) * N]
    at = at + 2 * R + 2 * N
    stb_g[...] = e_pack[at : at + 2]
    skip_g[...] = e_pack[at + 2 : at + 4]
    gain_g[:, :LANES] = gain_sum[:1].astype(F32)
    gain_g[:, LANES:] = gain_sum[8:9].astype(F32)


def swap(value, axis, distance):
    count = lax.axis_size(axis)
    return lax.ppermute(value, axis, [(i, i ^ distance) for i in range(count)])


def gather_channels(value):
    across = swap(value, "ch", 2)
    return value, swap(value, "ch", 1), across, swap(across, "ch", 1)


def partner_sum(value):
    joined = low(value.astype(F32) + swap(value, "ch", 2).astype(F32))
    return joined, swap(joined, "ch", 1)


def on_device(
    hidden_in, lengths, norm_gain, in_weight, conv_weight, conv_bias, select_weight,
    step_weight, step_bias, decay_log, skip_gain, out_weight, cotangent,
):
    tok = hidden_in.shape[0]
    rows = lax.axis_size("rows")
    geo = Geometry(tok, rows)
    steps = geo.steps
    width = in_weight.shape[1]
    gain = norm_gain[None, :]
    small_mesh = geo.members == 4 and rows == 8
    padded_rows = (steps + 2 * (conv_weight.shape[1] - 1)) * CHUNKS

    def kernel(f):
        return functools.partial(f, geo)

    def lifted(f, first, amount):
        def body(*refs):
            return f(*refs[:first], refs[first : first + amount], *refs[first + amount :])

        return body

    vm = pltpu.VMEM
    strands = ((2, tok, LANES), F32)
    strands_low = ((2, tok, LANES), BF16)
    members = ((4, tok, LANES), F32)
    members_low = ((4, tok, LANES), BF16)
    chunked = ((4, N * CHUNKS, LANES), F32)
    summary = ((4 * N + 8, LANES), F32)
    full = ((tok, width), F32)
    full_low = ((tok, width), BF16)

    x_parts = gather_channels(hidden_in)
    x_own, c_own, valid, edge, turn, mover, back, gains, weights, outs, select, table, spread, tiny, stw = run(
        kernel(prepare_kernel),
        [
            ((tok, LANES), BF16),
            ((tok, LANES), BF16),
            ((tok, LANES), F32),
            ((32, LANES), F32),
            ((width, width), BF16),
            ((tok, tok), BF16),
            ((tok, tok), BF16),
            ((2, width), F32),
            ((4, width, LANES), BF16),
            ((2, LANES, width), BF16),
            ((2, LANES, LANES), BF16),
            ((4, N, CHUNKS, LANES), F32),
            ((LANES, 2 * N * LANES), BF16),
            ((24 + 2 * N, LANES), F32),
            (step_weight.shape, BF16),
        ],
        lengths, hidden_in, cotangent, in_weight, out_weight, step_weight, gain, conv_weight, conv_bias,
        jnp.swapaxes(select_weight, 1, 2), step_bias, decay_log, skip_gain,
        anywhere=13,
        scratch=[
            pltpu.SMEM(lengths.shape, jnp.int32),
            vm(gain.shape, F32),
            vm(conv_weight.shape, F32),
            vm(conv_bias.shape, F32),
            vm((2, select_weight.shape[2], LANES), BF16),
            vm(step_bias.shape, F32),
            vm(decay_log.shape, F32),
            vm(skip_gain.shape, F32),
            pltpu.SemaphoreType.DMA((13,)),
        ],
        name="prepare", micros=2,
    )
    cot, x_across = lax.optimization_barrier((cotangent, x_parts[2]))
    x_parts = (x_own, x_parts[1], x_across, x_parts[3])
    c_parts = (c_own,) + gather_channels(cot)[1:]

    normed, inputs, gates, near, far = run(
        kernel(project_kernel),
        [((2, tok, width), BF16), strands_low, strands, ((16, 2 * width), BF16), ((16, 2 * width), BF16)],
        *x_parts, valid, turn, mover, gains, weights,
        scratch=[vm((4, tok, LANES), BF16)], name="project",
    )
    near = lax.ppermute(near, "rows", geo.near())
    far = lax.ppermute(far, "rows", geo.far())
    moved, gm, dys = run(
        kernel(cotangent_kernel),
        [((2, tok, width), BF16), strands, strands],
        *c_parts, gates, valid, turn, mover, outs,
        scratch=[vm((4, tok, LANES), BF16)], name="cotangents", micros=1,
    )
    padded, rims_normed, pre, act, message = run(
        kernel(conv_kernel),
        [((2, padded_rows, LANES), F32), ((2, 32, width), BF16), members, members_low, strands_low],
        inputs, near, far, edge, turn, gains, weights, select, tiny, dys,
        name="conv",
    )
    one, two = partner_sum(message)
    shapes = [members_low, members, members, members, chunked, chunked, chunked]
    shapes += [((4, tok, 2 * N * LANES), F32)]

    def summarise(*refs):
        if small_mesh:
            summary_kernel(geo, *refs)
        else:
            summary_kernel(geo, *refs[:17], None, None, *refs[17:])

    got = run(
        summarise, shapes + [summary, summary],
        one, two, act, dys, stw, tiny, table, spread, valid,
        scratch=[vm(summary[0], F32), vm(summary[0], F32)] if small_mesh else (), name="summary", micros=10,
    )
    proj, raw, step, drive, chunk_p, chunk_h, chunk_w, wide = got[:8]
    if small_mesh:
        slots = (
            lax.ppermute(got[8], "rows", geo.near()),
            lax.ppermute(got[9], "rows", geo.across()),
            lax.ppermute(got[9], "rows", geo.far()),
        )
        slot_scratch = vm((4,) + summary[0], F32)
    else:
        up, down = lax.all_gather(got[8], "rows"), lax.all_gather(got[9], "rows")
        place = lax.axis_index("rows")
        index = place - geo.local() + jnp.arange(geo.members)
        inside = jnp.clip(index, 0, rows - 1)
        slots = (jnp.where((index < place)[:, None, None], up[inside], down[inside]),)
        slot_scratch = vm((8, LANES), F32)
    mixed, dgate, dact, message, small = run(
        lifted(kernel(scan_kernel), 0, len(slots)),
        [strands_low, strands_low, members, ((2, LANES, tok), BF16), ((80, LANES), F32)],
        *slots, act, proj, raw, step, drive, chunk_p, chunk_h, chunk_w, wide, spread,
        dys, gm, gates, stw, tiny, table, valid,
        scratch=[
            slot_scratch,
            vm(chunked[0], F32),
            vm(chunked[0], F32),
            vm(((steps + 1) * N * CHUNKS, LANES), F32),
            vm((tok, 2 * N * LANES), BF16),
            vm(members[0], F32),
            vm(members[0], F32),
            vm(members[0], F32),
            vm((4, 64, tok), F32),
            vm((2, N * CHUNKS, LANES), F32),
        ],
        name="scan", micros=16,
    )
    one, two = partner_sum(message)
    e_half = E_ROWS // 2
    l_half = L_ROWS // 2 + GAIN_ROWS
    res_kept, res_sent, e_keep, e_send, g_gate, dn_gate = run(
        kernel(dense_kernel),
        [
            full,
            full_low,
            ((e_half if small_mesh else E_ROWS, LANES), F32),
            ((e_half, LANES), BF16),
            ((width, LANES), F32),
            ((2, tok, width), F32),
        ],
        mixed, outs, moved, dgate, normed, weights, back, small,
        scratch=[vm((E_ROWS, LANES), F32)], name="dense",
    )
    res_got = swap(res_sent, "ch", 2)
    if small_mesh:
        e_sum = low(e_keep + swap(e_send, "rows", 1).astype(F32))
    xg, near, far, l_keep, l_send, res_own, res_sent = run(
        kernel(conv_back_kernel),
        [
            strands,
            ((2, 16, LANES), F32),
            ((2, 16, LANES), F32),
            ((l_half if small_mesh else L_ROWS + GAIN_ROWS, LANES), F32),
            ((l_half, LANES), BF16),
            ((tok, LANES), F32),
            ((tok, LANES), BF16),
        ],
        one, two, act, dact, pre, padded, tiny, select, normed, rims_normed, gains, weights, g_gate, valid, edge,
        res_kept, res_got,
        scratch=[vm((padded_rows, LANES), F32), vm((L_ROWS, LANES), F32)],
        name="conv_back",
    )
    near = lax.ppermute(near, "rows", geo.near())
    if small_mesh:
        l_sum = low(l_keep + swap(l_send, "rows", 1).astype(F32))
        e_sum = low(e_sum.astype(F32) + swap(e_sum, "rows", 2).astype(F32))
    far = lax.ppermute(far, "rows", geo.far())
    res_got = swap(res_sent, "ch", 1)
    dn_kept, dn_sent, result = run(
        kernel(normed_back_kernel),
        [full, full_low, ((tok, LANES), BF16)],
        xg, near, far, dn_gate, weights, valid, back, x_own, res_own, res_got,
        name="normed_back",
    )
    dn_got = swap(dn_sent, "ch", 2)
    dn = low(dn_kept + dn_got.astype(F32))
    input_grad = run(
        kernel(finish_kernel), ((tok, LANES), F32),
        dn, swap(dn, "ch", 1), x_parts[0], x_parts[1], gains, c_own, name="finish",
    )
    if small_mesh:
        l_sum = low(l_sum.astype(F32) + swap(l_sum, "rows", 2).astype(F32))
        e_sum = low(e_sum.astype(F32) + swap(e_sum, "rows", 4).astype(F32))
        l_sum = low(l_sum.astype(F32) + swap(l_sum, "rows", 4).astype(F32))
        e_parts = (e_sum, swap(e_sum, "rows", 1))
        l_parts = (l_sum, swap(l_sum, "rows", 1))
        gain_part = l_sum[l_half - GAIN_ROWS :].astype(F32)
        gain_part = gain_part + swap(gain_part, "ch", 2)
        gain_part = gain_part + swap(gain_part, "ch", 1)
    else:
        e_parts = (lax.psum(e_keep, "rows"),)
        l_parts = (lax.psum(l_keep, "rows"),)
        gain_part = lax.psum(l_parts[0][L_ROWS:], "ch")

    def unpack(*refs):
        k = len(e_parts)
        unpack_kernel(refs[:k], refs[k : 2 * k], *refs[2 * k :])

    got = run(
        unpack,
        [
            (in_weight.shape, F32),
            (out_weight.shape, F32),
            (jnp.swapaxes(select_weight, 1, 2).shape, F32),
            (conv_weight.shape, F32),
            (conv_bias.shape, F32),
            (step_weight.shape, F32),
            (step_bias.shape, F32),
            (decay_log.shape, F32),
            (skip_gain.shape, F32),
            ((1, width), F32),
        ],
        *e_parts, *l_parts, gain_part,
        scratch=[vm((E_ROWS, LANES), F32), vm((L_ROWS, LANES), F32)], name="unpack",
    )
    in_g, out_g, sel_g, cw_g, cb_g, stw_g, stb_g, decay_g, skip_g, gain_g = got
    return (
        result, input_grad, gain_g[0], in_g, cw_g, cb_g, jnp.swapaxes(sel_g, 1, 2), stw_g, stb_g, decay_g, skip_g, out_g,
    )


def solution(mesh):
    lanes = P(None, None, "ch")
    pair = P(None, "ch")
    columns = P(None, "ch", None)
    tokens = P("rows", "ch")
    return jax.shard_map(
        on_device,
        mesh=mesh,
        in_specs=(
            tokens, P(), P(), lanes, lanes, pair, columns, lanes, pair, lanes, pair, P("ch", None), tokens,
        ),
        out_specs=(
            tokens, tokens, P(), lanes, lanes, pair, columns, lanes, pair, lanes, pair, P("ch", None),
        ),
        check_vma=False,
    )
```

time: 126 us -> 96.5 us (0.77)
  Pallas kernels: 55.7 us -> 37.4 us
  waiting for transfers between devices: 34.6 us -> 28.8 us
  local copies, waits for them, and re-layouts: 3.95 us -> 0 us
  starting transfers between devices: 30.6 us -> 29.1 us
    pallas_call x10 -> x11, Pallas kernels: 55.7 us -> 37.4 us  [run(): pl.pallas_call(kernel, out_shape=[jax.ShapeDtypeStruct(s, d) for s, d in...]
    ppermute x25 -> x24, waiting for transfers between devices: 27.6 us -> 21.5 us  [swap(): return lax.ppermute(value, axis, [(i, i ^ distance) for i in range(count)])]
    unnamed x32 -> x0, local copies, waits for them, and re-layouts: 3.95 us -> none
    ppermute x25 -> x24, starting transfers between devices: 23.8 us -> 22.7 us  [swap(): return lax.ppermute(value, axis, [(i, i ^ distance) for i in range(count)])]
  transfers between devices with their start and end apart: 32 -> 31, of which waited for: 20 -> 18; matrix products, arithmetic and copies ran while one was open for 0% -> 0% of each run, Pallas kernels for 4% -> 7%
where the time goes in v2:
time: 96.5 us; the launch traced here: 96.3 us
  Pallas kernels  37.4 us (39%)
  starting transfers between devices  29.1 us (30%)
  waiting for transfers between devices  28.8 us (30%)
    pallas_call x11, Pallas kernels, run(): pl.pallas_call(kernel, out_shape=[jax.ShapeDtypeStruct(s, d) for s, d in...  37.4 us
    ppermute x24, starting transfers between devices, swap(): return lax.ppermute(value, axis, [(i, i ^ distance) for i in range(count)])  22.7 us
    ppermute x24, waiting for transfers between devices, swap(): return lax.ppermute(value, axis, [(i, i ^ distance) for i in range(count)])  21.5 us
    ppermute x2, starting transfers between devices, on_device(): near = lax.ppermute(near, 'rows', geo.near())  3.13 us
    ppermute x2, waiting for transfers between devices, on_device(): far = lax.ppermute(far, 'rows', geo.far())  2.48 us
  transfers between devices with their start and end apart: 31, of which 18 were waited for; matrix products, arithmetic and copies ran while one was open for 0% of the time, Pallas kernels for 7%

profile of v2, /device:TPU:0, one launch (start us, length us, event | category | flops | bytes accessed | tf_op | source)
XLA Modules:
  0.0 96.3 jit_solution(1396436960903187443)
XLA Ops:
  0.6 3.1 %collective-permute-start.1 = (bf16[256,128]{1,0:T(8,128)(2,1)}, bf16[256,128]{1,0:T(8,128)(2,1)S(1)}, u32[]{:S(2)}, u32[]{:S(2)}) collective-permute-start(bf16[256,128]{1,0:T(8,128)(2,1)} %x_in.1), channel_id=1, source_target_pairs={{0,2},{1,3},{2,0},{3,1},{4,6},{5,7},{6,4},{7,5},{8,10},{9,11},{10,... | collective-permute-start | bytes 196616 | tf_op jit(solution)/shard_map/ppermute | solution.py:750
  3.7 2.5 %collective-permute-done.1.xy = bf16[256,128]{1,0:T(8,128)(2,1)S(1)} collective-permute-done((bf16[256,128]{1,0:T(8,128)(2,1)}, bf16[256,128]{1,0:T(8,128)(2,1)S(1)}, u32[]{:S(2)}, u32[]{:S(2)}) %collective-permute-start.1) | collective-permute-done | bytes 65568 | tf_op jit(solution)/shard_map/ppermute | solution.py:750
  6.2 2.0 %collective-permute-start.6 = (bf16[256,128]{1,0:T(8,128)(2,1)}, bf16[256,128]{1,0:T(8,128)(2,1)S(1)}, u32[]{:S(2)}, u32[]{:S(2)}) collective-permute-start(bf16[256,128]{1,0:T(8,128)(2,1)} %c_in.1), channel_id=1, source_target_pairs={{0,2},{1,3},{2,0},{3,1},{4,6},{5,7},{6,4},{7,5},{8,10},{9,11},{10,... | collective-permute-start | bytes 196616 | tf_op jit(solution)/shard_map/ppermute | solution.py:750
  8.2 0.5 collective-permute-start.2
  8.7 0.0 collective-permute-start.5
  8.7 1.9 %collective-permute-done.6.cy = bf16[256,128]{1,0:T(8,128)(2,1)S(1)} collective-permute-done((bf16[256,128]{1,0:T(8,128)(2,1)}, bf16[256,128]{1,0:T(8,128)(2,1)S(1)}, u32[]{:S(2)}, u32[]{:S(2)}) %collective-permute-start.6) | collective-permute-done | bytes 65568 | tf_op jit(solution)/shard_map/ppermute | solution.py:750
  10.6 0.0 collective-permute-start.7
  10.6 1.5 %prepare.1 = (bf16[256,128]{1,0:T(8,128)(2,1)S(1)}, bf16[256,128]{1,0:T(8,128)(2,1)S(1)}, f32[256,128]{1,0:T(8,128)S(1)}, f32[32,128]{1,0:T(8,128)S(1)}, bf16[25...) custom-call(s32[3]{0:T(128)} %lengths_in.1, ...), custom_call_target="tpu_custom_call" | custom-call | bytes 6000000 | tf_op jit(solution)/shard_map/prepare/pallas_call | solution.py:132
  12.1 0.0 collective-permute-done.xc
  12.1 0.0 collective-permute-done.2.xd
  12.2 0.7 project.1
  12.9 2.1 %collective-permute-start.3 = (bf16[16,512]{1,0:T(8,128)(2,1)S(1)}, bf16[16,512]{1,0:T(8,128)(2,1)S(1)}, u32[]{:S(2)}, u32[]{:S(2)}) collective-permute-start(bf16[16,512]{1,0:T(8,128)(2,1)S(1)} %get-tuple-element.91), channel_id=1, source_target_pairs={{0,4},{4,0},{8,12},{12,8},{16,20},{20,16},{24,28},{28,24},{1,5},{5... | collective-permute-start | bytes 49160 | tf_op jit(solution)/shard_map/ppermute | solution.py:841
  15.0 0.1 collective-permute-start.4
  15.0 0.0 collective-permute-done.5.cc
  15.0 0.6 cotangents.1
  15.6 1.1 %collective-permute-done.3.near = bf16[16,512]{1,0:T(8,128)(2,1)S(1)} collective-permute-done((bf16[16,512]{1,0:T(8,128)(2,1)S(1)}, bf16[16,512]{1,0:T(8,128)(2,1)S(1)}, u32[]{:S(2)}, u32[]{:S(2)}) %collective-permute-start.3) | collective-permute-done | bytes 16416 | tf_op jit(solution)/shard_map/ppermute | solution.py:841
  16.7 2.0 %collective-permute-done.4.far = bf16[16,512]{1,0:T(8,128)(2,1)S(1)} collective-permute-done((bf16[16,512]{1,0:T(8,128)(2,1)S(1)}, bf16[16,512]{1,0:T(8,128)(2,1)S(1)}, u32[]{:S(2)}, u32[]{:S(2)}) %collective-permute-start.4) | collective-permute-done | bytes 16416 | tf_op jit(solution)/shard_map/ppermute | solution.py:842
  18.7 0.8 conv.1
  19.5 1.6 %collective-permute-start.8 = (bf16[2,256,128]{2,1,0:T(8,128)(2,1)S(1)}, bf16[2,256,128]{2,1,0:T(8,128)(2,1)S(1)}, u32[]{:S(2)}, u32[]{:S(2)}) collective-permute-start(bf16[2,256,128]{2,1,0:T(8,128)(2,1)S(1)} %get-tuple-element.101), channel_id=1, source_target_pairs={{0,2},{1,3},{2,0},{3,1},{4,6},{5,7},{6,4},{7,5},{8,10},{9,11},{10,... | collective-permute-start | bytes 393224 | tf_op jit(solution)/shard_map/ppermute | solution.py:750
  21.1 3.4 %collective-permute-done.8 = bf16[2,256,128]{2,1,0:T(8,128)(2,1)S(1)} collective-permute-done((bf16[2,256,128]{2,1,0:T(8,128)(2,1)S(1)}, bf16[2,256,128]{2,1,0:T(8,128)(2,1)S(1)}, u32[]{:S(2)}, u32[]{:S(2)}) %collective-permute-start.8) | collective-permute-done | bytes 131104 | tf_op jit(solution)/shard_map/ppermute | solution.py:750
  24.6 0.1 collective-permute-start.9
  24.7 1.3 %collective-permute-done.9.refs_1_ = bf16[2,256,128]{2,1,0:T(8,128)(2,1)S(1)} collective-permute-done((bf16[2,256,128]{2,1,0:T(8,128)(2,1)S(1)}, bf16[2,256,128]{2,1,0:T(8,128)(2,1)S(1)}, u32[]{:S(2)}, u32[]{:S(2)}) %collective-permute-start.9) | collective-permute-done | bytes 131104 | tf_op jit(solution)/shard_map/ppermute | solution.py:750
  26.0 11.7 %summary.1 = (bf16[4,256,128]{2,1,0:T(8,128)(2,1)S(1)}, f32[4,256,128]{2,1,0:T(8,128)S(1)}, f32[4,256,128]{2,1,0:T(8,128)S(1)}, f32[4,256,128]{2,1,0:T(8,128)S(1...) custom-call(bf16[2,256,128]{2,1,0:T(8,128)(2,1)S(1)} %add_convert_fu, ...), custom_call_target="tpu_custom_call" | custom-call | bytes 30000000 | tf_op jit(solution)/shard_map/summary/pallas_call | solution.py:132
  37.7 0.2 collective-permute-start.10
  37.9 1.9 %collective-permute-start.12 = (f32[72,128]{1,0:T(8,128)S(1)}, f32[72,128]{1,0:T(8,128)S(1)}, u32[]{:S(2)}, u32[]{:S(2)}) collective-permute-start(f32[72,128]{1,0:T(8,128)S(1)} %get-tuple-element.107), channel_id=1, source_target_pairs={{0,4},{4,0},{8,20},{12,16},{16,12},{20,8},{24,28},{28,24},{1,5},{5... | collective-permute-start | bytes 110600 | tf_op jit(solution)/shard_map/ppermute | solution.py:875
  39.7 0.2 collective-permute-start.11
  39.9 1.8 %collective-permute-done.10.refs_0_ = f32[72,128]{1,0:T(8,128)S(1)} collective-permute-done((f32[72,128]{1,0:T(8,128)S(1)}, f32[72,128]{1,0:T(8,128)S(1)}, u32[]{:S(2)}, u32[]{:S(2)}) %collective-permute-start.10) | collective-permute-done | bytes 36896 | tf_op jit(solution)/shard_map/ppermute | solution.py:873
  41.7 0.5 collective-permute-done.12.refs_2_
  42.2 1.5 %collective-permute-done.11.refs_1_ = f32[72,128]{1,0:T(8,128)S(1)} collective-permute-done((f32[72,128]{1,0:T(8,128)S(1)}, f32[72,128]{1,0:T(8,128)S(1)}, u32[]{:S(2)}, u32[]{:S(2)}) %collective-permute-start.11) | collective-permute-done | bytes 36896 | tf_op jit(solution)/shard_map/ppermute | solution.py:874
  43.7 17.3 %scan.1 = (bf16[2,256,128]{2,1,0:T(8,128)(2,1)S(1)}, bf16[2,256,128]{2,1,0:T(8,128)(2,1)S(1)}, f32[4,256,128]{2,1,0:T(8,128)S(1)}, bf16[2,128,256]{2,1,0:T(8,128)(2,1)S(1)}, f32[80,128]{1,0:T(8,128)S(1)}) custom-call(f32[72,128]{1,0:T(8,128)S(1)} %collective-permute-done.10.refs_0_, f32[72,128]{1,0:T(8,128)S(1)} %collective-permute-done.11.refs_1_, ...), custom_call_target="tpu_custom_call" | custom-call | bytes 48000000 | tf_op jit(solution)/shard_map/scan/pallas_call | solution.py:132
  61.0 1.6 %collective-permute-start.13 = (bf16[2,128,256]{2,1,0:T(8,128)(2,1)S(1)}, bf16[2,128,256]{2,1,0:T(8,128)(2,1)S(1)}, u32[]{:S(2)}, u32[]{:S(2)}) collective-permute-start(bf16[2,128,256]{2,1,0:T(8,128)(2,1)S(1)} %get-tuple-element.117), channel_id=1, source_target_pairs={{0,2},{1,3},{2,0},{3,1},{4,6},{5,7},{6,4},{7,5},{8,10},{9,11},{10,... | collective-permute-start | bytes 393224 | tf_op jit(solution)/shard_map/ppermute | solution.py:750
  62.6 0.7 dense.1
  63.3 0.6 collective-permute-start.15
  63.9 3.5 %collective-permute-done.13 = bf16[2,128,256]{2,1,0:T(8,128)(2,1)S(1)} collective-permute-done((bf16[2,128,256]{2,1,0:T(8,128)(2,1)S(1)}, bf16[2,128,256]{2,1,0:T(8,128)(2,1)S(1)}, u32[]{:S(2)}, u32[]{:S(2)}) %collective-permute-start.13) | collective-permute-done | bytes 131104 | tf_op jit(solution)/shard_map/ppermute | solution.py:750
  67.4 0.1 collective-permute-start.14
  67.5 0.3 collective-permute-start.21
  67.8 1.0 %collective-permute-done.15.res_got = bf16[256,256]{1,0:T(8,128)(2,1)S(1)} collective-permute-done((bf16[256,256]{1,0:T(8,128)(2,1)S(1)}, bf16[256,256]{1,0:T(8,128)(2,1)S(1)}, u32[]{:S(2)}, u32[]{:S(2)}) %collective-permute-start.15) | collective-permute-done | bytes 131104 | tf_op jit(solution)/shard_map/ppermute | solution.py:750
  68.8 0.0 collective-permute-done.14.two
  68.8 1.2 %conv_back.1 = (f32[2,256,128]{2,1,0:T(8,128)S(1)}, f32[2,16,128]{2,1,0:T(8,128)S(1)}, f32[2,16,128]{2,1,0:T(8,128)S(1)}, f32[208,128]{1,0:T(8,128)S(1)}, bf16[2...) custom-call(bf16[2,128,256]{2,1,0:T(8,128)(2,1)S(1)} %add_convert_fusion.1.one, ...), custom_call_target="tpu_custom_call" | custom-call | bytes 3000000 | tf_op jit(solution)/shard_map/conv_back/pallas_call | solution.py:132
  70.0 0.8 collective-permute-start.25
  70.8 1.5 %collective-permute-done.21 = bf16[304,128]{1,0:T(8,128)(2,1)S(1)} collective-permute-done((bf16[304,128]{1,0:T(8,128)(2,1)S(1)}, bf16[304,128]{1,0:T(8,128)(2,1)S(1)}, u32[]{:S(2)}, u32[]{:S(2)}) %collective-permute-start.21) | collective-permute-done | bytes 77856 | tf_op jit(solution)/shard_map/ppermute | solution.py:750
  72.3 3.4 %collective-permute-start.22 = (bf16[304,128]{1,0:T(8,128)(2,1)S(1)}, bf16[304,128]{1,0:T(8,128)(2,1)S(1)}, u32[]{:S(2)}, u32[]{:S(2)}) collective-permute-start(bf16[304,128]{1,0:T(8,128)(2,1)S(1)} %add_convert_fusion.5), channel_id=1, source_target_pairs={{0,8},{4,12},{8,0},{12,4},{16,24},{20,28},{24,16},{28,20},{1,9},{5... | collective-permute-start | bytes 233480 | tf_op jit(solution)/shard_map/ppermute | solution.py:750
  75.7 0.0 collective-permute-done.25
  75.7 1.9 %collective-permute-start.26 = (bf16[208,128]{1,0:T(8,128)(2,1)S(1)}, bf16[208,128]{1,0:T(8,128)(2,1)S(1)}, u32[]{:S(2)}, u32[]{:S(2)}) collective-permute-start(bf16[208,128]{1,0:T(8,128)(2,1)S(1)} %add_convert_fusion.8), channel_id=1, source_target_pairs={{0,8},{4,12},{8,0},{12,4},{16,24},{20,28},{24,16},{28,20},{1,9},{5... | collective-permute-start | bytes 159752 | tf_op jit(solution)/shard_map/ppermute | solution.py:750
  77.6 0.9 collective-permute-done.22
  78.5 2.0 %collective-permute-start.23 = (bf16[304,128]{1,0:T(8,128)(2,1)S(1)}, bf16[304,128]{1,0:T(8,128)(2,1)S(1)}, u32[]{:S(2)}, u32[]{:S(2)}) collective-permute-start(bf16[304,128]{1,0:T(8,128)(2,1)S(1)} %add_convert_fusion.4), channel_id=1, source_target_pairs={{0,16},{4,20},{8,24},{12,28},{16,0},{20,4},{24,8},{28,12},{1,17},{... | collective-permute-start | bytes 233480 | tf_op jit(solution)/shard_map/ppermute | solution.py:750
  80.5 1.1 %collective-permute-start.16 = (f32[2,16,128]{2,1,0:T(8,128)S(1)}, f32[2,16,128]{2,1,0:T(8,128)S(1)}, u32[]{:S(2)}, u32[]{:S(2)}) collective-permute-start(f32[2,16,128]{2,1,0:T(8,128)S(1)} %get-tuple-element.132), channel_id=1, source_target_pairs={{0,4},{4,0},{8,12},{12,8},{16,20},{20,16},{24,28},{28,24},{1,5},{5... | collective-permute-start | bytes 49160 | tf_op jit(solution)/shard_map/ppermute | solution.py:939
  81.6 1.0 collective-permute-start.17
  82.6 2.0 %collective-permute-start.27 = (bf16[208,128]{1,0:T(8,128)(2,1)S(1)}, bf16[208,128]{1,0:T(8,128)(2,1)S(1)}, u32[]{:S(2)}, u32[]{:S(2)}) collective-permute-start(bf16[208,128]{1,0:T(8,128)(2,1)S(1)} %add_convert_fusion.7), channel_id=1, source_target_pairs={{0,16},{4,20},{8,24},{12,28},{16,0},{20,4},{24,8},{28,12},{1,17},{... | collective-permute-start | bytes 159752 | tf_op jit(solution)/shard_map/ppermute | solution.py:750
  84.6 0.2 collective-permute-start.24
  84.8 0.5 collective-permute-done.17.far
  85.3 0.0 collective-permute-done.18.res_got
  85.3 1.1 %normed_back.1 = (f32[256,256]{1,0:T(8,128)S(1)}, bf16[256,256]{1,0:T(8,128)(2,1)S(1)}, bf16[256,128]{1,0:T(8,128)(2,1)}) custom-call(f32[2,256,128]{2,1,0:T(8,128)S(1)} %get-tuple-element.131.xg, f32[2,16,128]{2,1,0:T(8,128)S(1)} %collective-permute-done.16.near, f32[2,16,128]{2,1,0:T(8,128)S(1)} %collective-permute-done.17.far, ...), custom_call_target="tpu_custom_call" | custom-call | bytes 3000000 | tf_op jit(solution)/shard_map/normed_back/pallas_call | solution.py:132
  86.4 0.9 collective-permute-start.19
  87.3 1.6 %collective-permute-done.27 = bf16[208,128]{1,0:T(8,128)(2,1)S(1)} collective-permute-done((bf16[208,128]{1,0:T(8,128)(2,1)S(1)}, bf16[208,128]{1,0:T(8,128)(2,1)S(1)}, u32[]{:S(2)}, u32[]{:S(2)}) %collective-permute-start.27) | collective-permute-done | bytes 53280 | tf_op jit(solution)/shard_map/ppermute | solution.py:750
  88.9 0.8 collective-permute-start.28
  89.8 0.9 collective-permute-start.29
  90.6 0.8 collective-permute-done.19
  91.5 0.1 collective-permute-start.20
  91.6 1.9 %collective-permute-done.29 = f32[16,128]{1,0:T(8,128)S(1)} collective-permute-done((f32[16,128]{1,0:T(8,128)S(1)}, f32[16,128]{1,0:T(8,128)S(1)}, u32[]{:S(2)}, u32[]{:S(2)}) %collective-permute-start.29) | collective-permute-done | bytes 8224 | tf_op jit(solution)/shard_map/ppermute | solution.py:750
  93.4 0.0 collective-permute-start.30
  93.4 1.2 %collective-permute-done.30 = f32[16,128]{1,0:T(8,128)S(1)} collective-permute-done((f32[16,128]{1,0:T(8,128)S(1)}, f32[16,128]{1,0:T(8,128)S(1)}, u32[]{:S(2)}, u32[]{:S(2)}) %collective-permute-start.30) | collective-permute-done | bytes 8224 | tf_op jit(solution)/shard_map/ppermute | solution.py:750
  94.6 0.8 unpack.1
  95.5 0.9 finish.1
  (21 shorter events, 0.3 us)
Async XLA Ops:
  0.6 5.5 %collective-permute-start.1 = (bf16[256,128]{1,0:T(8,128)(2,1)}, bf16[256,128]{1,0:T(8,128)(2,1)S(1)}, u32[]{:S(2)}, u32[]{:S(2)}) collective-permute-start(bf16[256,128]{1,0:T(8,128)(2,1)} %x_in.1), channel_id=1, source_target_pairs={{0,2},{1,3},{2,0},{3,1},{4,6},{5,7},{6,4},{7,5},{8,10},{9,11},{10,... | collective-permute-start | bytes 196616 | tf_op jit(solution)/shard_map/ppermute | solution.py:750
  6.2 4.5 %collective-permute-start.6 = (bf16[256,128]{1,0:T(8,128)(2,1)}, bf16[256,128]{1,0:T(8,128)(2,1)S(1)}, u32[]{:S(2)}, u32[]{:S(2)}) collective-permute-start(bf16[256,128]{1,0:T(8,128)(2,1)} %c_in.1), channel_id=1, source_target_pairs={{0,2},{1,3},{2,0},{3,1},{4,6},{5,7},{6,4},{7,5},{8,10},{9,11},{10,... | collective-permute-start | bytes 196616 | tf_op jit(solution)/shard_map/ppermute | solution.py:750
  8.2 4.0 %collective-permute-start = (bf16[256,128]{1,0:T(8,128)(2,1)}, bf16[256,128]{1,0:T(8,128)(2,1)S(1)}, u32[]{:S(2)}, u32[]{:S(2)}) collective-permute-start(bf16[256,128]{1,0:T(8,128)(2,1)} %x_in.1), channel_id=1, source_target_pairs={{0,1},{1,0},{2,3},{3,2},{4,5},{5,4},{6,7},{7,6},{8,9},{9,8},{10,11... | collective-permute-start | bytes 196616 | tf_op jit(solution)/shard_map/ppermute | solution.py:750
  8.2 4.0 %collective-permute-start.2 = (bf16[256,128]{1,0:T(8,128)(2,1)S(1)}, bf16[256,128]{1,0:T(8,128)(2,1)S(1)}, u32[]{:S(2)}, u32[]{:S(2)}) collective-permute-start(bf16[256,128]{1,0:T(8,128)(2,1)S(1)} %collective-permute-done.1.xy), channel_id=1, source_target_pairs={{0,1},{1,0},{2,3},{3,2},{4,5},{5,4},{6,7},{7,6},{8,9},{9,8},{10,11... | collective-permute-start | bytes 196616 | tf_op jit(solution)/shard_map/ppermute | solution.py:750
  8.7 6.3 %collective-permute-start.5 = (bf16[256,128]{1,0:T(8,128)(2,1)}, bf16[256,128]{1,0:T(8,128)(2,1)S(1)}, u32[]{:S(2)}, u32[]{:S(2)}) collective-permute-start(bf16[256,128]{1,0:T(8,128)(2,1)} %c_in.1), channel_id=1, source_target_pairs={{0,1},{1,0},{2,3},{3,2},{4,5},{5,4},{6,7},{7,6},{8,9},{9,8},{10,11... | collective-permute-start | bytes 196616 | tf_op jit(solution)/shard_map/ppermute | solution.py:750
  10.6 4.4 %collective-permute-start.7 = (bf16[256,128]{1,0:T(8,128)(2,1)S(1)}, bf16[256,128]{1,0:T(8,128)(2,1)S(1)}, u32[]{:S(2)}, u32[]{:S(2)}) collective-permute-start(bf16[256,128]{1,0:T(8,128)(2,1)S(1)} %collective-permute-done.6.cy), channel_id=1, source_target_pairs={{0,1},{1,0},{2,3},{3,2},{4,5},{5,4},{6,7},{7,6},{8,9},{9,8},{10,11... | collective-permute-start | bytes 196616 | tf_op jit(solution)/shard_map/ppermute | solution.py:750
  12.9 3.8 %collective-permute-start.3 = (bf16[16,512]{1,0:T(8,128)(2,1)S(1)}, bf16[16,512]{1,0:T(8,128)(2,1)S(1)}, u32[]{:S(2)}, u32[]{:S(2)}) collective-permute-start(bf16[16,512]{1,0:T(8,128)(2,1)S(1)} %get-tuple-element.91), channel_id=1, source_target_pairs={{0,4},{4,0},{8,12},{12,8},{16,20},{20,16},{24,28},{28,24},{1,5},{5... | collective-permute-start | bytes 49160 | tf_op jit(solution)/shard_map/ppermute | solution.py:841
  15.0 3.7 %collective-permute-start.4 = (bf16[16,512]{1,0:T(8,128)(2,1)S(1)}, bf16[16,512]{1,0:T(8,128)(2,1)S(1)}, u32[]{:S(2)}, u32[]{:S(2)}) collective-permute-start(bf16[16,512]{1,0:T(8,128)(2,1)S(1)} %get-tuple-element.92), channel_id=1, source_target_pairs={{0,4},{4,0},{8,20},{12,16},{16,12},{20,8},{24,28},{28,24},{1,5},{5... | collective-permute-start | bytes 49160 | tf_op jit(solution)/shard_map/ppermute | solution.py:842
  19.5 5.0 %collective-permute-start.8 = (bf16[2,256,128]{2,1,0:T(8,128)(2,1)S(1)}, bf16[2,256,128]{2,1,0:T(8,128)(2,1)S(1)}, u32[]{:S(2)}, u32[]{:S(2)}) collective-permute-start(bf16[2,256,128]{2,1,0:T(8,128)(2,1)S(1)} %get-tuple-element.101), channel_id=1, source_target_pairs={{0,2},{1,3},{2,0},{3,1},{4,6},{5,7},{6,4},{7,5},{8,10},{9,11},{10,... | collective-permute-start | bytes 393224 | tf_op jit(solution)/shard_map/ppermute | solution.py:750
  24.6 1.4 %collective-permute-start.9 = (bf16[2,256,128]{2,1,0:T(8,128)(2,1)S(1)}, bf16[2,256,128]{2,1,0:T(8,128)(2,1)S(1)}, u32[]{:S(2)}, u32[]{:S(2)}) collective-permute-start(bf16[2,256,128]{2,1,0:T(8,128)(2,1)S(1)} %add_convert_fusion.2.refs_0_), channel_id=1, source_target_pairs={{0,1},{1,0},{2,3},{3,2},{4,5},{5,4},{6,7},{7,6},{8,9},{9,8},{10,11... | collective-permute-start | bytes 393224 | tf_op jit(solution)/shard_map/ppermute | solution.py:750
  37.7 4.0 %collective-permute-start.10 = (f32[72,128]{1,0:T(8,128)S(1)}, f32[72,128]{1,0:T(8,128)S(1)}, u32[]{:S(2)}, u32[]{:S(2)}) collective-permute-start(f32[72,128]{1,0:T(8,128)S(1)} %get-tuple-element.106), channel_id=1, source_target_pairs={{0,4},{4,0},{8,12},{12,8},{16,20},{20,16},{24,28},{28,24},{1,5},{5... | collective-permute-start | bytes 110600 | tf_op jit(solution)/shard_map/ppermute | solution.py:873
  37.9 4.3 %collective-permute-start.12 = (f32[72,128]{1,0:T(8,128)S(1)}, f32[72,128]{1,0:T(8,128)S(1)}, u32[]{:S(2)}, u32[]{:S(2)}) collective-permute-start(f32[72,128]{1,0:T(8,128)S(1)} %get-tuple-element.107), channel_id=1, source_target_pairs={{0,4},{4,0},{8,20},{12,16},{16,12},{20,8},{24,28},{28,24},{1,5},{5... | collective-permute-start | bytes 110600 | tf_op jit(solution)/shard_map/ppermute | solution.py:875
  39.7 4.0 %collective-permute-start.11 = (f32[72,128]{1,0:T(8,128)S(1)}, f32[72,128]{1,0:T(8,128)S(1)}, u32[]{:S(2)}, u32[]{:S(2)}) collective-permute-start(f32[72,128]{1,0:T(8,128)S(1)} %get-tuple-element.107), channel_id=1, source_target_pairs={{0,4},{4,0},{8,16},{12,20},{16,8},{20,12},{24,28},{28,24},{1,5},{5... | collective-permute-start | bytes 110600 | tf_op jit(solution)/shard_map/ppermute | solution.py:874
  61.0 6.4 %collective-permute-start.13 = (bf16[2,128,256]{2,1,0:T(8,128)(2,1)S(1)}, bf16[2,128,256]{2,1,0:T(8,128)(2,1)S(1)}, u32[]{:S(2)}, u32[]{:S(2)}) collective-permute-start(bf16[2,128,256]{2,1,0:T(8,128)(2,1)S(1)} %get-tuple-element.117), channel_id=1, source_target_pairs={{0,2},{1,3},{2,0},{3,1},{4,6},{5,7},{6,4},{7,5},{8,10},{9,11},{10,... | collective-permute-start | bytes 393224 | tf_op jit(solution)/shard_map/ppermute | solution.py:750
  63.3 5.5 %collective-permute-start.15 = (bf16[256,256]{1,0:T(8,128)(2,1)S(1)}, bf16[256,256]{1,0:T(8,128)(2,1)S(1)}, u32[]{:S(2)}, u32[]{:S(2)}) collective-permute-start(bf16[256,256]{1,0:T(8,128)(2,1)S(1)} %get-tuple-element.130), channel_id=1, source_target_pairs={{0,2},{1,3},{2,0},{3,1},{4,6},{5,7},{6,4},{7,5},{8,10},{9,11},{10,... | collective-permute-start | bytes 393224 | tf_op jit(solution)/shard_map/ppermute | solution.py:750
  67.4 1.4 %collective-permute-start.14 = (bf16[2,128,256]{2,1,0:T(8,128)(2,1)S(1)}, bf16[2,128,256]{2,1,0:T(8,128)(2,1)S(1)}, u32[]{:S(2)}, u32[]{:S(2)}) collective-permute-start(bf16[2,128,256]{2,1,0:T(8,128)(2,1)S(1)} %add_convert_fusion.1.one), channel_id=1, source_target_pairs={{0,1},{1,0},{2,3},{3,2},{4,5},{5,4},{6,7},{7,6},{8,9},{9,8},{10,11... | collective-permute-start | bytes 393224 | tf_op jit(solution)/shard_map/ppermute | solution.py:750
  67.5 4.8 %collective-permute-start.21 = (bf16[304,128]{1,0:T(8,128)(2,1)S(1)}, bf16[304,128]{1,0:T(8,128)(2,1)S(1)}, u32[]{:S(2)}, u32[]{:S(2)}) collective-permute-start(bf16[304,128]{1,0:T(8,128)(2,1)S(1)} %get-tuple-element.141), channel_id=1, source_target_pairs={{0,4},{4,0},{8,12},{12,8},{16,20},{20,16},{24,28},{28,24},{1,5},{5... | collective-permute-start | bytes 233480 | tf_op jit(solution)/shard_map/ppermute | solution.py:750
  70.0 5.6 %collective-permute-start.25 = (bf16[208,128]{1,0:T(8,128)(2,1)S(1)}, bf16[208,128]{1,0:T(8,128)(2,1)S(1)}, u32[]{:S(2)}, u32[]{:S(2)}) collective-permute-start(bf16[208,128]{1,0:T(8,128)(2,1)S(1)} %get-tuple-element.143), channel_id=1, source_target_pairs={{0,4},{4,0},{8,12},{12,8},{16,20},{20,16},{24,28},{28,24},{1,5},{5... | collective-permute-start | bytes 159752 | tf_op jit(solution)/shard_map/ppermute | solution.py:750
  72.3 6.1 %collective-permute-start.22 = (bf16[304,128]{1,0:T(8,128)(2,1)S(1)}, bf16[304,128]{1,0:T(8,128)(2,1)S(1)}, u32[]{:S(2)}, u32[]{:S(2)}) collective-permute-start(bf16[304,128]{1,0:T(8,128)(2,1)S(1)} %add_convert_fusion.5), channel_id=1, source_target_pairs={{0,8},{4,12},{8,0},{12,4},{16,24},{20,28},{24,16},{28,20},{1,9},{5... | collective-permute-start | bytes 233480 | tf_op jit(solution)/shard_map/ppermute | solution.py:750
  75.7 6.8 %collective-permute-start.26 = (bf16[208,128]{1,0:T(8,128)(2,1)S(1)}, bf16[208,128]{1,0:T(8,128)(2,1)S(1)}, u32[]{:S(2)}, u32[]{:S(2)}) collective-permute-start(bf16[208,128]{1,0:T(8,128)(2,1)S(1)} %add_convert_fusion.8), channel_id=1, source_target_pairs={{0,8},{4,12},{8,0},{12,4},{16,24},{20,28},{24,16},{28,20},{1,9},{5... | collective-permute-start | bytes 159752 | tf_op jit(solution)/shard_map/ppermute | solution.py:750
  78.5 6.1 %collective-permute-start.23 = (bf16[304,128]{1,0:T(8,128)(2,1)S(1)}, bf16[304,128]{1,0:T(8,128)(2,1)S(1)}, u32[]{:S(2)}, u32[]{:S(2)}) collective-permute-start(bf16[304,128]{1,0:T(8,128)(2,1)S(1)} %add_convert_fusion.4), channel_id=1, source_target_pairs={{0,16},{4,20},{8,24},{12,28},{16,0},{20,4},{24,8},{28,12},{1,17},{... | collective-permute-start | bytes 233480 | tf_op jit(solution)/shard_map/ppermute | solution.py:750
  80.5 4.3 %collective-permute-start.16 = (f32[2,16,128]{2,1,0:T(8,128)S(1)}, f32[2,16,128]{2,1,0:T(8,128)S(1)}, u32[]{:S(2)}, u32[]{:S(2)}) collective-permute-start(f32[2,16,128]{2,1,0:T(8,128)S(1)} %get-tuple-element.132), channel_id=1, source_target_pairs={{0,4},{4,0},{8,12},{12,8},{16,20},{20,16},{24,28},{28,24},{1,5},{5... | collective-permute-start | bytes 49160 | tf_op jit(solution)/shard_map/ppermute | solution.py:939
  81.6 3.7 %collective-permute-start.17 = (f32[2,16,128]{2,1,0:T(8,128)S(1)}, f32[2,16,128]{2,1,0:T(8,128)S(1)}, u32[]{:S(2)}, u32[]{:S(2)}) collective-permute-start(f32[2,16,128]{2,1,0:T(8,128)S(1)} %get-tuple-element.133), channel_id=1, source_target_pairs={{0,4},{4,0},{8,20},{12,16},{16,12},{20,8},{24,28},{28,24},{1,5},{5... | collective-permute-start | bytes 49160 | tf_op jit(solution)/shard_map/ppermute | solution.py:943
  82.5 2.8 %collective-permute-start.18 = (bf16[256,128]{1,0:T(8,128)(2,1)S(1)}, bf16[256,128]{1,0:T(8,128)(2,1)S(1)}, u32[]{:S(2)}, u32[]{:S(2)}) collective-permute-start(bf16[256,128]{1,0:T(8,128)(2,1)S(1)} %get-tuple-element.136), channel_id=1, source_target_pairs={{0,1},{1,0},{2,3},{3,2},{4,5},{5,4},{6,7},{7,6},{8,9},{9,8},{10,11... | collective-permute-start | bytes 196616 | tf_op jit(solution)/shard_map/ppermute | solution.py:750
  82.6 6.3 %collective-permute-start.27 = (bf16[208,128]{1,0:T(8,128)(2,1)S(1)}, bf16[208,128]{1,0:T(8,128)(2,1)S(1)}, u32[]{:S(2)}, u32[]{:S(2)}) collective-permute-start(bf16[208,128]{1,0:T(8,128)(2,1)S(1)} %add_convert_fusion.7), channel_id=1, source_target_pairs={{0,16},{4,20},{8,24},{12,28},{16,0},{20,4},{24,8},{28,12},{1,17},{... | collective-permute-start | bytes 159752 | tf_op jit(solution)/shard_map/ppermute | solution.py:750
  84.6 10.0 %collective-permute-start.24 = (bf16[304,128]{1,0:T(8,128)(2,1)S(1)}, bf16[304,128]{1,0:T(8,128)(2,1)S(1)}, u32[]{:S(2)}, u32[]{:S(2)}) collective-permute-start(bf16[304,128]{1,0:T(8,128)(2,1)S(1)} %add_convert_fusion.3.refs_0_), channel_id=1, source_target_pairs={{0,4},{4,0},{8,12},{12,8},{16,20},{20,16},{24,28},{28,24},{1,5},{5... | collective-permute-start | bytes 233480 | tf_op jit(solution)/shard_map/ppermute | solution.py:750
  86.4 5.0 %collective-permute-start.19 = (bf16[256,256]{1,0:T(8,128)(2,1)S(1)}, bf16[256,256]{1,0:T(8,128)(2,1)S(1)}, u32[]{:S(2)}, u32[]{:S(2)}) collective-permute-start(bf16[256,256]{1,0:T(8,128)(2,1)S(1)} %get-tuple-element.139), channel_id=1, source_target_pairs={{0,2},{1,3},{2,0},{3,1},{4,6},{5,7},{6,4},{7,5},{8,10},{9,11},{10,... | collective-permute-start | bytes 393224 | tf_op jit(solution)/shard_map/ppermute | solution.py:750
  88.9 5.7 %collective-permute-start.28 = (bf16[208,128]{1,0:T(8,128)(2,1)S(1)}, bf16[208,128]{1,0:T(8,128)(2,1)S(1)}, u32[]{:S(2)}, u32[]{:S(2)}) collective-permute-start(bf16[208,128]{1,0:T(8,128)(2,1)S(1)} %add_convert_fusion.6.refs_2_), channel_id=1, source_target_pairs={{0,4},{4,0},{8,12},{12,8},{16,20},{20,16},{24,28},{28,24},{1,5},{5... | collective-permute-start | bytes 159752 | tf_op jit(solution)/shard_map/ppermute | solution.py:750
  89.8 3.7 %collective-permute-start.29 = (f32[16,128]{1,0:T(8,128)S(1)}, f32[16,128]{1,0:T(8,128)S(1)}, u32[]{:S(2)}, u32[]{:S(2)}) collective-permute-start(f32[16,128]{1,0:T(8,128)S(1)} %slice_convert_fusion), channel_id=1, source_target_pairs={{0,2},{1,3},{2,0},{3,1},{4,6},{5,7},{6,4},{7,5},{8,10},{9,11},{10,... | collective-permute-start | bytes 24584 | tf_op jit(solution)/shard_map/ppermute | solution.py:750
  91.5 4.0 %collective-permute-start.20 = (bf16[256,256]{1,0:T(8,128)(2,1)S(1)}, bf16[256,256]{1,0:T(8,128)(2,1)S(1)}, u32[]{:S(2)}, u32[]{:S(2)}) collective-permute-start(bf16[256,256]{1,0:T(8,128)(2,1)S(1)} %add_convert_fusion.one), channel_id=1, source_target_pairs={{0,1},{1,0},{2,3},{3,2},{4,5},{5,4},{6,7},{7,6},{8,9},{9,8},{10,11... | collective-permute-start | bytes 393224 | tf_op jit(solution)/shard_map/ppermute | solution.py:750
  93.4 1.2 %collective-permute-start.30 = (f32[16,128]{1,0:T(8,128)S(1)}, f32[16,128]{1,0:T(8,128)S(1)}, u32[]{:S(2)}, u32[]{:S(2)}) collective-permute-start(f32[16,128]{1,0:T(8,128)S(1)} %fusion), channel_id=1, source_target_pairs={{0,1},{1,0},{2,3},{3,2},{4,5},{5,4},{6,7},{7,6},{8,9},{9,8},{10,11... | collective-permute-start | bytes 24584 | tf_op jit(solution)/shard_map/ppermute | solution.py:750

commit v3 on v2

--- a/solution.py
+++ b/solution.py
@@ -6,6 +6,7 @@
 from jax.experimental import pallas as pl
 from jax.experimental.pallas import tpu as pltpu
 from jax.sharding import PartitionSpec as P
+
 
 N = 16
 R = 16
@@ -125,20 +126,20 @@
         return out
 
 
-def run(kernel, outs, *args, anywhere=0, scratch=(), name=None, micros=1):
+def run(kernel, outs, *args, anywhere=0, scratch=(), micros=1, limit=8):
     single = isinstance(outs, tuple)
     shapes = [outs] if single else list(outs)
     args = [pltpu.with_memory_space_constraint(a, pltpu.HBM) for a in args[:anywhere]] + list(args[anywhere:])
-    got = pl.pallas_call(
+    call = pl.pallas_call(
         kernel,
         out_shape=[jax.ShapeDtypeStruct(s, d) for s, d in shapes],
         in_specs=[pl.BlockSpec(memory_space=pltpu.HBM)] * anywhere + [VM] * (len(args) - anywhere),
         out_specs=[VM] * len(shapes),
         scratch_shapes=list(scratch),
-        name=name,
-        compiler_params=pltpu.CompilerParams(vmem_limit_bytes=48 * 1024 * 1024),
+        compiler_params=pltpu.CompilerParams(vmem_limit_bytes=limit * 1024 * 1024),
         cost_estimate=pl.CostEstimate(flops=0, bytes_accessed=int(micros * 3.0e6), transcendentals=0),
-    )(*args)
+    )
+    got = call(*args)
     return got[0] if single else got
 
 
@@ -233,7 +234,6 @@
 
 
 def cotangent_kernel(geo, co, cc, cy, cd, gates, valid, turn, mover, outs, moved, gm, dys, scratch):
-    tok = geo.tok
     sides = assemble((co, cc, cy, cd), scratch)
     for strand in range(2):
         side = sides[strand]
@@ -322,7 +322,7 @@
     geo, one, two, act, dys, stw, tiny, table, spread, valid,
     proj, raw, step, drive, chunk_p, chunk_h, chunk_w, wide, near, far, up, down,
 ):
-    tok, steps = geo.tok, geo.steps
+    steps = geo.steps
     for strand in range(2):
         total = one[strand].astype(F32) + two[strand].astype(F32)
         for course in range(2):
@@ -340,6 +340,7 @@
             raw[member] = step_raw
             step[member] = step_row
             drive[member] = step_row * act[member].astype(F32)
+
     def sweep(member, flipped):
         strand, course = member // 2, lax.rem(member, 2)
         for base in range(0, N, 8):
@@ -826,17 +827,16 @@
             vm(skip_gain.shape, F32),
             pltpu.SemaphoreType.DMA((13,)),
         ],
-        name="prepare", micros=2,
-    )
-    cot, x_across = lax.optimization_barrier((cotangent, x_parts[2]))
-    x_parts = (x_own, x_parts[1], x_across, x_parts[3])
-    c_parts = (c_own,) + gather_channels(cot)[1:]
+        micros=2,
+    )
+    x_parts = (x_own,) + x_parts[1:]
+    c_parts = (c_own,) + gather_channels(cotangent)[1:]
 
     normed, inputs, gates, near, far = run(
         kernel(project_kernel),
         [((2, tok, width), BF16), strands_low, strands, ((16, 2 * width), BF16), ((16, 2 * width), BF16)],
         *x_parts, valid, turn, mover, gains, weights,
-        scratch=[vm((4, tok, LANES), BF16)], name="project",
+        scratch=[vm((4, tok, LANES), BF16)],
     )
     near = lax.ppermute(near, "rows", geo.near())
     far = lax.ppermute(far, "rows", geo.far())
@@ -844,13 +844,12 @@
         kernel(cotangent_kernel),
         [((2, tok, width), BF16), strands, strands],
         *c_parts, gates, valid, turn, mover, outs,
-        scratch=[vm((4, tok, LANES), BF16)], name="cotangents", micros=1,
+        scratch=[vm((4, tok, LANES), BF16)], micros=1,
     )
     padded, rims_normed, pre, act, message = run(
         kernel(conv_kernel),
         [((2, padded_rows, LANES), F32), ((2, 32, width), BF16), members, members_low, strands_low],
         inputs, near, far, edge, turn, gains, weights, select, tiny, dys,
-        name="conv",
     )
     one, two = partner_sum(message)
     shapes = [members_low, members, members, members, chunked, chunked, chunked]
@@ -865,7 +864,7 @@
     got = run(
         summarise, shapes + [summary, summary],
         one, two, act, dys, stw, tiny, table, spread, valid,
-        scratch=[vm(summary[0], F32), vm(summary[0], F32)] if small_mesh else (), name="summary", micros=10,
+        scratch=[vm(summary[0], F32), vm(summary[0], F32)] if small_mesh else (), micros=10,
     )
     proj, raw, step, drive, chunk_p, chunk_h, chunk_w, wide = got[:8]
     if small_mesh:
@@ -899,7 +898,7 @@
             vm((4, 64, tok), F32),
             vm((2, N * CHUNKS, LANES), F32),
         ],
-        name="scan", micros=16,
+        micros=16, limit=14,
     )
     one, two = partner_sum(message)
     e_half = E_ROWS // 2
@@ -915,7 +914,7 @@
             ((2, tok, width), F32),
         ],
         mixed, outs, moved, dgate, normed, weights, back, small,
-        scratch=[vm((E_ROWS, LANES), F32)], name="dense",
+        scratch=[vm((E_ROWS, LANES), F32)],
     )
     res_got = swap(res_sent, "ch", 2)
     if small_mesh:
@@ -934,7 +933,6 @@
         one, two, act, dact, pre, padded, tiny, select, normed, rims_normed, gains, weights, g_gate, valid, edge,
         res_kept, res_got,
         scratch=[vm((padded_rows, LANES), F32), vm((L_ROWS, LANES), F32)],
-        name="conv_back",
     )
     near = lax.ppermute(near, "rows", geo.near())
     if small_mesh:
@@ -946,13 +944,12 @@
         kernel(normed_back_kernel),
         [full, full_low, ((tok, LANES), BF16)],
         xg, near, far, dn_gate, weights, valid, back, x_own, res_own, res_got,
-        name="normed_back",
     )
     dn_got = swap(dn_sent, "ch", 2)
     dn = low(dn_kept + dn_got.astype(F32))
     input_grad = run(
         kernel(finish_kernel), ((tok, LANES), F32),
-        dn, swap(dn, "ch", 1), x_parts[0], x_parts[1], gains, c_own, name="finish",
+        dn, swap(dn, "ch", 1), x_parts[0], x_parts[1], gains, c_own,
     )
     if small_mesh:
         l_sum = low(l_sum.astype(F32) + swap(l_sum, "rows", 2).astype(F32))
@@ -987,7 +984,7 @@
             ((1, width), F32),
         ],
         *e_parts, *l_parts, gain_part,
-        scratch=[vm((E_ROWS, LANES), F32), vm((L_ROWS, LANES), F32)], name="unpack",
+        scratch=[vm((E_ROWS, LANES), F32), vm((L_ROWS, LANES), F32)],
     )
     in_g, out_g, sel_g, cw_g, cb_g, stw_g, stb_g, decay_g, skip_g, gain_g = got
     return (

time: 96.5 us -> 81.7 us (0.85)
  Pallas kernels: 37.4 us -> 26 us
  starting transfers between devices: 29.1 us -> 27.3 us
  waiting for transfers between devices: 28.8 us -> 27.1 us
    pallas_call x11, Pallas kernels: 37.4 us -> 26 us  [run(): got = call(*args)]
    ppermute x24, starting transfers between devices: 22.7 us -> 20.6 us  [swap(): return lax.ppermute(value, axis, [(i, i ^ distance) for i in range(count)])]
  transfers between devices with their start and end apart: 31 -> 31, of which waited for: 18 -> 18; matrix products, arithmetic and copies ran while one was open for 0% -> 0% of each run, Pallas kernels for 7% -> 8%
where the time goes in v3:
time: 81.7 us; the launch traced here: 81.5 us
  starting transfers between devices  27.3 us (33%)
  waiting for transfers between devices  27.1 us (33%)
  Pallas kernels  26 us (32%)
    pallas_call x11, Pallas kernels, run(): got = call(*args)  26 us
    ppermute x24, waiting for transfers between devices, swap(): return lax.ppermute(value, axis, [(i, i ^ distance) for i in range(count)])  20.7 us
    ppermute x24, starting transfers between devices, swap(): return lax.ppermute(value, axis, [(i, i ^ distance) for i in range(count)])  20.6 us
    ppermute x2, starting transfers between devices, on_device(): near = lax.ppermute(near, 'rows', geo.near())  2.62 us
    ppermute x2, waiting for transfers between devices, on_device(): far = lax.ppermute(far, 'rows', geo.far())  1.95 us
  transfers between devices with their start and end apart: 31, of which 18 were waited for; matrix products, arithmetic and copies ran while one was open for 0% of the time, Pallas kernels for 8%

profile of v3, /device:TPU:0, one launch (start us, length us, event | category | flops | bytes accessed | tf_op | source)
XLA Modules:
  0.0 81.5 jit_solution(9182396502882467816)
XLA Ops:
  0.6 3.1 %collective-permute-start.1 = (bf16[256,128]{1,0:T(8,128)(2,1)}, bf16[256,128]{1,0:T(8,128)(2,1)S(1)}, u32[]{:S(2)}, u32[]{:S(2)}) collective-permute-start(bf16[256,128]{1,0:T(8,128)(2,1)} %x_in.1), channel_id=1, source_target_pairs={{0,2},{1,3},{2,0},{3,1},{4,6},{5,7},{6,4},{7,5},{8,10},{9,11},{10,... | collective-permute-start | bytes 196616 | tf_op jit(solution)/shard_map/ppermute | solution.py:751
  3.7 0.1 collective-permute-start.6
  3.8 0.0 collective-permute-start
  3.8 2.5 %collective-permute-done.1.xy = bf16[256,128]{1,0:T(8,128)(2,1)S(1)} collective-permute-done((bf16[256,128]{1,0:T(8,128)(2,1)}, bf16[256,128]{1,0:T(8,128)(2,1)S(1)}, u32[]{:S(2)}, u32[]{:S(2)}) %collective-permute-start.1) | collective-permute-done | bytes 65568 | tf_op jit(solution)/shard_map/ppermute | solution.py:751
  6.3 0.0 collective-permute-start.2
  6.3 0.5 collective-permute-start.5
  6.8 1.4 %collective-permute-done.6.cy = bf16[256,128]{1,0:T(8,128)(2,1)S(1)} collective-permute-done((bf16[256,128]{1,0:T(8,128)(2,1)}, bf16[256,128]{1,0:T(8,128)(2,1)S(1)}, u32[]{:S(2)}, u32[]{:S(2)}) %collective-permute-start.6) | collective-permute-done | bytes 65568 | tf_op jit(solution)/shard_map/ppermute | solution.py:751
  8.2 0.0 collective-permute-start.7
  8.2 1.5 %shard_map.220 = (bf16[256,128]{1,0:T(8,128)(2,1)S(1)}, bf16[256,128]{1,0:T(8,128)(2,1)S(1)}, f32[256,128]{1,0:T(8,128)S(1)}, f32[32,128]{1,0:T(8,128)S(1)}, bf1...) custom-call(s32[3]{0:T(128)} %lengths_in.1, ...), custom_call_target="tpu_custom_call" | custom-call | bytes 6000000 | tf_op jit(solution)/shard_map/pallas_call | solution.py:142
  9.7 0.0 collective-permute-done.xc
  9.7 0.7 shard_map.221
  10.4 1.6 %collective-permute-start.3 = (bf16[16,512]{1,0:T(8,128)(2,1)S(1)}, bf16[16,512]{1,0:T(8,128)(2,1)S(1)}, u32[]{:S(2)}, u32[]{:S(2)}) collective-permute-start(bf16[16,512]{1,0:T(8,128)(2,1)S(1)} %get-tuple-element.88), channel_id=1, source_target_pairs={{0,4},{4,0},{8,12},{12,8},{16,20},{20,16},{24,28},{28,24},{1,5},{5... | collective-permute-start | bytes 49160 | tf_op jit(solution)/shard_map/ppermute | solution.py:841
  12.0 0.5 collective-permute-start.4
  12.5 0.0 collective-permute-done.5.cc
  12.5 0.0 collective-permute-done.7.cd
  12.5 0.6 shard_map.222
  13.1 1.1 %collective-permute-done.3.near = bf16[16,512]{1,0:T(8,128)(2,1)S(1)} collective-permute-done((bf16[16,512]{1,0:T(8,128)(2,1)S(1)}, bf16[16,512]{1,0:T(8,128)(2,1)S(1)}, u32[]{:S(2)}, u32[]{:S(2)}) %collective-permute-start.3) | collective-permute-done | bytes 16416 | tf_op jit(solution)/shard_map/ppermute | solution.py:841
  14.3 1.5 %collective-permute-done.4.far = bf16[16,512]{1,0:T(8,128)(2,1)S(1)} collective-permute-done((bf16[16,512]{1,0:T(8,128)(2,1)S(1)}, bf16[16,512]{1,0:T(8,128)(2,1)S(1)}, u32[]{:S(2)}, u32[]{:S(2)}) %collective-permute-start.4) | collective-permute-done | bytes 16416 | tf_op jit(solution)/shard_map/ppermute | solution.py:842
  15.7 0.8 %shard_map.223 = (f32[2,304,128]{2,1,0:T(8,128)S(1)}, bf16[2,32,256]{2,1,0:T(8,128)(2,1)S(1)}, f32[4,256,128]{2,1,0:T(8,128)S(1)}, bf16[4,256,128]{2,1,0:T(8,128)(2,1)S(1)}, bf16[2,256,128]{2,1,0:T(8,128)(2,1)S(1)}) custom-call(bf16[2,256,128]{2,1,0:T(8,128)(2,1)S(1)} %get-tuple-element.87.inputs, bf16[16,512]{1,0:T(8,128)(2,1)S(1)} %collective-permute-done.3.near, ...), custom_call_target="tpu_custom_call" | custom-call | bytes 3000000 | tf_op jit(solution)/shard_map/pallas_call | solution.py:142
  16.6 1.0 %collective-permute-start.8 = (bf16[2,256,128]{2,1,0:T(8,128)(2,1)S(1)}, bf16[2,256,128]{2,1,0:T(8,128)(2,1)S(1)}, u32[]{:S(2)}, u32[]{:S(2)}) collective-permute-start(bf16[2,256,128]{2,1,0:T(8,128)(2,1)S(1)} %get-tuple-element.97), channel_id=1, source_target_pairs={{0,2},{1,3},{2,0},{3,1},{4,6},{5,7},{6,4},{7,5},{8,10},{9,11},{10,... | collective-permute-start | bytes 393224 | tf_op jit(solution)/shard_map/ppermute | solution.py:751
  17.6 4.0 %collective-permute-done.8 = bf16[2,256,128]{2,1,0:T(8,128)(2,1)S(1)} collective-permute-done((bf16[2,256,128]{2,1,0:T(8,128)(2,1)S(1)}, bf16[2,256,128]{2,1,0:T(8,128)(2,1)S(1)}, u32[]{:S(2)}, u32[]{:S(2)}) %collective-permute-start.8) | collective-permute-done | bytes 131104 | tf_op jit(solution)/shard_map/ppermute | solution.py:751
  21.7 0.1 collective-permute-start.9
  21.7 1.3 %collective-permute-done.9.refs_1_ = bf16[2,256,128]{2,1,0:T(8,128)(2,1)S(1)} collective-permute-done((bf16[2,256,128]{2,1,0:T(8,128)(2,1)S(1)}, bf16[2,256,128]{2,1,0:T(8,128)(2,1)S(1)}, u32[]{:S(2)}, u32[]{:S(2)}) %collective-permute-start.9) | collective-permute-done | bytes 131104 | tf_op jit(solution)/shard_map/ppermute | solution.py:751
  23.1 6.0 %shard_map.224 = (bf16[4,256,128]{2,1,0:T(8,128)(2,1)S(1)}, f32[4,256,128]{2,1,0:T(8,128)S(1)}, f32[4,256,128]{2,1,0:T(8,128)S(1)}, f32[4,256,128]{2,1,0:T(8,128...) custom-call(bf16[2,256,128]{2,1,0:T(8,128)(2,1)S(1)} %add_convert_fu, ...), custom_call_target="tpu_custom_call" | custom-call | bytes 30000000 | tf_op jit(solution)/shard_map/pallas_call | solution.py:142
  29.1 0.6 collective-permute-start.10
  29.7 1.5 %collective-permute-start.12 = (f32[72,128]{1,0:T(8,128)S(1)}, f32[72,128]{1,0:T(8,128)S(1)}, u32[]{:S(2)}, u32[]{:S(2)}) collective-permute-start(f32[72,128]{1,0:T(8,128)S(1)} %get-tuple-element.103), channel_id=1, source_target_pairs={{0,4},{4,0},{8,20},{12,16},{16,12},{20,8},{24,28},{28,24},{1,5},{5... | collective-permute-start | bytes 110600 | tf_op jit(solution)/shard_map/ppermute | solution.py:874
  31.2 0.5 collective-permute-start.11
  31.7 1.4 %collective-permute-done.10.refs_0_ = f32[72,128]{1,0:T(8,128)S(1)} collective-permute-done((f32[72,128]{1,0:T(8,128)S(1)}, f32[72,128]{1,0:T(8,128)S(1)}, u32[]{:S(2)}, u32[]{:S(2)}) %collective-permute-start.10) | collective-permute-done | bytes 36896 | tf_op jit(solution)/shard_map/ppermute | solution.py:872
  33.1 0.8 collective-permute-done.12.refs_2_
  33.9 1.2 %collective-permute-done.11.refs_1_ = f32[72,128]{1,0:T(8,128)S(1)} collective-permute-done((f32[72,128]{1,0:T(8,128)S(1)}, f32[72,128]{1,0:T(8,128)S(1)}, u32[]{:S(2)}, u32[]{:S(2)}) %collective-permute-start.11) | collective-permute-done | bytes 36896 | tf_op jit(solution)/shard_map/ppermute | solution.py:873
  35.2 11.5 %shard_map.225 = (bf16[2,256,128]{2,1,0:T(8,128)(2,1)S(1)}, bf16[2,256,128]{2,1,0:T(8,128)(2,1)S(1)}, f32[4,256,128]{2,1,0:T(8,128)S(1)}, bf16[2,128,256]{2,1,0:T(8,128)(2,1)S(1)}, f32[80,128]{1,0:T(8,128)S(1)}) custom-call(f32[72,128]{1,0:T(8,128)S(1)} %collective-permute-done.10.refs_0_, f32[72,128]{1,0:T(8,128)S(1)} %collective-permute-done.11.refs_1_, ...), custom_call_target="tpu_custom_call" | custom-call | bytes 48000000 | tf_op jit(solution)/shard_map/pallas_call | solution.py:142
  46.7 1.0 %collective-permute-start.13 = (bf16[2,128,256]{2,1,0:T(8,128)(2,1)S(1)}, bf16[2,128,256]{2,1,0:T(8,128)(2,1)S(1)}, u32[]{:S(2)}, u32[]{:S(2)}) collective-permute-start(bf16[2,128,256]{2,1,0:T(8,128)(2,1)S(1)} %get-tuple-element.113), channel_id=1, source_target_pairs={{0,2},{1,3},{2,0},{3,1},{4,6},{5,7},{6,4},{7,5},{8,10},{9,11},{10,... | collective-permute-start | bytes 393224 | tf_op jit(solution)/shard_map/ppermute | solution.py:751
  47.7 0.7 shard_map.226
  48.5 1.1 %collective-permute-start.15 = (bf16[256,256]{1,0:T(8,128)(2,1)S(1)}, bf16[256,256]{1,0:T(8,128)(2,1)S(1)}, u32[]{:S(2)}, u32[]{:S(2)}) collective-permute-start(bf16[256,256]{1,0:T(8,128)(2,1)S(1)} %get-tuple-element.126), channel_id=1, source_target_pairs={{0,2},{1,3},{2,0},{3,1},{4,6},{5,7},{6,4},{7,5},{8,10},{9,11},{10,... | collective-permute-start | bytes 393224 | tf_op jit(solution)/shard_map/ppermute | solution.py:751
  49.6 3.0 %collective-permute-done.13 = bf16[2,128,256]{2,1,0:T(8,128)(2,1)S(1)} collective-permute-done((bf16[2,128,256]{2,1,0:T(8,128)(2,1)S(1)}, bf16[2,128,256]{2,1,0:T(8,128)(2,1)S(1)}, u32[]{:S(2)}, u32[]{:S(2)}) %collective-permute-start.13) | collective-permute-done | bytes 131104 | tf_op jit(solution)/shard_map/ppermute | solution.py:751
  52.6 0.1 collective-permute-start.14
  52.7 0.3 collective-permute-start.21
  53.0 1.0 %collective-permute-done.15.res_got = bf16[256,256]{1,0:T(8,128)(2,1)S(1)} collective-permute-done((bf16[256,256]{1,0:T(8,128)(2,1)S(1)}, bf16[256,256]{1,0:T(8,128)(2,1)S(1)}, u32[]{:S(2)}, u32[]{:S(2)}) %collective-permute-start.15) | collective-permute-done | bytes 131104 | tf_op jit(solution)/shard_map/ppermute | solution.py:751
  54.0 0.0 collective-permute-done.14.two
  54.0 1.2 %shard_map.227 = (f32[2,256,128]{2,1,0:T(8,128)S(1)}, f32[2,16,128]{2,1,0:T(8,128)S(1)}, f32[2,16,128]{2,1,0:T(8,128)S(1)}, f32[208,128]{1,0:T(8,128)S(1)}, bf16...) custom-call(bf16[2,128,256]{2,1,0:T(8,128)(2,1)S(1)} %add_convert_fusion.1.one, ...), custom_call_target="tpu_custom_call" | custom-call | bytes 3000000 | tf_op jit(solution)/shard_map/pallas_call | solution.py:142
  55.2 0.8 collective-permute-start.25
  56.0 1.5 %collective-permute-done.21 = bf16[304,128]{1,0:T(8,128)(2,1)S(1)} collective-permute-done((bf16[304,128]{1,0:T(8,128)(2,1)S(1)}, bf16[304,128]{1,0:T(8,128)(2,1)S(1)}, u32[]{:S(2)}, u32[]{:S(2)}) %collective-permute-start.21) | collective-permute-done | bytes 77856 | tf_op jit(solution)/shard_map/ppermute | solution.py:751
  57.5 3.4 %collective-permute-start.22 = (bf16[304,128]{1,0:T(8,128)(2,1)S(1)}, bf16[304,128]{1,0:T(8,128)(2,1)S(1)}, u32[]{:S(2)}, u32[]{:S(2)}) collective-permute-start(bf16[304,128]{1,0:T(8,128)(2,1)S(1)} %add_convert_fusion.5), channel_id=1, source_target_pairs={{0,8},{4,12},{8,0},{12,4},{16,24},{20,28},{24,16},{28,20},{1,9},{5... | collective-permute-start | bytes 233480 | tf_op jit(solution)/shard_map/ppermute | solution.py:751
  60.8 0.0 collective-permute-done.25
  60.9 1.9 %collective-permute-start.26 = (bf16[208,128]{1,0:T(8,128)(2,1)S(1)}, bf16[208,128]{1,0:T(8,128)(2,1)S(1)}, u32[]{:S(2)}, u32[]{:S(2)}) collective-permute-start(bf16[208,128]{1,0:T(8,128)(2,1)S(1)} %add_convert_fusion.8), channel_id=1, source_target_pairs={{0,8},{4,12},{8,0},{12,4},{16,24},{20,28},{24,16},{28,20},{1,9},{5... | collective-permute-start | bytes 159752 | tf_op jit(solution)/shard_map/ppermute | solution.py:751
  62.7 0.9 %collective-permute-done.22 = bf16[304,128]{1,0:T(8,128)(2,1)S(1)} collective-permute-done((bf16[304,128]{1,0:T(8,128)(2,1)S(1)}, bf16[304,128]{1,0:T(8,128)(2,1)S(1)}, u32[]{:S(2)}, u32[]{:S(2)}) %collective-permute-start.22) | collective-permute-done | bytes 77856 | tf_op jit(solution)/shard_map/ppermute | solution.py:751
  63.7 2.0 %collective-permute-start.23 = (bf16[304,128]{1,0:T(8,128)(2,1)S(1)}, bf16[304,128]{1,0:T(8,128)(2,1)S(1)}, u32[]{:S(2)}, u32[]{:S(2)}) collective-permute-start(bf16[304,128]{1,0:T(8,128)(2,1)S(1)} %add_convert_fusion.4), channel_id=1, source_target_pairs={{0,16},{4,20},{8,24},{12,28},{16,0},{20,4},{24,8},{28,12},{1,17},{... | collective-permute-start | bytes 233480 | tf_op jit(solution)/shard_map/ppermute | solution.py:751
  65.7 1.1 %collective-permute-start.16 = (f32[2,16,128]{2,1,0:T(8,128)S(1)}, f32[2,16,128]{2,1,0:T(8,128)S(1)}, u32[]{:S(2)}, u32[]{:S(2)}) collective-permute-start(f32[2,16,128]{2,1,0:T(8,128)S(1)} %get-tuple-element.128), channel_id=1, source_target_pairs={{0,4},{4,0},{8,12},{12,8},{16,20},{20,16},{24,28},{28,24},{1,5},{5... | collective-permute-start | bytes 49160 | tf_op jit(solution)/shard_map/ppermute | solution.py:937
  66.7 1.0 %collective-permute-start.17 = (f32[2,16,128]{2,1,0:T(8,128)S(1)}, f32[2,16,128]{2,1,0:T(8,128)S(1)}, u32[]{:S(2)}, u32[]{:S(2)}) collective-permute-start(f32[2,16,128]{2,1,0:T(8,128)S(1)} %get-tuple-element.129), channel_id=1, source_target_pairs={{0,4},{4,0},{8,20},{12,16},{16,12},{20,8},{24,28},{28,24},{1,5},{5... | collective-permute-start | bytes 49160 | tf_op jit(solution)/shard_map/ppermute | solution.py:941
  67.7 2.0 %collective-permute-start.27 = (bf16[208,128]{1,0:T(8,128)(2,1)S(1)}, bf16[208,128]{1,0:T(8,128)(2,1)S(1)}, u32[]{:S(2)}, u32[]{:S(2)}) collective-permute-start(bf16[208,128]{1,0:T(8,128)(2,1)S(1)} %add_convert_fusion.7), channel_id=1, source_target_pairs={{0,16},{4,20},{8,24},{12,28},{16,0},{20,4},{24,8},{28,12},{1,17},{... | collective-permute-start | bytes 159752 | tf_op jit(solution)/shard_map/ppermute | solution.py:751
  69.8 0.3 collective-permute-start.24
  70.0 0.5 collective-permute-done.17.far
  70.5 1.1 %shard_map.228 = (f32[256,256]{1,0:T(8,128)S(1)}, bf16[256,256]{1,0:T(8,128)(2,1)S(1)}, bf16[256,128]{1,0:T(8,128)(2,1)}) custom-call(f32[2,256,128]{2,1,0:T(8,128)S(1)} %get-tuple-element.127.xg, f32[2,16,128]{2,1,0:T(8,128)S(1)} %collective-permute-done.16.near, f32[2,16,128]{2,1,0:T(8,128)S(1)} %collective-permute-done.17.far, ...), custom_call_target="tpu_custom_call" | custom-call | bytes 3000000 | tf_op jit(solution)/shard_map/pallas_call | solution.py:142
  71.6 1.1 %collective-permute-start.19 = (bf16[256,256]{1,0:T(8,128)(2,1)S(1)}, bf16[256,256]{1,0:T(8,128)(2,1)S(1)}, u32[]{:S(2)}, u32[]{:S(2)}) collective-permute-start(bf16[256,256]{1,0:T(8,128)(2,1)S(1)} %get-tuple-element.135), channel_id=1, source_target_pairs={{0,2},{1,3},{2,0},{3,1},{4,6},{5,7},{6,4},{7,5},{8,10},{9,11},{10,... | collective-permute-start | bytes 393224 | tf_op jit(solution)/shard_map/ppermute | solution.py:751
  72.7 1.4 %collective-permute-done.27 = bf16[208,128]{1,0:T(8,128)(2,1)S(1)} collective-permute-done((bf16[208,128]{1,0:T(8,128)(2,1)S(1)}, bf16[208,128]{1,0:T(8,128)(2,1)S(1)}, u32[]{:S(2)}, u32[]{:S(2)}) %collective-permute-start.27) | collective-permute-done | bytes 53280 | tf_op jit(solution)/shard_map/ppermute | solution.py:751
  74.1 0.8 %collective-permute-start.28 = (bf16[208,128]{1,0:T(8,128)(2,1)S(1)}, bf16[208,128]{1,0:T(8,128)(2,1)S(1)}, u32[]{:S(2)}, u32[]{:S(2)}) collective-permute-start(bf16[208,128]{1,0:T(8,128)(2,1)S(1)} %add_convert_fusion.6.refs_2_), channel_id=1, source_target_pairs={{0,4},{4,0},{8,12},{12,8},{16,20},{20,16},{24,28},{28,24},{1,5},{5... | collective-permute-start | bytes 159752 | tf_op jit(solution)/shard_map/ppermute | solution.py:751
  74.9 1.1 %collective-permute-start.29 = (f32[16,128]{1,0:T(8,128)S(1)}, f32[16,128]{1,0:T(8,128)S(1)}, u32[]{:S(2)}, u32[]{:S(2)}) collective-permute-start(f32[16,128]{1,0:T(8,128)S(1)} %slice_convert_fusion), channel_id=1, source_target_pairs={{0,2},{1,3},{2,0},{3,1},{4,6},{5,7},{6,4},{7,5},{8,10},{9,11},{10,... | collective-permute-start | bytes 24584 | tf_op jit(solution)/shard_map/ppermute | solution.py:751
  76.0 0.6 collective-permute-done.19
  76.7 0.1 collective-permute-start.20
  76.7 1.9 %collective-permute-done.29 = f32[16,128]{1,0:T(8,128)S(1)} collective-permute-done((f32[16,128]{1,0:T(8,128)S(1)}, f32[16,128]{1,0:T(8,128)S(1)}, u32[]{:S(2)}, u32[]{:S(2)}) %collective-permute-start.29) | collective-permute-done | bytes 8224 | tf_op jit(solution)/shard_map/ppermute | solution.py:751
  78.6 1.2 %collective-permute-done.30 = f32[16,128]{1,0:T(8,128)S(1)} collective-permute-done((f32[16,128]{1,0:T(8,128)S(1)}, f32[16,128]{1,0:T(8,128)S(1)}, u32[]{:S(2)}, u32[]{:S(2)}) %collective-permute-start.30) | collective-permute-done | bytes 8224 | tf_op jit(solution)/shard_map/ppermute | solution.py:751
  79.8 0.8 %shard_map.230 = (f32[2,256,128]{2,1,0:T(8,128)}, f32[128,256]{1,0:T(8,128)}, f32[2,48,128]{2,1,0:T(8,128)}, f32[2,4,128]{2,1,0:T(4,128)}, f32[2,128]{1,0:T(2,12...) custom-call(bf16[304,128]{1,0:T(8,128)(2,1)S(1)} %add_convert_fusion, ...), custom_call_target="tpu_custom_call" | custom-call | bytes 3000000 | tf_op jit(solution)/shard_map/pallas_call | solution.py:142
  80.6 0.0 collective-permute-done.20.two
  80.6 0.9 %shard_map.229 = f32[256,128]{1,0:T(8,128)} custom-call(bf16[256,256]{1,0:T(8,128)(2,1)S(1)} %add_convert_fusion.one, bf16[256,256]{1,0:T(8,128)(2,1)S(1)} %collective-permute-done.20.two, bf16[256,128]{1,0:T(8,128)(2,1)S(1)} %get-tuple-element.81.xo.hidden, bf16[256,128]{1,0:T(8,128)(2,1)S(1)} %collective-permute-done.xc, ...), custom_call_target="tpu_custom_call" | custom-call | bytes 3000000 | tf_op jit(solution)/shard_map/pallas_call | solution.py:142
  (21 shorter events, 0.3 us)
Async XLA Ops:
  0.6 5.6 %collective-permute-start.1 = (bf16[256,128]{1,0:T(8,128)(2,1)}, bf16[256,128]{1,0:T(8,128)(2,1)S(1)}, u32[]{:S(2)}, u32[]{:S(2)}) collective-permute-start(bf16[256,128]{1,0:T(8,128)(2,1)} %x_in.1), channel_id=1, source_target_pairs={{0,2},{1,3},{2,0},{3,1},{4,6},{5,7},{6,4},{7,5},{8,10},{9,11},{10,... | collective-permute-start | bytes 196616 | tf_op jit(solution)/shard_map/ppermute | solution.py:751
  3.7 4.5 %collective-permute-start.6 = (bf16[256,128]{1,0:T(8,128)(2,1)}, bf16[256,128]{1,0:T(8,128)(2,1)S(1)}, u32[]{:S(2)}, u32[]{:S(2)}) collective-permute-start(bf16[256,128]{1,0:T(8,128)(2,1)} %c_in.1), channel_id=1, source_target_pairs={{0,2},{1,3},{2,0},{3,1},{4,6},{5,7},{6,4},{7,5},{8,10},{9,11},{10,... | collective-permute-start | bytes 196616 | tf_op jit(solution)/shard_map/ppermute | solution.py:751
  3.8 5.9 %collective-permute-start = (bf16[256,128]{1,0:T(8,128)(2,1)}, bf16[256,128]{1,0:T(8,128)(2,1)S(1)}, u32[]{:S(2)}, u32[]{:S(2)}) collective-permute-start(bf16[256,128]{1,0:T(8,128)(2,1)} %x_in.1), channel_id=1, source_target_pairs={{0,1},{1,0},{2,3},{3,2},{4,5},{5,4},{6,7},{7,6},{8,9},{9,8},{10,11... | collective-permute-start | bytes 196616 | tf_op jit(solution)/shard_map/ppermute | solution.py:751
  6.3 3.4 %collective-permute-start.2 = (bf16[256,128]{1,0:T(8,128)(2,1)S(1)}, bf16[256,128]{1,0:T(8,128)(2,1)S(1)}, u32[]{:S(2)}, u32[]{:S(2)}) collective-permute-start(bf16[256,128]{1,0:T(8,128)(2,1)S(1)} %collective-permute-done.1.xy), channel_id=1, source_target_pairs={{0,1},{1,0},{2,3},{3,2},{4,5},{5,4},{6,7},{7,6},{8,9},{9,8},{10,11... | collective-permute-start | bytes 196616 | tf_op jit(solution)/shard_map/ppermute | solution.py:751
  6.3 6.3 %collective-permute-start.5 = (bf16[256,128]{1,0:T(8,128)(2,1)}, bf16[256,128]{1,0:T(8,128)(2,1)S(1)}, u32[]{:S(2)}, u32[]{:S(2)}) collective-permute-start(bf16[256,128]{1,0:T(8,128)(2,1)} %c_in.1), channel_id=1, source_target_pairs={{0,1},{1,0},{2,3},{3,2},{4,5},{5,4},{6,7},{7,6},{8,9},{9,8},{10,11... | collective-permute-start | bytes 196616 | tf_op jit(solution)/shard_map/ppermute | solution.py:751
  8.2 4.4 %collective-permute-start.7 = (bf16[256,128]{1,0:T(8,128)(2,1)S(1)}, bf16[256,128]{1,0:T(8,128)(2,1)S(1)}, u32[]{:S(2)}, u32[]{:S(2)}) collective-permute-start(bf16[256,128]{1,0:T(8,128)(2,1)S(1)} %collective-permute-done.6.cy), channel_id=1, source_target_pairs={{0,1},{1,0},{2,3},{3,2},{4,5},{5,4},{6,7},{7,6},{8,9},{9,8},{10,11... | collective-permute-start | bytes 196616 | tf_op jit(solution)/shard_map/ppermute | solution.py:751
  10.4 3.8 %collective-permute-start.3 = (bf16[16,512]{1,0:T(8,128)(2,1)S(1)}, bf16[16,512]{1,0:T(8,128)(2,1)S(1)}, u32[]{:S(2)}, u32[]{:S(2)}) collective-permute-start(bf16[16,512]{1,0:T(8,128)(2,1)S(1)} %get-tuple-element.88), channel_id=1, source_target_pairs={{0,4},{4,0},{8,12},{12,8},{16,20},{20,16},{24,28},{28,24},{1,5},{5... | collective-permute-start | bytes 49160 | tf_op jit(solution)/shard_map/ppermute | solution.py:841
  12.0 3.7 %collective-permute-start.4 = (bf16[16,512]{1,0:T(8,128)(2,1)S(1)}, bf16[16,512]{1,0:T(8,128)(2,1)S(1)}, u32[]{:S(2)}, u32[]{:S(2)}) collective-permute-start(bf16[16,512]{1,0:T(8,128)(2,1)S(1)} %get-tuple-element.89), channel_id=1, source_target_pairs={{0,4},{4,0},{8,20},{12,16},{16,12},{20,8},{24,28},{28,24},{1,5},{5... | collective-permute-start | bytes 49160 | tf_op jit(solution)/shard_map/ppermute | solution.py:842
  16.6 5.0 %collective-permute-start.8 = (bf16[2,256,128]{2,1,0:T(8,128)(2,1)S(1)}, bf16[2,256,128]{2,1,0:T(8,128)(2,1)S(1)}, u32[]{:S(2)}, u32[]{:S(2)}) collective-permute-start(bf16[2,256,128]{2,1,0:T(8,128)(2,1)S(1)} %get-tuple-element.97), channel_id=1, source_target_pairs={{0,2},{1,3},{2,0},{3,1},{4,6},{5,7},{6,4},{7,5},{8,10},{9,11},{10,... | collective-permute-start | bytes 393224 | tf_op jit(solution)/shard_map/ppermute | solution.py:751
  21.7 1.4 %collective-permute-start.9 = (bf16[2,256,128]{2,1,0:T(8,128)(2,1)S(1)}, bf16[2,256,128]{2,1,0:T(8,128)(2,1)S(1)}, u32[]{:S(2)}, u32[]{:S(2)}) collective-permute-start(bf16[2,256,128]{2,1,0:T(8,128)(2,1)S(1)} %add_convert_fusion.2.refs_0_), channel_id=1, source_target_pairs={{0,1},{1,0},{2,3},{3,2},{4,5},{5,4},{6,7},{7,6},{8,9},{9,8},{10,11... | collective-permute-start | bytes 393224 | tf_op jit(solution)/shard_map/ppermute | solution.py:751
  29.1 4.0 %collective-permute-start.10 = (f32[72,128]{1,0:T(8,128)S(1)}, f32[72,128]{1,0:T(8,128)S(1)}, u32[]{:S(2)}, u32[]{:S(2)}) collective-permute-start(f32[72,128]{1,0:T(8,128)S(1)} %get-tuple-element.102), channel_id=1, source_target_pairs={{0,4},{4,0},{8,12},{12,8},{16,20},{20,16},{24,28},{28,24},{1,5},{5... | collective-permute-start | bytes 110600 | tf_op jit(solution)/shard_map/ppermute | solution.py:872
  29.7 4.2 %collective-permute-start.12 = (f32[72,128]{1,0:T(8,128)S(1)}, f32[72,128]{1,0:T(8,128)S(1)}, u32[]{:S(2)}, u32[]{:S(2)}) collective-permute-start(f32[72,128]{1,0:T(8,128)S(1)} %get-tuple-element.103), channel_id=1, source_target_pairs={{0,4},{4,0},{8,20},{12,16},{16,12},{20,8},{24,28},{28,24},{1,5},{5... | collective-permute-start | bytes 110600 | tf_op jit(solution)/shard_map/ppermute | solution.py:874
  31.2 4.0 %collective-permute-start.11 = (f32[72,128]{1,0:T(8,128)S(1)}, f32[72,128]{1,0:T(8,128)S(1)}, u32[]{:S(2)}, u32[]{:S(2)}) collective-permute-start(f32[72,128]{1,0:T(8,128)S(1)} %get-tuple-element.103), channel_id=1, source_target_pairs={{0,4},{4,0},{8,16},{12,20},{16,8},{20,12},{24,28},{28,24},{1,5},{5... | collective-permute-start | bytes 110600 | tf_op jit(solution)/shard_map/ppermute | solution.py:873
  46.7 5.9 %collective-permute-start.13 = (bf16[2,128,256]{2,1,0:T(8,128)(2,1)S(1)}, bf16[2,128,256]{2,1,0:T(8,128)(2,1)S(1)}, u32[]{:S(2)}, u32[]{:S(2)}) collective-permute-start(bf16[2,128,256]{2,1,0:T(8,128)(2,1)S(1)} %get-tuple-element.113), channel_id=1, source_target_pairs={{0,2},{1,3},{2,0},{3,1},{4,6},{5,7},{6,4},{7,5},{8,10},{9,11},{10,... | collective-permute-start | bytes 393224 | tf_op jit(solution)/shard_map/ppermute | solution.py:751
  48.5 5.5 %collective-permute-start.15 = (bf16[256,256]{1,0:T(8,128)(2,1)S(1)}, bf16[256,256]{1,0:T(8,128)(2,1)S(1)}, u32[]{:S(2)}, u32[]{:S(2)}) collective-permute-start(bf16[256,256]{1,0:T(8,128)(2,1)S(1)} %get-tuple-element.126), channel_id=1, source_target_pairs={{0,2},{1,3},{2,0},{3,1},{4,6},{5,7},{6,4},{7,5},{8,10},{9,11},{10,... | collective-permute-start | bytes 393224 | tf_op jit(solution)/shard_map/ppermute | solution.py:751
  52.6 1.4 %collective-permute-start.14 = (bf16[2,128,256]{2,1,0:T(8,128)(2,1)S(1)}, bf16[2,128,256]{2,1,0:T(8,128)(2,1)S(1)}, u32[]{:S(2)}, u32[]{:S(2)}) collective-permute-start(bf16[2,128,256]{2,1,0:T(8,128)(2,1)S(1)} %add_convert_fusion.1.one), channel_id=1, source_target_pairs={{0,1},{1,0},{2,3},{3,2},{4,5},{5,4},{6,7},{7,6},{8,9},{9,8},{10,11... | collective-permute-start | bytes 393224 | tf_op jit(solution)/shard_map/ppermute | solution.py:751
  52.7 4.8 %collective-permute-start.21 = (bf16[304,128]{1,0:T(8,128)(2,1)S(1)}, bf16[304,128]{1,0:T(8,128)(2,1)S(1)}, u32[]{:S(2)}, u32[]{:S(2)}) collective-permute-start(bf16[304,128]{1,0:T(8,128)(2,1)S(1)} %get-tuple-element.137), channel_id=1, source_target_pairs={{0,4},{4,0},{8,12},{12,8},{16,20},{20,16},{24,28},{28,24},{1,5},{5... | collective-permute-start | bytes 233480 | tf_op jit(solution)/shard_map/ppermute | solution.py:751
  55.2 5.6 %collective-permute-start.25 = (bf16[208,128]{1,0:T(8,128)(2,1)S(1)}, bf16[208,128]{1,0:T(8,128)(2,1)S(1)}, u32[]{:S(2)}, u32[]{:S(2)}) collective-permute-start(bf16[208,128]{1,0:T(8,128)(2,1)S(1)} %get-tuple-element.139), channel_id=1, source_target_pairs={{0,4},{4,0},{8,12},{12,8},{16,20},{20,16},{24,28},{28,24},{1,5},{5... | collective-permute-start | bytes 159752 | tf_op jit(solution)/shard_map/ppermute | solution.py:751
  57.5 6.1 %collective-permute-start.22 = (bf16[304,128]{1,0:T(8,128)(2,1)S(1)}, bf16[304,128]{1,0:T(8,128)(2,1)S(1)}, u32[]{:S(2)}, u32[]{:S(2)}) collective-permute-start(bf16[304,128]{1,0:T(8,128)(2,1)S(1)} %add_convert_fusion.5), channel_id=1, source_target_pairs={{0,8},{4,12},{8,0},{12,4},{16,24},{20,28},{24,16},{28,20},{1,9},{5... | collective-permute-start | bytes 233480 | tf_op jit(solution)/shard_map/ppermute | solution.py:751
  60.9 6.8 %collective-permute-start.26 = (bf16[208,128]{1,0:T(8,128)(2,1)S(1)}, bf16[208,128]{1,0:T(8,128)(2,1)S(1)}, u32[]{:S(2)}, u32[]{:S(2)}) collective-permute-start(bf16[208,128]{1,0:T(8,128)(2,1)S(1)} %add_convert_fusion.8), channel_id=1, source_target_pairs={{0,8},{4,12},{8,0},{12,4},{16,24},{20,28},{24,16},{28,20},{1,9},{5... | collective-permute-start | bytes 159752 | tf_op jit(solution)/shard_map/ppermute | solution.py:751
  63.7 6.1 %collective-permute-start.23 = (bf16[304,128]{1,0:T(8,128)(2,1)S(1)}, bf16[304,128]{1,0:T(8,128)(2,1)S(1)}, u32[]{:S(2)}, u32[]{:S(2)}) collective-permute-start(bf16[304,128]{1,0:T(8,128)(2,1)S(1)} %add_convert_fusion.4), channel_id=1, source_target_pairs={{0,16},{4,20},{8,24},{12,28},{16,0},{20,4},{24,8},{28,12},{1,17},{... | collective-permute-start | bytes 233480 | tf_op jit(solution)/shard_map/ppermute | solution.py:751
  65.7 4.4 %collective-permute-start.16 = (f32[2,16,128]{2,1,0:T(8,128)S(1)}, f32[2,16,128]{2,1,0:T(8,128)S(1)}, u32[]{:S(2)}, u32[]{:S(2)}) collective-permute-start(f32[2,16,128]{2,1,0:T(8,128)S(1)} %get-tuple-element.128), channel_id=1, source_target_pairs={{0,4},{4,0},{8,12},{12,8},{16,20},{20,16},{24,28},{28,24},{1,5},{5... | collective-permute-start | bytes 49160 | tf_op jit(solution)/shard_map/ppermute | solution.py:937
  66.7 3.7 %collective-permute-start.17 = (f32[2,16,128]{2,1,0:T(8,128)S(1)}, f32[2,16,128]{2,1,0:T(8,128)S(1)}, u32[]{:S(2)}, u32[]{:S(2)}) collective-permute-start(f32[2,16,128]{2,1,0:T(8,128)S(1)} %get-tuple-element.129), channel_id=1, source_target_pairs={{0,4},{4,0},{8,20},{12,16},{16,12},{20,8},{24,28},{28,24},{1,5},{5... | collective-permute-start | bytes 49160 | tf_op jit(solution)/shard_map/ppermute | solution.py:941
  67.7 2.8 %collective-permute-start.18 = (bf16[256,128]{1,0:T(8,128)(2,1)S(1)}, bf16[256,128]{1,0:T(8,128)(2,1)S(1)}, u32[]{:S(2)}, u32[]{:S(2)}) collective-permute-start(bf16[256,128]{1,0:T(8,128)(2,1)S(1)} %get-tuple-element.132), channel_id=1, source_target_pairs={{0,1},{1,0},{2,3},{3,2},{4,5},{5,4},{6,7},{7,6},{8,9},{9,8},{10,11... | collective-permute-start | bytes 196616 | tf_op jit(solution)/shard_map/ppermute | solution.py:751
  67.7 6.3 %collective-permute-start.27 = (bf16[208,128]{1,0:T(8,128)(2,1)S(1)}, bf16[208,128]{1,0:T(8,128)(2,1)S(1)}, u32[]{:S(2)}, u32[]{:S(2)}) collective-permute-start(bf16[208,128]{1,0:T(8,128)(2,1)S(1)} %add_convert_fusion.7), channel_id=1, source_target_pairs={{0,16},{4,20},{8,24},{12,28},{16,0},{20,4},{24,8},{28,12},{1,17},{... | collective-permute-start | bytes 159752 | tf_op jit(solution)/shard_map/ppermute | solution.py:751
  69.8 10.0 %collective-permute-start.24 = (bf16[304,128]{1,0:T(8,128)(2,1)S(1)}, bf16[304,128]{1,0:T(8,128)(2,1)S(1)}, u32[]{:S(2)}, u32[]{:S(2)}) collective-permute-start(bf16[304,128]{1,0:T(8,128)(2,1)S(1)} %add_convert_fusion.3.refs_0_), channel_id=1, source_target_pairs={{0,4},{4,0},{8,12},{12,8},{16,20},{20,16},{24,28},{28,24},{1,5},{5... | collective-permute-start | bytes 233480 | tf_op jit(solution)/shard_map/ppermute | solution.py:751
  71.6 5.0 %collective-permute-start.19 = (bf16[256,256]{1,0:T(8,128)(2,1)S(1)}, bf16[256,256]{1,0:T(8,128)(2,1)S(1)}, u32[]{:S(2)}, u32[]{:S(2)}) collective-permute-start(bf16[256,256]{1,0:T(8,128)(2,1)S(1)} %get-tuple-element.135), channel_id=1, source_target_pairs={{0,2},{1,3},{2,0},{3,1},{4,6},{5,7},{6,4},{7,5},{8,10},{9,11},{10,... | collective-permute-start | bytes 393224 | tf_op jit(solution)/shard_map/ppermute | solution.py:751
  74.1 5.7 %collective-permute-start.28 = (bf16[208,128]{1,0:T(8,128)(2,1)S(1)}, bf16[208,128]{1,0:T(8,128)(2,1)S(1)}, u32[]{:S(2)}, u32[]{:S(2)}) collective-permute-start(bf16[208,128]{1,0:T(8,128)(2,1)S(1)} %add_convert_fusion.6.refs_2_), channel_id=1, source_target_pairs={{0,4},{4,0},{8,12},{12,8},{16,20},{20,16},{24,28},{28,24},{1,5},{5... | collective-permute-start | bytes 159752 | tf_op jit(solution)/shard_map/ppermute | solution.py:751
  74.9 3.7 %collective-permute-start.29 = (f32[16,128]{1,0:T(8,128)S(1)}, f32[16,128]{1,0:T(8,128)S(1)}, u32[]{:S(2)}, u32[]{:S(2)}) collective-permute-start(f32[16,128]{1,0:T(8,128)S(1)} %slice_convert_fusion), channel_id=1, source_target_pairs={{0,2},{1,3},{2,0},{3,1},{4,6},{5,7},{6,4},{7,5},{8,10},{9,11},{10,... | collective-permute-start | bytes 24584 | tf_op jit(solution)/shard_map/ppermute | solution.py:751
  76.7 4.0 %collective-permute-start.20 = (bf16[256,256]{1,0:T(8,128)(2,1)S(1)}, bf16[256,256]{1,0:T(8,128)(2,1)S(1)}, u32[]{:S(2)}, u32[]{:S(2)}) collective-permute-start(bf16[256,256]{1,0:T(8,128)(2,1)S(1)} %add_convert_fusion.one), channel_id=1, source_target_pairs={{0,1},{1,0},{2,3},{3,2},{4,5},{5,4},{6,7},{7,6},{8,9},{9,8},{10,11... | collective-permute-start | bytes 393224 | tf_op jit(solution)/shard_map/ppermute | solution.py:751
  78.6 1.2 %collective-permute-start.30 = (f32[16,128]{1,0:T(8,128)S(1)}, f32[16,128]{1,0:T(8,128)S(1)}, u32[]{:S(2)}, u32[]{:S(2)}) collective-permute-start(f32[16,128]{1,0:T(8,128)S(1)} %fusion), channel_id=1, source_target_pairs={{0,1},{1,0},{2,3},{3,2},{4,5},{5,4},{6,7},{7,6},{8,9},{9,8},{10,11... | collective-permute-start | bytes 24584 | tf_op jit(solution)/shard_map/ppermute | solution.py:751

commit v4 on v3

--- a/solution.py
+++ b/solution.py
@@ -13,6 +13,7 @@
 WINDOW = 16384
 LANES = 128
 CHUNKS = 8
+COLUMNS = R + 2 * N
 EPSILON = 1e-06
 LOG2E = 1.4426950408889634
 F32 = jnp.float32
@@ -156,11 +157,11 @@
 def prepare_kernel(
     geo, lengths_in, x_in, c_in, w_in, ow_in, stw_in, gain_in, cw_in, cb_in, sw_in, stb_in, decay_in, skip_in,
     x_out, c_out, valid, edge, turn, mover, back, gains, weights, outs, select, table, spread, tiny, stw,
-    lengths, gain, cw, cb, sw, stb, decay, skip, sems,
+    lengths, gain, cw, cb, stb, decay, skip, sems,
 ):
     pairs = (
         (lengths_in, lengths), (w_in, weights.at[0:2]), (ow_in, outs.at[0]), (stw_in, stw), (gain_in, gain),
-        (cw_in, cw), (cb_in, cb), (sw_in, sw), (stb_in, stb), (decay_in, decay), (skip_in, skip),
+        (cw_in, cw), (cb_in, cb), (sw_in, select), (stb_in, stb), (decay_in, decay), (skip_in, skip),
         (x_in, x_out), (c_in, c_out),
     )
     copies = [pltpu.make_async_copy(source, target, sems.at[i]) for i, (source, target) in enumerate(pairs)]
@@ -173,9 +174,8 @@
     mover[...] = permuter(tok)
     back[...] = unpermuter(tok)
     for at in range(0, 2 * N):
-        key = iota((LANES, LANES), 0) % 64
+        key = iota((2 * COLUMNS, LANES), 0) % COLUMNS
         spread[:, at * LANES : (at + 1) * LANES] = one_hot(key == R + at)
-    select[...] = jnp.zeros_like(select)
     tiny[...] = jnp.zeros_like(tiny)
     for copy in copies:
         copy.wait()
@@ -191,9 +191,7 @@
     for k in range(2):
         weights[2 + k] = low(nn(flip, weights[k]))
     outs[1] = low(nn(outs[0], flip))
-    amount = sw.shape[1]
     for course in range(2):
-        select[course, 64 * course : 64 * course + amount] = sw[course]
         natural = -jnp.exp(decay[course])
         for n in range(N):
             level = jnp.broadcast_to(natural[n : n + 1], (CHUNKS, LANES))
@@ -299,7 +297,6 @@
         edges = low(nn(rows, w[0]) * edge[...]).astype(F32)
         main = inputs[strand].astype(F32)
         fill_padded(padded.at[strand], main, edges, steps)
-        total = jnp.zeros((tok, LANES), F32)
         for course in range(2):
             member = 2 * strand + course
             running = jnp.broadcast_to(tiny[8 + course : 9 + course], (tok, lanes))
@@ -310,8 +307,7 @@
             pre[member] = running
             active = low(silu(running))
             act[member] = active
-            total = total + nt(active, select[course])
-        message[strand] = low(total)
+            message[strand, COLUMNS * course : COLUMNS * (course + 1)] = low(nt(select[course], active))
 
 
 def columns(n):
@@ -319,7 +315,7 @@
 
 
 def summary_kernel(
-    geo, one, two, act, dys, stw, tiny, table, spread, valid,
+    geo, split_devices, one, two, act, dys, stw, tiny, table, spread, valid,
     proj, raw, step, drive, chunk_p, chunk_h, chunk_w, wide, near, far, up, down,
 ):
     steps = geo.steps
@@ -327,15 +323,14 @@
         total = one[strand].astype(F32) + two[strand].astype(F32)
         for course in range(2):
             member = 2 * strand + course
-            here = total if course == 0 else pltpu.roll(total, 64, 1)
+            here = total[COLUMNS * course : COLUMNS * (course + 1)]
             rounded = low(here)
             proj[member] = rounded
-            rest = pltpu.roll(here - rounded.astype(F32), 64, 1)
-            lane = iota(here.shape, 1)
-            split = low(jnp.where(lane < 64, here, rest))
+            rest = here - rounded.astype(F32)
+            split = low(jnp.concatenate([here, rest], axis=0).T)
             for at in range(0, 2 * N * LANES, 512):
                 wide[member, :, at : at + 512] = nn(split, spread[:, at : at + 512])
-            step_raw = nn(rounded[:, :R], stw[course]) + tiny[10 + course : 11 + course]
+            step_raw = tn(rounded[:R], stw[course]) + tiny[10 + course : 11 + course]
             step_row = softplus(step_raw) * valid[...]
             raw[member] = step_raw
             step[member] = step_row
@@ -346,19 +341,17 @@
         for base in range(0, N, 8):
 
             def body(k, carry):
-                ps, hs, ws = carry
+                ps, hs, ws = (list(c) for c in carry)
                 t = steps - 1 - k if flipped else k
                 rows = pl.ds(pl.multiple_of(t * CHUNKS, CHUNKS), CHUNKS)
                 s, d, y = step[member, rows], drive[member, rows], dys[strand, rows]
-                np_, nh, nw = [], [], []
                 for i in range(8):
                     n = base + i
                     decay_here = jnp.exp2(s * table[2 + course, n])
-                    p = ps[i] * decay_here
-                    np_.append(p)
-                    nh.append(hs[i] * decay_here + wide[member, rows, columns(n)] * d)
-                    nw.append(ws[i] + p * (wide[member, rows, columns(N + n)] * y))
-                return tuple(np_), tuple(nh), tuple(nw)
+                    ps[i] = ps[i] * decay_here
+                    hs[i] = hs[i] * decay_here + wide[member, rows, columns(n)] * d
+                    ws[i] = ws[i] + ps[i] * (wide[member, rows, columns(N + n)] * y)
+                return tuple(ps), tuple(hs), tuple(ws)
 
             zero = jnp.zeros((CHUNKS, LANES), F32)
             start = (tuple([zero + 1.0] * 8), (zero,) * 8, (zero,) * 8)
@@ -389,14 +382,19 @@
         goes_up, goes_down = (w, h) if FLIPS[member] else (h, w)
         up[slot_up * N : (slot_up + 1) * N] = goes_up
         down[slot_down * N : (slot_down + 1) * N] = goes_down
-        up[4 * N + slot_up : 4 * N + slot_up + 1] = length
-        down[4 * N + slot_down : 4 * N + slot_down + 1] = length
-    up[4 * N + 4 :] = jnp.zeros((4, LANES), F32)
-    down[4 * N + 4 :] = jnp.zeros((4, LANES), F32)
-    if near is not None:
+        high = low(length).astype(F32)
+        for message, slot in ((up, slot_up), (down, slot_down)):
+            message[4 * N + slot : 4 * N + slot + 1] = high
+            message[4 * N + 4 + slot : 4 * N + 5 + slot] = length - high
+    up[4 * N + 8 :] = jnp.zeros((8, LANES), F32)
+    down[4 * N + 8 :] = jnp.zeros((8, LANES), F32)
+    if split_devices:
         local = geo.local()
-        near[...] = jnp.where(lax.rem(local, 2) == 0, up[...], down[...])
-        far[...] = jnp.where(local < 2, up[...], down[...])
+        near[...] = low(jnp.where(lax.rem(local, 2) == 0, up[...], down[...]))
+        far[...] = low(jnp.where(local < 2, up[...], down[...]))
+    else:
+        near[...] = low(up[...])
+        far[...] = low(down[...])
 
 
 UP_MEMBERS = (0, 3, 1, 2)
@@ -417,7 +415,7 @@
     if len(slot_refs) == 1:
         slots = slot_refs[0]
     else:
-        slots[local] = jnp.zeros(slots.shape[1:], F32)
+        slots[local] = jnp.zeros(slots.shape[1:], BF16)
         others = (lax.bitwise_xor(local, 1), lax.rem(local + 2, 4), 3 - local)
         for at, ref in zip(others, slot_refs):
             slots[at] = ref[...]
@@ -434,8 +432,9 @@
             use = use & (there >= 0) & (there < geo.rows)
             out = []
             for q in range(4):
-                length = slots[k, 4 * N + q : 4 * N + q + 1]
-                new = jnp.exp2(tables[q] * length) * carried[q] + slots[k, q * N : (q + 1) * N]
+                lengths = slots[k, 4 * N : 5 * N].astype(F32)
+                length = lengths[q : q + 1] + lengths[4 + q : 5 + q]
+                new = jnp.exp2(tables[q] * length) * carried[q] + slots[k, q * N : (q + 1) * N].astype(F32)
                 out.append(jnp.where(use, new, carried[q]))
             return tuple(out)
 
@@ -526,7 +525,11 @@
         for n in range(N):
             rows = slice(n * CHUNKS, (n + 1) * CHUNKS)
             dacc[course, rows] = dacc[course, rows] + ds[n]
-        dproj[member] = nt(spread[:64], quads[...])
+        for part in range(2):
+            rows = slice(R + part * N, R + (part + 1) * N)
+            lanes = slice(part * N * LANES, (part + 1) * N * LANES)
+            for at in range(0, tok, LANES):
+                dproj[member, rows, at : at + LANES] = nt(spread[rows, lanes], quads[at : at + LANES, lanes])
 
     lax.fori_loop(0, 2, lambda i, c: (sweep(3 * i, False), c)[1], 0)
     lax.fori_loop(0, 2, lambda i, c: (sweep(1 + i, True), c)[1], 0)
@@ -548,12 +551,13 @@
             rounded = low(raw_grad * valid[...] * sigmoid(raw[member]))
             dact[member] = pull_y[member] * step[member] + grad * tiny[12 + course : 13 + course]
             rows = slice(course * R, (course + 1) * R)
-            small[rows] += tn(proj[member], rounded)[:R]
+            small[rows] += nn(proj[member, :R], rounded)
             at = 2 * R + 2 * N + course
             small[at : at + 1] += jnp.sum(rounded.astype(F32), axis=0, keepdims=True)
             small[at + 2 : at + 3] += jnp.sum(grad * active, axis=0, keepdims=True)
-            message[strand, 64 * course : 64 * course + R] = low(nt(stw[course], rounded))
-            message[strand, 64 * course + R : 64 * course + 64] = low(dproj[member, R:])
+            at = COLUMNS * course
+            message[strand, at : at + R] = low(nt(stw[course], rounded))
+            message[strand, at + R : at + COLUMNS] = low(dproj[member, R:])
         gate = gates[strand]
         mixed[strand] = low(joined * silu(gate) * valid[...])
         dgate[strand] = low(gm[strand] * joined * silu_slope(gate))
@@ -601,8 +605,7 @@
 
 def conv_back_kernel(
     geo, one, two, act, dact, pre, padded, tiny, select, normed, rims_normed, gains, w, g_gate, valid, edge,
-    res_kept, res_got,
-    xg, near, far, keep, send, res_own, res_sent,
+    xg, near, far, keep, send, gain_rows,
     pad_grad, pack,
 ):
     tok, steps = geo.tok, geo.steps
@@ -612,7 +615,7 @@
     rim = taps - 1
     sub = iota((CHUNKS, LANES), 0)
     pack[...] = jnp.zeros_like(pack)
-    grad_select = [jnp.zeros((64, LANES), F32)] * 2
+    grad_select = [jnp.zeros((COLUMNS, LANES), F32)] * 2
     grad_in = jnp.zeros((width, LANES), F32)
     at_conv = width + LANES - 32
     for strand in range(2):
@@ -620,9 +623,9 @@
         rounded = low(one[strand].astype(F32) + two[strand].astype(F32))
         for course in range(2):
             member = 2 * strand + course
-            mine = slice(64 * course, 64 * course + 64)
+            mine = slice(COLUMNS * course, COLUMNS * (course + 1))
             grad_select[course] = grad_select[course] + nn(rounded[mine], act[member])
-            total = dact[member] + tn(rounded, select[course])
+            total = dact[member] + tn(rounded[mine], select[course])
             grad = total * silu_slope(pre[member])
             row = at_conv + 8 + course
             pack[row : row + 1] += jnp.sum(grad, axis=0, keepdims=True)
@@ -655,27 +658,19 @@
         near[strand] = jnp.where(even, rims[16:], rims[:16])
         far[strand] = jnp.where(even, rims[:16], rims[16:])
     pack[:width] = grad_in
-    amount = LANES // 2 - 16
     for course in range(2):
-        pack[width + course * amount : width + (course + 1) * amount] = grad_select[course][:amount]
+        pack[width + course * COLUMNS : width + (course + 1) * COLUMNS] = grad_select[course]
     halves(pack, L_ROWS, keep, send)
     product = grad_in * w[0].astype(F32) + g_gate[...] * w[1].astype(F32)
     high = low(product)
     ones = jnp.ones((8, LANES), BF16)
     gain_part = (nt(ones, high) + nt(ones, low(product - high.astype(F32)))) / gains[:1]
-    at = keep.shape[0] - GAIN_ROWS
-    keep[at : at + 8] = gain_part[:, :LANES]
-    keep[at + 8 :] = gain_part[:, LANES:]
-    at = send.shape[0] - GAIN_ROWS
-    send[at:] = low(jnp.concatenate([gain_part[:, :LANES], gain_part[:, LANES:]], axis=0))
-    total = res_kept[...] + res_got[...].astype(F32)
-    odd = lax.rem(lax.axis_index("ch"), 2) == 1
-    res_own[...] = jnp.where(odd, total[:, LANES:], total[:, :LANES])
-    res_sent[...] = low(jnp.where(odd, total[:, :LANES], total[:, LANES:]))
+    gain_rows[:8] = gain_part[:, :LANES]
+    gain_rows[8:] = gain_part[:, LANES:]
 
 
 def normed_back_kernel(
-    geo, xg, near, far, dn_gate, weights, valid, back, hidden, res_own, res_got, kept, sent, result
+    geo, xg, near, far, dn_gate, weights, valid, back, kept, sent
 ):
     tok, steps = geo.tok, geo.steps
     even = lax.rem(lax.axis_index("rows"), 2) == 0
@@ -695,11 +690,9 @@
         grads.append(nt(low(nn(back[...], rounded)), weights[2 * strand]) + dn_gate[strand])
     kept[...] = jnp.where(second, grads[1], grads[0])
     sent[...] = low(jnp.where(second, grads[0], grads[1]))
-    out = hidden[...].astype(F32) + res_own[...] + res_got[...].astype(F32)
-    result[...] = low(out)
-
-
-def finish_kernel(geo, one, two, xo, xc, gains, cot, input_grad):
+
+
+def finish_kernel(geo, one, two, xo, xc, gains, cot, res_own, res_got, input_grad, result):
     mine = lax.axis_index("ch")
     odd = lax.rem(mine, 2) == 1
     a, b = xo[...].astype(F32), xc[...].astype(F32)
@@ -709,10 +702,11 @@
     here = jnp.where(mine >= 2, gains[1:], gains[:1])
     scaled = (one[...].astype(F32) + two[...].astype(F32)) * here
     back = inverse * (scaled - unit * jnp.mean(scaled * unit, axis=-1, keepdims=True))
+    result[...] = low(xo[...].astype(F32) + res_own[...] + res_got[...].astype(F32))
     input_grad[...] = cot[...].astype(F32) + jnp.where(odd, back[:, LANES:], back[:, :LANES])
 
 
-def unpack_kernel(e_parts, l_parts, gain_sum, in_g, out_g, sel_g, cw_g, cb_g, stw_g, stb_g, decay_g, skip_g, gain_g, e_pack, l_pack):
+def unpack_kernel(e_parts, l_parts, in_g, out_g, sel_g, cw_g, cb_g, stw_g, stb_g, decay_g, skip_g, gain_g, e_pack, l_pack):
     mine = lax.rem(lax.axis_index("rows"), 2)
     for parts, pack in ((e_parts, e_pack), (l_parts, l_pack)):
         total = pack.shape[0]
@@ -742,8 +736,9 @@
     at = at + 2 * R + 2 * N
     stb_g[...] = e_pack[at : at + 2]
     skip_g[...] = e_pack[at + 2 : at + 4]
-    gain_g[:, :LANES] = gain_sum[:1].astype(F32)
-    gain_g[:, LANES:] = gain_sum[8:9].astype(F32)
+    total = sum(part[part.shape[0] - GAIN_ROWS :].astype(F32) for part in l_parts)
+    gain_g[:, :LANES] = total[:1]
+    gain_g[:, LANES:] = total[8:9]
 
 
 def swap(value, axis, distance):
@@ -789,7 +784,7 @@
     members = ((4, tok, LANES), F32)
     members_low = ((4, tok, LANES), BF16)
     chunked = ((4, N * CHUNKS, LANES), F32)
-    summary = ((4 * N + 8, LANES), F32)
+    summary = ((5 * N, LANES), BF16)
     full = ((tok, width), F32)
     full_low = ((tok, width), BF16)
 
@@ -807,9 +802,9 @@
             ((2, width), F32),
             ((4, width, LANES), BF16),
             ((2, LANES, width), BF16),
-            ((2, LANES, LANES), BF16),
+            ((2, COLUMNS, LANES), BF16),
             ((4, N, CHUNKS, LANES), F32),
-            ((LANES, 2 * N * LANES), BF16),
+            ((2 * COLUMNS, 2 * N * LANES), BF16),
             ((24 + 2 * N, LANES), F32),
             (step_weight.shape, BF16),
         ],
@@ -821,7 +816,6 @@
             vm(gain.shape, F32),
             vm(conv_weight.shape, F32),
             vm(conv_bias.shape, F32),
-            vm((2, select_weight.shape[2], LANES), BF16),
             vm(step_bias.shape, F32),
             vm(decay_log.shape, F32),
             vm(skip_gain.shape, F32),
@@ -848,23 +842,17 @@
     )
     padded, rims_normed, pre, act, message = run(
         kernel(conv_kernel),
-        [((2, padded_rows, LANES), F32), ((2, 32, width), BF16), members, members_low, strands_low],
+        [((2, padded_rows, LANES), F32), ((2, 32, width), BF16), members, members_low, ((2, 2 * COLUMNS, tok), BF16)],
         inputs, near, far, edge, turn, gains, weights, select, tiny, dys,
     )
     one, two = partner_sum(message)
-    shapes = [members_low, members, members, members, chunked, chunked, chunked]
+    shapes = [((4, COLUMNS, tok), BF16), members, members, members, chunked, chunked, chunked]
     shapes += [((4, tok, 2 * N * LANES), F32)]
 
-    def summarise(*refs):
-        if small_mesh:
-            summary_kernel(geo, *refs)
-        else:
-            summary_kernel(geo, *refs[:17], None, None, *refs[17:])
-
     got = run(
-        summarise, shapes + [summary, summary],
+        functools.partial(summary_kernel, geo, small_mesh), shapes + [summary, summary],
         one, two, act, dys, stw, tiny, table, spread, valid,
-        scratch=[vm(summary[0], F32), vm(summary[0], F32)] if small_mesh else (), micros=10,
+        scratch=[vm(summary[0], F32), vm(summary[0], F32)], micros=6,
     )
     proj, raw, step, drive, chunk_p, chunk_h, chunk_w, wide = got[:8]
     if small_mesh:
@@ -873,17 +861,17 @@
             lax.ppermute(got[9], "rows", geo.across()),
             lax.ppermute(got[9], "rows", geo.far()),
         )
-        slot_scratch = vm((4,) + summary[0], F32)
+        slot_scratch = vm((4,) + summary[0], BF16)
     else:
         up, down = lax.all_gather(got[8], "rows"), lax.all_gather(got[9], "rows")
         place = lax.axis_index("rows")
         index = place - geo.local() + jnp.arange(geo.members)
         inside = jnp.clip(index, 0, rows - 1)
         slots = (jnp.where((index < place)[:, None, None], up[inside], down[inside]),)
-        slot_scratch = vm((8, LANES), F32)
+        slot_scratch = vm((16, LANES), BF16)
     mixed, dgate, dact, message, small = run(
         lifted(kernel(scan_kernel), 0, len(slots)),
-        [strands_low, strands_low, members, ((2, LANES, tok), BF16), ((80, LANES), F32)],
+        [strands_low, strands_low, members, ((2, 2 * COLUMNS, tok), BF16), ((80, LANES), F32)],
         *slots, act, proj, raw, step, drive, chunk_p, chunk_h, chunk_w, wide, spread,
         dys, gm, gates, stw, tiny, table, valid,
         scratch=[
@@ -895,14 +883,14 @@
             vm(members[0], F32),
             vm(members[0], F32),
             vm(members[0], F32),
-            vm((4, 64, tok), F32),
+            vm((4, COLUMNS, tok), F32),
             vm((2, N * CHUNKS, LANES), F32),
         ],
         micros=16, limit=14,
     )
     one, two = partner_sum(message)
     e_half = E_ROWS // 2
-    l_half = L_ROWS // 2 + GAIN_ROWS
+    l_half = L_ROWS // 2
     res_kept, res_sent, e_keep, e_send, g_gate, dn_gate = run(
         kernel(dense_kernel),
         [
@@ -919,51 +907,51 @@
     res_got = swap(res_sent, "ch", 2)
     if small_mesh:
         e_sum = low(e_keep + swap(e_send, "rows", 1).astype(F32))
-    xg, near, far, l_keep, l_send, res_own, res_sent = run(
+    xg, near, far, l_keep, l_send, gain_part = run(
         kernel(conv_back_kernel),
         [
             strands,
             ((2, 16, LANES), F32),
             ((2, 16, LANES), F32),
-            ((l_half if small_mesh else L_ROWS + GAIN_ROWS, LANES), F32),
+            ((l_half if small_mesh else L_ROWS, LANES), F32),
             ((l_half, LANES), BF16),
-            ((tok, LANES), F32),
-            ((tok, LANES), BF16),
+            ((GAIN_ROWS, LANES), F32),
         ],
         one, two, act, dact, pre, padded, tiny, select, normed, rims_normed, gains, weights, g_gate, valid, edge,
-        res_kept, res_got,
         scratch=[vm((padded_rows, LANES), F32), vm((L_ROWS, LANES), F32)],
     )
     near = lax.ppermute(near, "rows", geo.near())
     if small_mesh:
-        l_sum = low(l_keep + swap(l_send, "rows", 1).astype(F32))
+        gain_part = gain_part + swap(gain_part, "ch", 2)
+        gain_part = gain_part + swap(gain_part, "ch", 1)
+        l_sum = jnp.concatenate([l_keep + swap(l_send, "rows", 1).astype(F32), gain_part], axis=0)
         e_sum = low(e_sum.astype(F32) + swap(e_sum, "rows", 2).astype(F32))
+        e_sum = low(e_sum.astype(F32) + swap(e_sum, "rows", 4).astype(F32))
     far = lax.ppermute(far, "rows", geo.far())
-    res_got = swap(res_sent, "ch", 1)
-    dn_kept, dn_sent, result = run(
+    total = res_kept + res_got.astype(F32)
+    odd = lax.axis_index("ch") % 2 == 1
+    res_own = jnp.where(odd, total[:, LANES:], total[:, :LANES])
+    res_got = swap(low(jnp.where(odd, total[:, :LANES], total[:, LANES:])), "ch", 1)
+    dn_kept, dn_sent = run(
         kernel(normed_back_kernel),
-        [full, full_low, ((tok, LANES), BF16)],
-        xg, near, far, dn_gate, weights, valid, back, x_own, res_own, res_got,
+        [full, full_low],
+        xg, near, far, dn_gate, weights, valid, back,
     )
     dn_got = swap(dn_sent, "ch", 2)
     dn = low(dn_kept + dn_got.astype(F32))
-    input_grad = run(
-        kernel(finish_kernel), ((tok, LANES), F32),
-        dn, swap(dn, "ch", 1), x_parts[0], x_parts[1], gains, c_own,
+    input_grad, result = run(
+        kernel(finish_kernel), [((tok, LANES), F32), ((tok, LANES), BF16)],
+        dn, swap(dn, "ch", 1), x_parts[0], x_parts[1], gains, c_own, res_own, res_got,
     )
     if small_mesh:
-        l_sum = low(l_sum.astype(F32) + swap(l_sum, "rows", 2).astype(F32))
-        e_sum = low(e_sum.astype(F32) + swap(e_sum, "rows", 4).astype(F32))
+        l_sum = low(l_sum + swap(low(l_sum), "rows", 2).astype(F32))
         l_sum = low(l_sum.astype(F32) + swap(l_sum, "rows", 4).astype(F32))
         e_parts = (e_sum, swap(e_sum, "rows", 1))
         l_parts = (l_sum, swap(l_sum, "rows", 1))
-        gain_part = l_sum[l_half - GAIN_ROWS :].astype(F32)
-        gain_part = gain_part + swap(gain_part, "ch", 2)
-        gain_part = gain_part + swap(gain_part, "ch", 1)
     else:
         e_parts = (lax.psum(e_keep, "rows"),)
-        l_parts = (lax.psum(l_keep, "rows"),)
-        gain_part = lax.psum(l_parts[0][L_ROWS:], "ch")
+        gain_part = lax.psum(gain_part, ("rows", "ch"))
+        l_parts = (jnp.concatenate([lax.psum(l_keep, "rows"), gain_part], axis=0),)
 
     def unpack(*refs):
         k = len(e_parts)
@@ -983,7 +971,7 @@
             (skip_gain.shape, F32),
             ((1, width), F32),
         ],
-        *e_parts, *l_parts, gain_part,
+        *e_parts, *l_parts,
         scratch=[vm((E_ROWS, LANES), F32), vm((L_ROWS, LANES), F32)],
     )
     in_g, out_g, sel_g, cw_g, cb_g, stw_g, stb_g, decay_g, skip_g, gain_g = got

time: 81.7 us -> 88.4 us (1.082)
  local copies, waits for them, and re-layouts: 0 us -> 4.15 us
  other arithmetic: 0.23 us -> 2.13 us
    unnamed x0 -> x18, local copies, waits for them, and re-layouts: none -> 4.15 us
    convert_element_type x9 -> x10, other arithmetic: 0.22 us -> 2.06 us  [low(): return v.astype(BF16)]
    ppermute x2, waiting for transfers between devices: 1.11 us -> 2.28 us  [on_device(): near = lax.ppermute(near, 'rows', geo.near())]
    ppermute x24, waiting for transfers between devices: 20.7 us -> 19.7 us  [swap(): return lax.ppermute(value, axis, [(i, i ^ distance) for i in range(count)])]
    ppermute x1, starting transfers between devices: 0.53 us -> 1.49 us  [on_device(): lax.ppermute(got[9], 'rows', geo.across())]
    ppermute x1, starting transfers between devices: 1.49 us -> 0.54 us  [on_device(): lax.ppermute(got[9], 'rows', geo.far())]
  transfers between devices with their start and end apart: 31 -> 31, of which waited for: 18 -> 17; matrix products, arithmetic and copies ran while one was open for 0% -> 2% of each run, Pallas kernels for 8% -> 6%
where the time goes in v4:
time: 88.4 us; the launch traced here: 88.1 us
  starting transfers between devices  27.9 us (32%)
  waiting for transfers between devices  27.7 us (31%)
  Pallas kernels  25.3 us (29%)
  local copies, waits for them, and re-layouts  4.15 us (5%)
  other arithmetic  2.13 us (2%)
    pallas_call x11, Pallas kernels, run(): got = call(*args)  25.3 us
    ppermute x24, starting transfers between devices, swap(): return lax.ppermute(value, axis, [(i, i ^ distance) for i in range(count)])  21.1 us
    ppermute x24, waiting for transfers between devices, swap(): return lax.ppermute(value, axis, [(i, i ^ distance) for i in range(count)])  19.7 us
    unnamed x18, local copies, waits for them, and re-layouts  4.15 us
    ppermute x2, waiting for transfers between devices, on_device(): far = lax.ppermute(far, 'rows', geo.far())  2.51 us
    ppermute x2, waiting for transfers between devices, on_device(): near = lax.ppermute(near, 'rows', geo.near())  2.28 us
    ppermute x2, starting transfers between devices, on_device(): near = lax.ppermute(near, 'rows', geo.near())  2.09 us
    convert_element_type x10, other arithmetic, low(): return v.astype(BF16)  2.06 us
  transfers between devices with their start and end apart: 31, of which 17 were waited for; matrix products, arithmetic and copies ran while one was open for 2% of the time, Pallas kernels for 6%

profile of v4, /device:TPU:0, one launch (start us, length us, event | category | flops | bytes accessed | tf_op | source)
XLA Modules:
  0.0 88.1 jit_solution(6245017393453128806)
XLA Ops:
  0.6 3.1 %collective-permute-start.1 = (bf16[256,128]{1,0:T(8,128)(2,1)}, bf16[256,128]{1,0:T(8,128)(2,1)S(1)}, u32[]{:S(2)}, u32[]{:S(2)}) collective-permute-start(bf16[256,128]{1,0:T(8,128)(2,1)} %x_in.1), channel_id=1, source_target_pairs={{0,2},{1,3},{2,0},{3,1},{4,6},{5,7},{6,4},{7,5},{8,10},{9,11},{10,... | collective-permute-start | bytes 196616 | tf_op jit(solution)/shard_map/ppermute | solution.py:746
  3.7 0.1 collective-permute-start.6
  3.8 2.5 %collective-permute-done.1.xy = bf16[256,128]{1,0:T(8,128)(2,1)S(1)} collective-permute-done((bf16[256,128]{1,0:T(8,128)(2,1)}, bf16[256,128]{1,0:T(8,128)(2,1)S(1)}, u32[]{:S(2)}, u32[]{:S(2)}) %collective-permute-start.1) | collective-permute-done | bytes 65568 | tf_op jit(solution)/shard_map/ppermute | solution.py:746
  6.3 0.5 collective-permute-start.5
  6.8 1.4 %collective-permute-done.6.cy = bf16[256,128]{1,0:T(8,128)(2,1)S(1)} collective-permute-done((bf16[256,128]{1,0:T(8,128)(2,1)}, bf16[256,128]{1,0:T(8,128)(2,1)S(1)}, u32[]{:S(2)}, u32[]{:S(2)}) %collective-permute-start.6) | collective-permute-done | bytes 65568 | tf_op jit(solution)/shard_map/ppermute | solution.py:746
  8.2 1.5 %shard_map.220 = (bf16[256,128]{1,0:T(8,128)(2,1)S(1)}, bf16[256,128]{1,0:T(8,128)(2,1)S(1)}, f32[256,128]{1,0:T(8,128)S(1)}, f32[32,128]{1,0:T(8,128)S(1)}, bf1...) custom-call(s32[3]{0:T(128)} %lengths_in.1, ...), custom_call_target="tpu_custom_call" | custom-call | bytes 6000000 | tf_op jit(solution)/shard_map/pallas_call | solution.py:143
  9.7 0.0 copy-start.1
  9.7 0.7 shard_map.221
  10.5 1.6 %collective-permute-start.3 = (bf16[16,512]{1,0:T(8,128)(2,1)S(1)}, bf16[16,512]{1,0:T(8,128)(2,1)S(1)}, u32[]{:S(2)}, u32[]{:S(2)}) collective-permute-start(bf16[16,512]{1,0:T(8,128)(2,1)S(1)} %get-tuple-element.88), channel_id=1, source_target_pairs={{0,4},{4,0},{8,12},{12,8},{16,20},{20,16},{24,28},{28,24},{1,5},{5... | collective-permute-start | bytes 49160 | tf_op jit(solution)/shard_map/ppermute | solution.py:835
  12.0 0.5 collective-permute-start.4
  12.6 0.6 shard_map.222
  13.2 1.1 %collective-permute-done.3.near = bf16[16,512]{1,0:T(8,128)(2,1)S(1)} collective-permute-done((bf16[16,512]{1,0:T(8,128)(2,1)S(1)}, bf16[16,512]{1,0:T(8,128)(2,1)S(1)}, u32[]{:S(2)}, u32[]{:S(2)}) %collective-permute-start.3) | collective-permute-done | bytes 16416 | tf_op jit(solution)/shard_map/ppermute | solution.py:835
  14.3 1.5 %collective-permute-done.4.far = bf16[16,512]{1,0:T(8,128)(2,1)S(1)} collective-permute-done((bf16[16,512]{1,0:T(8,128)(2,1)S(1)}, bf16[16,512]{1,0:T(8,128)(2,1)S(1)}, u32[]{:S(2)}, u32[]{:S(2)}) %collective-permute-start.4) | collective-permute-done | bytes 16416 | tf_op jit(solution)/shard_map/ppermute | solution.py:836
  15.8 0.8 shard_map.223
  16.6 0.0 copy-start.6
  16.6 0.6 copy-done.6
  17.2 1.0 %collective-permute-start.8 = (bf16[2,96,256]{2,1,0:T(8,128)(2,1)S(1)}, bf16[2,96,256]{2,1,0:T(8,128)(2,1)S(1)}, u32[]{:S(2)}, u32[]{:S(2)}) collective-permute-start(bf16[2,96,256]{2,1,0:T(8,128)(2,1)S(1)} %get-tuple-element.97), channel_id=1, source_target_pairs={{0,2},{1,3},{2,0},{3,1},{4,6},{5,7},{6,4},{7,5},{8,10},{9,11},{10,... | collective-permute-start | bytes 294920 | tf_op jit(solution)/shard_map/ppermute | solution.py:746
  18.2 3.6 %collective-permute-done.8 = bf16[2,96,256]{2,1,0:T(8,128)(2,1)S(1)} collective-permute-done((bf16[2,96,256]{2,1,0:T(8,128)(2,1)S(1)}, bf16[2,96,256]{2,1,0:T(8,128)(2,1)S(1)}, u32[]{:S(2)}, u32[]{:S(2)}) %collective-permute-start.8) | collective-permute-done | bytes 98336 | tf_op jit(solution)/shard_map/ppermute | solution.py:746
  21.9 0.1 collective-permute-start.9
  22.0 1.3 %collective-permute-done.9.two = bf16[2,96,256]{2,1,0:T(8,128)(2,1)S(1)} collective-permute-done((bf16[2,96,256]{2,1,0:T(8,128)(2,1)S(1)}, bf16[2,96,256]{2,1,0:T(8,128)(2,1)S(1)}, u32[]{:S(2)}, u32[]{:S(2)}) %collective-permute-start.9) | collective-permute-done | bytes 98336 | tf_op jit(solution)/shard_map/ppermute | solution.py:746
  23.2 6.1 %shard_map.224 = (bf16[4,48,256]{2,1,0:T(8,128)(2,1)S(1)}, f32[4,256,128]{2,1,0:T(8,128)S(1)}, f32[4,256,128]{2,1,0:T(8,128)S(1)}, f32[4,256,128]{2,1,0:T(8,128)...) custom-call(bf16[2,96,256]{2,1,0:T(8,128)(2,1)S(1)} %add_convert_fus, ...), custom_call_target="tpu_custom_call" | custom-call | bytes 18000000 | tf_op jit(solution)/shard_map/pallas_call | solution.py:143
  29.3 0.6 collective-permute-start.10
  29.9 1.5 %collective-permute-start.11 = (bf16[80,128]{1,0:T(8,128)(2,1)S(1)}, bf16[80,128]{1,0:T(8,128)(2,1)S(1)}, u32[]{:S(2)}, u32[]{:S(2)}) collective-permute-start(bf16[80,128]{1,0:T(8,128)(2,1)S(1)} %get-tuple-element.103), channel_id=1, source_target_pairs={{0,4},{4,0},{8,16},{12,20},{16,8},{20,12},{24,28},{28,24},{1,5},{5... | collective-permute-start | bytes 61448 | tf_op jit(solution)/shard_map/ppermute | solution.py:861
  31.4 0.5 collective-permute-start.12
  31.9 1.2 %collective-permute-done.10.refs_0_ = bf16[80,128]{1,0:T(8,128)(2,1)S(1)} collective-permute-done((bf16[80,128]{1,0:T(8,128)(2,1)S(1)}, bf16[80,128]{1,0:T(8,128)(2,1)S(1)}, u32[]{:S(2)}, u32[]{:S(2)}) %collective-permute-start.10) | collective-permute-done | bytes 20512 | tf_op jit(solution)/shard_map/ppermute | solution.py:860
  33.2 0.6 collective-permute-done.11.refs_1_
  33.8 1.4 %collective-permute-done.12.refs_2_ = bf16[80,128]{1,0:T(8,128)(2,1)S(1)} collective-permute-done((bf16[80,128]{1,0:T(8,128)(2,1)S(1)}, bf16[80,128]{1,0:T(8,128)(2,1)S(1)}, u32[]{:S(2)}, u32[]{:S(2)}) %collective-permute-start.12) | collective-permute-done | bytes 20512 | tf_op jit(solution)/shard_map/ppermute | solution.py:862
  35.2 11.0 %shard_map.225 = (bf16[2,256,128]{2,1,0:T(8,128)(2,1)S(1)}, bf16[2,256,128]{2,1,0:T(8,128)(2,1)S(1)}, f32[4,256,128]{2,1,0:T(8,128)S(1)}, bf16[2,96,256]{2,1,0:T(8,128)(2,1)S(1)}, f32[80,128]{1,0:T(8,128)S(1)}) custom-call(bf16[80,128]{1,0:T(8,128)(2,1)S(1)} %collective-permute-done.10.refs_0_, bf16[80,128]{1,0:T(8,128)(2,1)S(1)} %collective-permute-done.11.refs_1_, ...), custom_call_target="tpu_custom_call" | custom-call | bytes 48000000 | tf_op jit(solution)/shard_map/pallas_call | solution.py:143
  46.2 1.3 %shard_map.226 = (f32[256,256]{1,0:T(8,128)S(1)}, bf16[256,256]{1,0:T(8,128)(2,1)S(1)}, f32[304,128]{1,0:T(8,128)S(1)}, bf16[304,128]{1,0:T(8,128)(2,1)}, f32[25...) custom-call(bf16[2,256,128]{2,1,0:T(8,128)(2,1)S(1)} %get-tuple-element.119.mixed, ...), custom_call_target="tpu_custom_call" | custom-call | bytes 3000000 | tf_op jit(solution)/shard_map/pallas_call | solution.py:143
  47.5 0.7 copy-done
  48.1 0.7 copy-done.8
  48.8 0.5 collective-permute-start.21
  49.3 1.0 %collective-permute-start.13 = (bf16[2,96,256]{2,1,0:T(8,128)(2,1)}, bf16[2,96,256]{2,1,0:T(8,128)(2,1)S(1)}, u32[]{:S(2)}, u32[]{:S(2)}) collective-permute-start(bf16[2,96,256]{2,1,0:T(8,128)(2,1)} %copy-done.3), channel_id=1, source_target_pairs={{0,2},{1,3},{2,0},{3,1},{4,6},{5,7},{6,4},{7,5},{8,10},{9,11},{10,... | collective-permute-start | bytes 294920 | tf_op jit(solution)/shard_map/ppermute | solution.py:746
  50.3 1.1 %collective-permute-start.19 = (bf16[256,256]{1,0:T(8,128)(2,1)}, bf16[256,256]{1,0:T(8,128)(2,1)S(1)}, u32[]{:S(2)}, u32[]{:S(2)}) collective-permute-start(bf16[256,256]{1,0:T(8,128)(2,1)} %copy-done.8), channel_id=1, source_target_pairs={{0,2},{1,3},{2,0},{3,1},{4,6},{5,7},{6,4},{7,5},{8,10},{9,11},{10,... | collective-permute-start | bytes 393224 | tf_op jit(solution)/shard_map/ppermute | solution.py:746
  51.3 2.2 %collective-permute-done.21 = bf16[304,128]{1,0:T(8,128)(2,1)} collective-permute-done((bf16[304,128]{1,0:T(8,128)(2,1)}, bf16[304,128]{1,0:T(8,128)(2,1)}, u32[]{:S(2)}, u32[]{:S(2)}) %collective-permute-start.21) | collective-permute-done | bytes 77856 | tf_op jit(solution)/shard_map/ppermute | solution.py:746
  53.5 1.0 %add_convert_fusion.5 = bf16[304,128]{1,0:T(8,128)(2,1)S(1)} fusion(f32[304,128]{1,0:T(8,128)} %copy-done, bf16[304,128]{1,0:T(8,128)(2,1)} %collective-permute-done.21), kind=kLoop, calls=%fused_computation.6 | loop fusion | flops 116736 | bytes 311296 | tf_op jit(solution)/shard_map/convert_element_type | solution.py:79
  54.5 3.5 %collective-permute-start.22 = (bf16[304,128]{1,0:T(8,128)(2,1)S(1)}, bf16[304,128]{1,0:T(8,128)(2,1)S(1)}, u32[]{:S(2)}, u32[]{:S(2)}) collective-permute-start(bf16[304,128]{1,0:T(8,128)(2,1)S(1)} %add_convert_fusion.5), channel_id=1, source_target_pairs={{0,8},{4,12},{8,0},{12,4},{16,24},{20,28},{24,16},{28,20},{1,9},{5... | collective-permute-start | bytes 233480 | tf_op jit(solution)/shard_map/ppermute | solution.py:746
  58.0 0.9 %add_convert_fusion.1.one = bf16[2,96,256]{2,1,0:T(8,128)(2,1)S(1)} fusion(bf16[2,96,256]{2,1,0:T(8,128)(2,1)S(1)} %collective-permute-done.13, bf16[2,96,256]{2,1,0:T(8,128)(2,1)} %copy-done.3), kind=kLoop, calls=%fused_computation.2 | loop fusion | flops 196608 | bytes 294912 | tf_op jit(solution)/shard_map/convert_element_type | solution.py:79
  58.9 0.1 collective-permute-start.14
  59.0 1.2 %collective-permute-done.14.two = bf16[2,96,256]{2,1,0:T(8,128)(2,1)S(1)} collective-permute-done((bf16[2,96,256]{2,1,0:T(8,128)(2,1)S(1)}, bf16[2,96,256]{2,1,0:T(8,128)(2,1)S(1)}, u32[]{:S(2)}, u32[]{:S(2)}) %collective-permute-start.14) | collective-permute-done | bytes 98336 | tf_op jit(solution)/shard_map/ppermute | solution.py:746
  60.3 0.7 copy-done.2
  61.0 0.7 copy-done.5
  61.7 0.8 copy-done.7
  62.5 1.1 %shard_map.227 = (f32[2,256,128]{2,1,0:T(8,128)S(1)}, f32[2,16,128]{2,1,0:T(8,128)S(1)}, f32[2,16,128]{2,1,0:T(8,128)S(1)}, f32[192,128]{1,0:T(8,128)S(1)}, bf16...) custom-call(bf16[2,96,256]{2,1,0:T(8,128)(2,1)S(1)} %add_convert_fusion.1.one, ...), custom_call_target="tpu_custom_call" | custom-call | bytes 3000000 | tf_op jit(solution)/shard_map/pallas_call | solution.py:143
  63.6 1.0 %collective-permute-start.26 = (f32[16,128]{1,0:T(8,128)S(1)}, f32[16,128]{1,0:T(8,128)S(1)}, u32[]{:S(2)}, u32[]{:S(2)}) collective-permute-start(f32[16,128]{1,0:T(8,128)S(1)} %get-tuple-element.139), channel_id=1, source_target_pairs={{0,2},{1,3},{2,0},{3,1},{4,6},{5,7},{6,4},{7,5},{8,10},{9,11},{10,... | collective-permute-start | bytes 24584 | tf_op jit(solution)/shard_map/ppermute | solution.py:746
  64.6 0.1 collective-permute-start.20
  64.7 1.6 %collective-permute-start.25 = (bf16[192,128]{1,0:T(8,128)(2,1)S(1)}, bf16[192,128]{1,0:T(8,128)(2,1)S(1)}, u32[]{:S(2)}, u32[]{:S(2)}) collective-permute-start(bf16[192,128]{1,0:T(8,128)(2,1)S(1)} %get-tuple-element.138), channel_id=1, source_target_pairs={{0,4},{4,0},{8,12},{12,8},{16,20},{20,16},{24,28},{28,24},{1,5},{5... | collective-permute-start | bytes 147464 | tf_op jit(solution)/shard_map/ppermute | solution.py:746
  66.2 0.5 collective-permute-start.15
  66.8 0.5 collective-permute-done.26
  67.3 1.5 %collective-permute-start.16 = (f32[2,16,128]{2,1,0:T(8,128)S(1)}, f32[2,16,128]{2,1,0:T(8,128)S(1)}, u32[]{:S(2)}, u32[]{:S(2)}) collective-permute-start(f32[2,16,128]{2,1,0:T(8,128)S(1)} %get-tuple-element.127), channel_id=1, source_target_pairs={{0,4},{4,0},{8,20},{12,16},{16,12},{20,8},{24,28},{28,24},{1,5},{5... | collective-permute-start | bytes 49160 | tf_op jit(solution)/shard_map/ppermute | solution.py:930
  68.8 1.2 %collective-permute-done.15.near = f32[2,16,128]{2,1,0:T(8,128)S(1)} collective-permute-done((f32[2,16,128]{2,1,0:T(8,128)S(1)}, f32[2,16,128]{2,1,0:T(8,128)S(1)}, u32[]{:S(2)}, u32[]{:S(2)}) %collective-permute-start.15) | collective-permute-done | bytes 16416 | tf_op jit(solution)/shard_map/ppermute | solution.py:923
  70.0 1.0 %collective-permute-done.16.far = f32[2,16,128]{2,1,0:T(8,128)S(1)} collective-permute-done((f32[2,16,128]{2,1,0:T(8,128)S(1)}, f32[2,16,128]{2,1,0:T(8,128)S(1)}, u32[]{:S(2)}, u32[]{:S(2)}) %collective-permute-start.16) | collective-permute-done | bytes 16416 | tf_op jit(solution)/shard_map/ppermute | solution.py:930
  71.0 0.5 shard_map.228
  71.5 1.0 %collective-permute-start.17 = (bf16[256,256]{1,0:T(8,128)(2,1)S(1)}, bf16[256,256]{1,0:T(8,128)(2,1)S(1)}, u32[]{:S(2)}, u32[]{:S(2)}) collective-permute-start(bf16[256,256]{1,0:T(8,128)(2,1)S(1)} %get-tuple-element.130), channel_id=1, source_target_pairs={{0,2},{1,3},{2,0},{3,1},{4,6},{5,7},{6,4},{7,5},{8,10},{9,11},{10,... | collective-permute-start | bytes 393224 | tf_op jit(solution)/shard_map/ppermute | solution.py:746
  72.6 1.5 %collective-permute-start.28 = (bf16[208,128]{1,0:T(8,128)(2,1)S(1)}, bf16[208,128]{1,0:T(8,128)(2,1)S(1)}, u32[]{:S(2)}, u32[]{:S(2)}) collective-permute-start(bf16[208,128]{1,0:T(8,128)(2,1)S(1)} %fusion), channel_id=1, source_target_pairs={{0,8},{4,12},{8,0},{12,4},{16,24},{20,28},{24,16},{28,20},{1,9},{5... | collective-permute-start | bytes 159752 | tf_op jit(solution)/shard_map/ppermute | solution.py:746
  74.1 1.6 %collective-permute-done.23 = bf16[304,128]{1,0:T(8,128)(2,1)S(1)} collective-permute-done((bf16[304,128]{1,0:T(8,128)(2,1)S(1)}, bf16[304,128]{1,0:T(8,128)(2,1)S(1)}, u32[]{:S(2)}, u32[]{:S(2)}) %collective-permute-start.23) | collective-permute-done | bytes 77856 | tf_op jit(solution)/shard_map/ppermute | solution.py:746
  75.8 1.2 %collective-permute-start.24 = (bf16[304,128]{1,0:T(8,128)(2,1)S(1)}, bf16[304,128]{1,0:T(8,128)(2,1)S(1)}, u32[]{:S(2)}, u32[]{:S(2)}) collective-permute-start(bf16[304,128]{1,0:T(8,128)(2,1)S(1)} %add_convert_fusion.3.refs_0_), channel_id=1, source_target_pairs={{0,4},{4,0},{8,12},{12,8},{16,20},{20,16},{24,28},{28,24},{1,5},{5... | collective-permute-start | bytes 233480 | tf_op jit(solution)/shard_map/ppermute | solution.py:746
  77.0 1.9 %collective-permute-start.29 = (bf16[208,128]{1,0:T(8,128)(2,1)S(1)}, bf16[208,128]{1,0:T(8,128)(2,1)S(1)}, u32[]{:S(2)}, u32[]{:S(2)}) collective-permute-start(bf16[208,128]{1,0:T(8,128)(2,1)S(1)} %add_convert_fusion.7), channel_id=1, source_target_pairs={{0,16},{4,20},{8,24},{12,28},{16,0},{20,4},{24,8},{28,12},{1,17},{... | collective-permute-start | bytes 159752 | tf_op jit(solution)/shard_map/ppermute | solution.py:746
  78.9 0.1 collective-permute-start.18
  79.0 3.1 %collective-permute-done.29 = bf16[208,128]{1,0:T(8,128)(2,1)S(1)} collective-permute-done((bf16[208,128]{1,0:T(8,128)(2,1)S(1)}, bf16[208,128]{1,0:T(8,128)(2,1)S(1)}, u32[]{:S(2)}, u32[]{:S(2)}) %collective-permute-start.29) | collective-permute-done | bytes 53280 | tf_op jit(solution)/shard_map/ppermute | solution.py:746
  82.1 2.0 %collective-permute-start.30 = (bf16[208,128]{1,0:T(8,128)(2,1)S(1)}, bf16[208,128]{1,0:T(8,128)(2,1)S(1)}, u32[]{:S(2)}, u32[]{:S(2)}) collective-permute-start(bf16[208,128]{1,0:T(8,128)(2,1)S(1)} %add_convert_fusion.6.refs_2_), channel_id=1, source_target_pairs={{0,4},{4,0},{8,12},{12,8},{16,20},{20,16},{24,28},{28,24},{1,5},{5... | collective-permute-start | bytes 159752 | tf_op jit(solution)/shard_map/ppermute | solution.py:746
  84.1 2.2 %collective-permute-done.30.refs_3_ = bf16[208,128]{1,0:T(8,128)(2,1)S(1)} collective-permute-done((bf16[208,128]{1,0:T(8,128)(2,1)S(1)}, bf16[208,128]{1,0:T(8,128)(2,1)S(1)}, u32[]{:S(2)}, u32[]{:S(2)}) %collective-permute-start.30) | collective-permute-done | bytes 53280 | tf_op jit(solution)/shard_map/ppermute | solution.py:746
  86.3 0.8 shard_map.230
  87.2 0.9 %shard_map.229 = (f32[256,128]{1,0:T(8,128)}, bf16[256,128]{1,0:T(8,128)(2,1)}) custom-call(bf16[256,256]{1,0:T(8,128)(2,1)S(1)} %add_convert_fusion.one, bf16[256,256]{1,0:T(8,128)(2,1)S(1)} %collective-permute-done.18.two, bf16[256,128]{1,0:T(8,128)(2,1)S(1)} %get-tuple-element.81.xo, bf16[256,128]{1,0:T(8,128)(2,1)S(1)} %collective-permute-done.xc, ...), custom_call_target="tpu_custom_call" | custom-call | bytes 3000000 | tf_op jit(solution)/shard_map/pallas_call | solution.py:143
  (42 shorter events, 0.3 us)
Async XLA Ops:
  0.6 5.6 %collective-permute-start.1 = (bf16[256,128]{1,0:T(8,128)(2,1)}, bf16[256,128]{1,0:T(8,128)(2,1)S(1)}, u32[]{:S(2)}, u32[]{:S(2)}) collective-permute-start(bf16[256,128]{1,0:T(8,128)(2,1)} %x_in.1), channel_id=1, source_target_pairs={{0,2},{1,3},{2,0},{3,1},{4,6},{5,7},{6,4},{7,5},{8,10},{9,11},{10,... | collective-permute-start | bytes 196616 | tf_op jit(solution)/shard_map/ppermute | solution.py:746
  3.7 4.5 %collective-permute-start.6 = (bf16[256,128]{1,0:T(8,128)(2,1)}, bf16[256,128]{1,0:T(8,128)(2,1)S(1)}, u32[]{:S(2)}, u32[]{:S(2)}) collective-permute-start(bf16[256,128]{1,0:T(8,128)(2,1)} %c_in.1), channel_id=1, source_target_pairs={{0,2},{1,3},{2,0},{3,1},{4,6},{5,7},{6,4},{7,5},{8,10},{9,11},{10,... | collective-permute-start | bytes 196616 | tf_op jit(solution)/shard_map/ppermute | solution.py:746
  3.8 5.9 %collective-permute-start = (bf16[256,128]{1,0:T(8,128)(2,1)}, bf16[256,128]{1,0:T(8,128)(2,1)S(1)}, u32[]{:S(2)}, u32[]{:S(2)}) collective-permute-start(bf16[256,128]{1,0:T(8,128)(2,1)} %x_in.1), channel_id=1, source_target_pairs={{0,1},{1,0},{2,3},{3,2},{4,5},{5,4},{6,7},{7,6},{8,9},{9,8},{10,11... | collective-permute-start | bytes 196616 | tf_op jit(solution)/shard_map/ppermute | solution.py:746
  6.3 3.5 %collective-permute-start.2 = (bf16[256,128]{1,0:T(8,128)(2,1)S(1)}, bf16[256,128]{1,0:T(8,128)(2,1)S(1)}, u32[]{:S(2)}, u32[]{:S(2)}) collective-permute-start(bf16[256,128]{1,0:T(8,128)(2,1)S(1)} %collective-permute-done.1.xy), channel_id=1, source_target_pairs={{0,1},{1,0},{2,3},{3,2},{4,5},{5,4},{6,7},{7,6},{8,9},{9,8},{10,11... | collective-permute-start | bytes 196616 | tf_op jit(solution)/shard_map/ppermute | solution.py:746
  6.3 6.3 %collective-permute-start.5 = (bf16[256,128]{1,0:T(8,128)(2,1)}, bf16[256,128]{1,0:T(8,128)(2,1)S(1)}, u32[]{:S(2)}, u32[]{:S(2)}) collective-permute-start(bf16[256,128]{1,0:T(8,128)(2,1)} %c_in.1), channel_id=1, source_target_pairs={{0,1},{1,0},{2,3},{3,2},{4,5},{5,4},{6,7},{7,6},{8,9},{9,8},{10,11... | collective-permute-start | bytes 196616 | tf_op jit(solution)/shard_map/ppermute | solution.py:746
  8.2 4.4 %collective-permute-start.7 = (bf16[256,128]{1,0:T(8,128)(2,1)S(1)}, bf16[256,128]{1,0:T(8,128)(2,1)S(1)}, u32[]{:S(2)}, u32[]{:S(2)}) collective-permute-start(bf16[256,128]{1,0:T(8,128)(2,1)S(1)} %collective-permute-done.6.cy), channel_id=1, source_target_pairs={{0,1},{1,0},{2,3},{3,2},{4,5},{5,4},{6,7},{7,6},{8,9},{9,8},{10,11... | collective-permute-start | bytes 196616 | tf_op jit(solution)/shard_map/ppermute | solution.py:746
  9.7 8.5 %copy-start.1 = (bf16[2,48,128]{2,1,0:T(8,128)(2,1)}, bf16[2,48,128]{2,1,0:T(8,128)(2,1)S(1)}, u32[]{:S(2)}) copy-start(bf16[2,48,128]{2,1,0:T(8,128)(2,1)S(1)} %get-tuple-element.91.select) | copy-start | bytes 73732
  9.7 8.5 %copy-start.4 = (f32[32,128]{1,0:T(8,128)}, f32[32,128]{1,0:T(8,128)S(1)}, u32[]{:S(2)}) copy-start(f32[32,128]{1,0:T(8,128)S(1)} %get-tuple-element.90.edge) | copy-start | bytes 49156
  10.5 3.8 %collective-permute-start.3 = (bf16[16,512]{1,0:T(8,128)(2,1)S(1)}, bf16[16,512]{1,0:T(8,128)(2,1)S(1)}, u32[]{:S(2)}, u32[]{:S(2)}) collective-permute-start(bf16[16,512]{1,0:T(8,128)(2,1)S(1)} %get-tuple-element.88), channel_id=1, source_target_pairs={{0,4},{4,0},{8,12},{12,8},{16,20},{20,16},{24,28},{28,24},{1,5},{5... | collective-permute-start | bytes 49160 | tf_op jit(solution)/shard_map/ppermute | solution.py:835
  12.0 3.7 %collective-permute-start.4 = (bf16[16,512]{1,0:T(8,128)(2,1)S(1)}, bf16[16,512]{1,0:T(8,128)(2,1)S(1)}, u32[]{:S(2)}, u32[]{:S(2)}) collective-permute-start(bf16[16,512]{1,0:T(8,128)(2,1)S(1)} %get-tuple-element.89), channel_id=1, source_target_pairs={{0,4},{4,0},{8,20},{12,16},{16,12},{20,8},{24,28},{28,24},{1,5},{5... | collective-permute-start | bytes 49160 | tf_op jit(solution)/shard_map/ppermute | solution.py:836
  16.6 0.6 copy-start.6
  17.2 4.6 %collective-permute-start.8 = (bf16[2,96,256]{2,1,0:T(8,128)(2,1)S(1)}, bf16[2,96,256]{2,1,0:T(8,128)(2,1)S(1)}, u32[]{:S(2)}, u32[]{:S(2)}) collective-permute-start(bf16[2,96,256]{2,1,0:T(8,128)(2,1)S(1)} %get-tuple-element.97), channel_id=1, source_target_pairs={{0,2},{1,3},{2,0},{3,1},{4,6},{5,7},{6,4},{7,5},{8,10},{9,11},{10,... | collective-permute-start | bytes 294920 | tf_op jit(solution)/shard_map/ppermute | solution.py:746
  21.9 1.4 %collective-permute-start.9 = (bf16[2,96,256]{2,1,0:T(8,128)(2,1)S(1)}, bf16[2,96,256]{2,1,0:T(8,128)(2,1)S(1)}, u32[]{:S(2)}, u32[]{:S(2)}) collective-permute-start(bf16[2,96,256]{2,1,0:T(8,128)(2,1)S(1)} %add_convert_fusion.2.one), channel_id=1, source_target_pairs={{0,1},{1,0},{2,3},{3,2},{4,5},{5,4},{6,7},{7,6},{8,9},{9,8},{10,11... | collective-permute-start | bytes 294920 | tf_op jit(solution)/shard_map/ppermute | solution.py:746
  29.3 3.8 %collective-permute-start.10 = (bf16[80,128]{1,0:T(8,128)(2,1)S(1)}, bf16[80,128]{1,0:T(8,128)(2,1)S(1)}, u32[]{:S(2)}, u32[]{:S(2)}) collective-permute-start(bf16[80,128]{1,0:T(8,128)(2,1)S(1)} %get-tuple-element.102), channel_id=1, source_target_pairs={{0,4},{4,0},{8,12},{12,8},{16,20},{20,16},{24,28},{28,24},{1,5},{5... | collective-permute-start | bytes 61448 | tf_op jit(solution)/shard_map/ppermute | solution.py:860
  29.9 3.9 %collective-permute-start.11 = (bf16[80,128]{1,0:T(8,128)(2,1)S(1)}, bf16[80,128]{1,0:T(8,128)(2,1)S(1)}, u32[]{:S(2)}, u32[]{:S(2)}) collective-permute-start(bf16[80,128]{1,0:T(8,128)(2,1)S(1)} %get-tuple-element.103), channel_id=1, source_target_pairs={{0,4},{4,0},{8,16},{12,20},{16,8},{20,12},{24,28},{28,24},{1,5},{5... | collective-permute-start | bytes 61448 | tf_op jit(solution)/shard_map/ppermute | solution.py:861
  31.4 3.8 %collective-permute-start.12 = (bf16[80,128]{1,0:T(8,128)(2,1)S(1)}, bf16[80,128]{1,0:T(8,128)(2,1)S(1)}, u32[]{:S(2)}, u32[]{:S(2)}) collective-permute-start(bf16[80,128]{1,0:T(8,128)(2,1)S(1)} %get-tuple-element.103), channel_id=1, source_target_pairs={{0,4},{4,0},{8,20},{12,16},{16,12},{20,8},{24,28},{28,24},{1,5},{5... | collective-permute-start | bytes 61448 | tf_op jit(solution)/shard_map/ppermute | solution.py:862
  46.2 1.3 %copy-start.3 = (bf16[2,96,256]{2,1,0:T(8,128)(2,1)}, bf16[2,96,256]{2,1,0:T(8,128)(2,1)S(1)}, u32[]{:S(2)}) copy-start(bf16[2,96,256]{2,1,0:T(8,128)(2,1)S(1)} %get-tuple-element.113) | copy-start | bytes 294916
  47.5 0.7 copy-start
  48.1 0.7 copy-start.8
  48.8 4.7 %collective-permute-start.21 = (bf16[304,128]{1,0:T(8,128)(2,1)}, bf16[304,128]{1,0:T(8,128)(2,1)}, u32[]{:S(2)}, u32[]{:S(2)}) collective-permute-start(bf16[304,128]{1,0:T(8,128)(2,1)} %get-tuple-element.136), channel_id=1, source_target_pairs={{0,4},{4,0},{8,12},{12,8},{16,20},{20,16},{24,28},{28,24},{1,5},{5... | collective-permute-start | bytes 233480 | tf_op jit(solution)/shard_map/ppermute | solution.py:746
  49.3 8.7 %collective-permute-start.13 = (bf16[2,96,256]{2,1,0:T(8,128)(2,1)}, bf16[2,96,256]{2,1,0:T(8,128)(2,1)S(1)}, u32[]{:S(2)}, u32[]{:S(2)}) collective-permute-start(bf16[2,96,256]{2,1,0:T(8,128)(2,1)} %copy-done.3), channel_id=1, source_target_pairs={{0,2},{1,3},{2,0},{3,1},{4,6},{5,7},{6,4},{7,5},{8,10},{9,11},{10,... | collective-permute-start | bytes 294920 | tf_op jit(solution)/shard_map/ppermute | solution.py:746
  50.3 8.7 %collective-permute-start.19 = (bf16[256,256]{1,0:T(8,128)(2,1)}, bf16[256,256]{1,0:T(8,128)(2,1)S(1)}, u32[]{:S(2)}, u32[]{:S(2)}) collective-permute-start(bf16[256,256]{1,0:T(8,128)(2,1)} %copy-done.8), channel_id=1, source_target_pairs={{0,2},{1,3},{2,0},{3,1},{4,6},{5,7},{6,4},{7,5},{8,10},{9,11},{10,... | collective-permute-start | bytes 393224 | tf_op jit(solution)/shard_map/ppermute | solution.py:746
  54.5 14.3 %collective-permute-start.22 = (bf16[304,128]{1,0:T(8,128)(2,1)S(1)}, bf16[304,128]{1,0:T(8,128)(2,1)S(1)}, u32[]{:S(2)}, u32[]{:S(2)}) collective-permute-start(bf16[304,128]{1,0:T(8,128)(2,1)S(1)} %add_convert_fusion.5), channel_id=1, source_target_pairs={{0,8},{4,12},{8,0},{12,4},{16,24},{20,28},{24,16},{28,20},{1,9},{5... | collective-permute-start | bytes 233480 | tf_op jit(solution)/shard_map/ppermute | solution.py:746
  58.9 1.4 %collective-permute-start.14 = (bf16[2,96,256]{2,1,0:T(8,128)(2,1)S(1)}, bf16[2,96,256]{2,1,0:T(8,128)(2,1)S(1)}, u32[]{:S(2)}, u32[]{:S(2)}) collective-permute-start(bf16[2,96,256]{2,1,0:T(8,128)(2,1)S(1)} %add_convert_fusion.1.one), channel_id=1, source_target_pairs={{0,1},{1,0},{2,3},{3,2},{4,5},{5,4},{6,7},{7,6},{8,9},{9,8},{10,11... | collective-permute-start | bytes 294920 | tf_op jit(solution)/shard_map/ppermute | solution.py:746
  60.3 0.7 copy-start.2
  61.0 0.7 copy-start.5
  61.7 0.8 copy-start.7
  63.6 3.7 %collective-permute-start.26 = (f32[16,128]{1,0:T(8,128)S(1)}, f32[16,128]{1,0:T(8,128)S(1)}, u32[]{:S(2)}, u32[]{:S(2)}) collective-permute-start(f32[16,128]{1,0:T(8,128)S(1)} %get-tuple-element.139), channel_id=1, source_target_pairs={{0,2},{1,3},{2,0},{3,1},{4,6},{5,7},{6,4},{7,5},{8,10},{9,11},{10,... | collective-permute-start | bytes 24584 | tf_op jit(solution)/shard_map/ppermute | solution.py:746
  64.6 22.5 %collective-permute-start.20 = (bf16[256,128]{1,0:T(8,128)(2,1)S(1)}, bf16[256,128]{1,0:T(8,128)(2,1)S(1)}, u32[]{:S(2)}, u32[]{:S(2)}) collective-permute-start(bf16[256,128]{1,0:T(8,128)(2,1)S(1)} %select_convert_fusion), channel_id=1, source_target_pairs={{0,1},{1,0},{2,3},{3,2},{4,5},{5,4},{6,7},{7,6},{8,9},{9,8},{10,11... | collective-permute-start | bytes 196616 | tf_op jit(solution)/shard_map/ppermute | solution.py:746
  64.7 7.9 %collective-permute-start.25 = (bf16[192,128]{1,0:T(8,128)(2,1)S(1)}, bf16[192,128]{1,0:T(8,128)(2,1)S(1)}, u32[]{:S(2)}, u32[]{:S(2)}) collective-permute-start(bf16[192,128]{1,0:T(8,128)(2,1)S(1)} %get-tuple-element.138), channel_id=1, source_target_pairs={{0,4},{4,0},{8,12},{12,8},{16,20},{20,16},{24,28},{28,24},{1,5},{5... | collective-permute-start | bytes 147464 | tf_op jit(solution)/shard_map/ppermute | solution.py:746
  66.2 3.7 %collective-permute-start.15 = (f32[2,16,128]{2,1,0:T(8,128)S(1)}, f32[2,16,128]{2,1,0:T(8,128)S(1)}, u32[]{:S(2)}, u32[]{:S(2)}) collective-permute-start(f32[2,16,128]{2,1,0:T(8,128)S(1)} %get-tuple-element.126), channel_id=1, source_target_pairs={{0,4},{4,0},{8,12},{12,8},{16,20},{20,16},{24,28},{28,24},{1,5},{5... | collective-permute-start | bytes 49160 | tf_op jit(solution)/shard_map/ppermute | solution.py:923
  67.3 3.7 %collective-permute-start.16 = (f32[2,16,128]{2,1,0:T(8,128)S(1)}, f32[2,16,128]{2,1,0:T(8,128)S(1)}, u32[]{:S(2)}, u32[]{:S(2)}) collective-permute-start(f32[2,16,128]{2,1,0:T(8,128)S(1)} %get-tuple-element.127), channel_id=1, source_target_pairs={{0,4},{4,0},{8,20},{12,16},{16,12},{20,8},{24,28},{28,24},{1,5},{5... | collective-permute-start | bytes 49160 | tf_op jit(solution)/shard_map/ppermute | solution.py:930
  68.8 3.8 %collective-permute-start.27 = (f32[16,128]{1,0:T(8,128)S(1)}, f32[16,128]{1,0:T(8,128)S(1)}, u32[]{:S(2)}, u32[]{:S(2)}) collective-permute-start(f32[16,128]{1,0:T(8,128)S(1)} %add.49), channel_id=1, source_target_pairs={{0,1},{1,0},{2,3},{3,2},{4,5},{5,4},{6,7},{7,6},{8,9},{9,8},{10,11... | collective-permute-start | bytes 24584 | tf_op jit(solution)/shard_map/ppermute | solution.py:746
  70.0 5.8 %collective-permute-start.23 = (bf16[304,128]{1,0:T(8,128)(2,1)S(1)}, bf16[304,128]{1,0:T(8,128)(2,1)S(1)}, u32[]{:S(2)}, u32[]{:S(2)}) collective-permute-start(bf16[304,128]{1,0:T(8,128)(2,1)S(1)} %add_convert_fusion.4), channel_id=1, source_target_pairs={{0,16},{4,20},{8,24},{12,28},{16,0},{20,4},{24,8},{28,12},{1,17},{... | collective-permute-start | bytes 233480 | tf_op jit(solution)/shard_map/ppermute | solution.py:746
  71.5 7.4 %collective-permute-start.17 = (bf16[256,256]{1,0:T(8,128)(2,1)S(1)}, bf16[256,256]{1,0:T(8,128)(2,1)S(1)}, u32[]{:S(2)}, u32[]{:S(2)}) collective-permute-start(bf16[256,256]{1,0:T(8,128)(2,1)S(1)} %get-tuple-element.130), channel_id=1, source_target_pairs={{0,2},{1,3},{2,0},{3,1},{4,6},{5,7},{6,4},{7,5},{8,10},{9,11},{10,... | collective-permute-start | bytes 393224 | tf_op jit(solution)/shard_map/ppermute | solution.py:746
  72.6 4.4 %collective-permute-start.28 = (bf16[208,128]{1,0:T(8,128)(2,1)S(1)}, bf16[208,128]{1,0:T(8,128)(2,1)S(1)}, u32[]{:S(2)}, u32[]{:S(2)}) collective-permute-start(bf16[208,128]{1,0:T(8,128)(2,1)S(1)} %fusion), channel_id=1, source_target_pairs={{0,8},{4,12},{8,0},{12,4},{16,24},{20,28},{24,16},{28,20},{1,9},{5... | collective-permute-start | bytes 159752 | tf_op jit(solution)/shard_map/ppermute | solution.py:746
  75.8 8.3 %collective-permute-start.24 = (bf16[304,128]{1,0:T(8,128)(2,1)S(1)}, bf16[304,128]{1,0:T(8,128)(2,1)S(1)}, u32[]{:S(2)}, u32[]{:S(2)}) collective-permute-start(bf16[304,128]{1,0:T(8,128)(2,1)S(1)} %add_convert_fusion.3.refs_0_), channel_id=1, source_target_pairs={{0,4},{4,0},{8,12},{12,8},{16,20},{20,16},{24,28},{28,24},{1,5},{5... | collective-permute-start | bytes 233480 | tf_op jit(solution)/shard_map/ppermute | solution.py:746
  77.0 5.1 %collective-permute-start.29 = (bf16[208,128]{1,0:T(8,128)(2,1)S(1)}, bf16[208,128]{1,0:T(8,128)(2,1)S(1)}, u32[]{:S(2)}, u32[]{:S(2)}) collective-permute-start(bf16[208,128]{1,0:T(8,128)(2,1)S(1)} %add_convert_fusion.7), channel_id=1, source_target_pairs={{0,16},{4,20},{8,24},{12,28},{16,0},{20,4},{24,8},{28,12},{1,17},{... | collective-permute-start | bytes 159752 | tf_op jit(solution)/shard_map/ppermute | solution.py:746
  78.9 8.2 %collective-permute-start.18 = (bf16[256,256]{1,0:T(8,128)(2,1)S(1)}, bf16[256,256]{1,0:T(8,128)(2,1)S(1)}, u32[]{:S(2)}, u32[]{:S(2)}) collective-permute-start(bf16[256,256]{1,0:T(8,128)(2,1)S(1)} %add_convert_fusion.one), channel_id=1, source_target_pairs={{0,1},{1,0},{2,3},{3,2},{4,5},{5,4},{6,7},{7,6},{8,9},{9,8},{10,11... | collective-permute-start | bytes 393224 | tf_op jit(solution)/shard_map/ppermute | solution.py:746
  82.1 4.2 %collective-permute-start.30 = (bf16[208,128]{1,0:T(8,128)(2,1)S(1)}, bf16[208,128]{1,0:T(8,128)(2,1)S(1)}, u32[]{:S(2)}, u32[]{:S(2)}) collective-permute-start(bf16[208,128]{1,0:T(8,128)(2,1)S(1)} %add_convert_fusion.6.refs_2_), channel_id=1, source_target_pairs={{0,4},{4,0},{8,12},{12,8},{16,20},{20,16},{24,28},{28,24},{1,5},{5... | collective-permute-start | bytes 159752 | tf_op jit(solution)/shard_map/ppermute | solution.py:746
